TPU v7x, 32 devices: a whole 2x2x4 slice. The times are simulated.
32 devices in a mesh: gx: 4 (over z), gy: 8 (over y, x, core).
Axes of the slice: x: 2, y: 2, z: 4, core: 2. Of those that a mesh axis runs over, the one named last changes fastest.
Arguments:
- water_depth: float32 [256, 512], P('gy', 'gx'), may hold values from 0 to 2
- tracers: float32 [3, 256, 512], P(None, 'gy', 'gx'), may hold values from 0 to 2
- rainfall: float32 [256, 512], P('gy', 'gx'), may hold values from 0.2 to 1.5
- roughness: float32 [256, 512], P('gy', 'gx'), may hold values from 0.05 to 0.6
- flow_codes: int32 [256, 512], P('gy', 'gx'), may hold values from 0 to 7
- land_mask: int32 [256, 512], P('gy', 'gx'), may hold values 0 or 1
- leakance: float32 [64, 128], P('gy', 'gx'), may hold values from 0.05 to 2
- pumping: float32 [64, 128], P('gy', 'gx'), may hold values from -6 to 6
- active: int32 [64, 128], P('gy', 'gx'), may hold values 0 or 1
Outputs:
- depth_out: float32 [256, 512], P('gy', 'gx')
- tracers_out: float32 [3, 256, 512], P(None, 'gy', 'gx')
- head: float32 [64, 128], P('gy', 'gx')
All inputs are finite; a program needn't handle non-finite values. No bound on the sum of `land_mask` or of `active` on one device may be relied on, other than what follows from the above.
Results may differ from a plain program's by a relative error of at most 0.0003.
Values sent between devices are 32-bit elements; how exact they have to be, the bound alone decides.
No kernel may reach another device: no remote copies, remote signals or barrier semaphores. Data moves between devices by JAX's collectives and lax.ppermute only.
A program may use at most 64 MiB of HBM per device.

v0:
```python
import jax
import jax.numpy as jnp
from jax import lax
from jax.sharding import PartitionSpec as P

SUBSTEPS = 12
ITERS = 2


TIME_STEP = 0.2
INFILTRATION = 0.05
NEIGHBOUR_MOVES = ((-1, -1), (-1, 0), (-1, 1), (0, -1), (0, 1), (1, -1), (1, 0), (1, 1))


def with_halo(block, sides, width):
    for axis, dim in sides:
        count = lax.axis_size(axis)
        forward = [(i, i + 1) for i in range(count - 1)]
        backward = [(target, source) for source, target in forward]
        low = lax.ppermute(
            lax.slice_in_dim(block, block.shape[dim] - width, None, axis=dim), axis, forward
        )
        high = lax.ppermute(lax.slice_in_dim(block, 0, width, axis=dim), axis, backward)
        block = jnp.concatenate([low, block, high], axis=dim)
    return block


def shift_into(field, drow, dcol):
    padded = jnp.pad(field, ((0, 0), (1, 1), (1, 1)))
    height = field.shape[1]
    breadth = field.shape[2]
    return lax.slice(
        padded, (0, 1 - drow, 1 - dcol), (field.shape[0], 1 - drow + height, 1 - dcol + breadth)
    )


def overland_step(water_state, coef, flow_codes, land, rainfall):
    depth_now = water_state[0]
    rate = coef * jnp.cbrt(depth_now * depth_now)
    flux = rate[None] * water_state
    incoming = jnp.zeros_like(water_state)
    for heading in range(8):
        drow, dcol = NEIGHBOUR_MOVES[heading]
        leaving = jnp.where((flow_codes == heading)[None], flux, 0.0)
        incoming = incoming + shift_into(leaving, drow, dcol)
    source = jnp.concatenate([rainfall[None], jnp.zeros_like(water_state[1:])], axis=0)
    return land[None] * (
        water_state + TIME_STEP * (source - flux - INFILTRATION * water_state + incoming)
    )


def aquifer_apply(field, actf, leakance):
    masked = with_halo(actf * field, (("gx", 1), ("gy", 0)), 1)
    neighbours = masked[2:, 1:-1] + masked[:-2, 1:-1] + masked[1:-1, 2:] + masked[1:-1, :-2]
    return actf * ((4.0 + leakance) * field - neighbours) + (1.0 - actf) * field


def weighted_total(resid, precond):
    return lax.psum(jnp.sum(resid * precond), ("gx", "gy"))


def shards(
    water_depth, tracers, rainfall, roughness, flow_codes, land_mask, leakance, pumping, active
):
    land = land_mask.astype(jnp.float32)
    coef = roughness * land
    water_state = jnp.concatenate([water_depth[None], tracers], axis=0) * land[None]
    tile_rows = water_depth.shape[0]
    tile_cols = water_depth.shape[1]
    codes_float = flow_codes.astype(jnp.float32)
    recharge = jnp.zeros_like(water_depth)
    fixed_fields = jnp.stack([coef, codes_float, land])
    fixed_wide = with_halo(fixed_fields, (("gx", 2), ("gy", 1)), 1)
    rain_wide = jnp.pad(rainfall, 1)

    def one_step(carried, ignored):
        state_now, recharge_now = carried
        recharge_now = recharge_now + INFILTRATION * TIME_STEP * state_now[0]
        extended = with_halo(state_now, (("gx", 2), ("gy", 1)), 1)
        advanced = overland_step(extended, fixed_wide[0], fixed_wide[1], fixed_wide[2], rain_wide)
        return ((advanced[:, 1:-1, 1:-1], recharge_now), None)

    (water_state, recharge), unused = lax.scan(
        one_step, (water_state, recharge), None, length=SUBSTEPS
    )
    recharge_coarse = recharge.reshape(tile_rows // 4, 4, tile_cols // 4, 4).sum(axis=(1, 3))
    actf = active.astype(jnp.float32)
    rhs = actf * (recharge_coarse - pumping)
    jacobi_diag = actf * (4.0 + leakance) + (1.0 - actf)
    head = jnp.zeros_like(rhs)
    resid = rhs
    precond = resid / jacobi_diag
    direction = precond
    weighted = weighted_total(resid, precond)
    for sweep in range(ITERS):
        image = aquifer_apply(direction, actf, leakance)
        step_size = weighted / lax.psum(jnp.sum(direction * image), ("gx", "gy"))
        head = head + step_size * direction
        resid = resid - step_size * image
        if sweep + 1 < ITERS:
            precond = resid / jacobi_diag
            weighted_next = weighted_total(resid, precond)
            direction = precond + weighted_next / weighted * direction
            weighted = weighted_next
    return (water_state[0], water_state[1:], head)


def solution(mesh):
    placed = (
        P("gy", "gx"),
        P(None, "gy", "gx"),
        P("gy", "gx"),
        P("gy", "gx"),
        P("gy", "gx"),
        P("gy", "gx"),
        P("gy", "gx"),
        P("gy", "gx"),
        P("gy", "gx"),
    )
    return jax.shard_map(
        shards,
        mesh=mesh,
        in_specs=placed,
        out_specs=(P("gy", "gx"), P(None, "gy", "gx"), P("gy", "gx")),
        check_vma=False,
    )
```

profile of v0, /device:TPU:0, one launch (start us, length us, event | category | flops | bytes accessed | tf_op | source)
XLA Modules:
  0.0 390.2 jit_solution(12906299571049415490)
XLA Ops:
  2.2 4.9 %collective-permute-start.4 = (f32[3,32,1]{2,1,0:T(8,128)S(1)}, f32[3,32,1]{2,1,0:T(8,128)S(1)}, u32[]{:S(2)}, u32[]{:S(2)}) collective-permute-start(f32[3,32,1]{2,1,0:T(8,128)S(1)} %get-tuple-element.136), channel_id=1, source_target_pairs={{0,8},{8,16},{16,24},{1,9},{9,17},{17,25},{2,10},{10,18},{18,26},{... | collective-permute-start | bytes 1160 | tf_op jit(solution)/shard_map/ppermute | solution.py:20
  7.2 1.4 collective-permute-start.5
  8.9 4.4 %collective-permute-done.5 = f32[3,32,1]{2,1,0:T(8,128)S(1)} collective-permute-done((f32[3,32,1]{2,1,0:T(8,128)S(1)}, f32[3,32,1]{2,1,0:T(8,128)S(1)}, u32[]{:S(2)}, u32[]{:S(2)}) %collective-permute-start.5) | collective-permute-done | bytes 416 | tf_op jit(solution)/shard_map/ppermute | solution.py:23
  14.7 1.3 collective-permute-start.7
  16.8 2.7 collective-permute-done.7
  19.6 196.4 %while.15 = (s32[]{:T(128)}, f32[4,32,128]{2,1,0:T(8,128)S(1)}, f32[32,128]{1,0:T(8,128)S(1)}, f32[3,34,130]{2,1,0:T(8,128)S(1)}, f32[34,130]{1,0:T(8,128)S(1)}, /*index=5*/s32[]{:T(128)}, s32[]{:T(128)}) while((s32[]{:T(128)}, f32[4,32,128]{2,1,0:T(8,128)S(1)}, f32[32,128]{1,0:T(8,128)S(1)}, f32[3,34,130]{2,1,0:T(8,128)S(1)}, ...), condition=%wide.region_1.2_spmd.clone, body=%wide.region_0.1_spmd.clone.sunk | while | flops 594987 | bytes 2494711 | solution.py:83
  21.0 4.5 %collective-permute-start.1 = (f32[4,32,1]{2,1,0:T(8,128)S(1)}, f32[4,32,1]{2,1,0:T(8,128)S(1)}, u32[]{:S(2)}, u32[]{:S(2)}) collective-permute-start(f32[4,32,1]{2,1,0:T(8,128)S(1)} %get-tuple-element.210), channel_id=1, source_target_pairs={{0,8},{8,16},{16,24},{1,9},{9,17},{17,25},{2,10},{10,18},{18,26},{... | collective-permute-start | bytes 1544 | tf_op jit(solution)/shard_map/while/body/eval_jaxpr/ppermute | solution.py:20
  25.8 1.6 collective-permute-done.1
  27.5 1.3 collective-permute-start.2
  28.8 3.8 collective-permute-start.3
  35.9 4.6 %collective-permute-start.1 = (f32[4,32,1]{2,1,0:T(8,128)S(1)}, f32[4,32,1]{2,1,0:T(8,128)S(1)}, u32[]{:S(2)}, u32[]{:S(2)}) collective-permute-start(f32[4,32,1]{2,1,0:T(8,128)S(1)} %get-tuple-element.210), channel_id=1, source_target_pairs={{0,8},{8,16},{16,24},{1,9},{9,17},{17,25},{2,10},{10,18},{18,26},{... | collective-permute-start | bytes 1544 | tf_op jit(solution)/shard_map/while/body/eval_jaxpr/ppermute | solution.py:20
  40.8 1.6 collective-permute-done.1
  42.4 1.3 collective-permute-start.2
  43.7 3.3 collective-permute-start.3
  50.4 4.6 %collective-permute-start.1 = (f32[4,32,1]{2,1,0:T(8,128)S(1)}, f32[4,32,1]{2,1,0:T(8,128)S(1)}, u32[]{:S(2)}, u32[]{:S(2)}) collective-permute-start(f32[4,32,1]{2,1,0:T(8,128)S(1)} %get-tuple-element.210), channel_id=1, source_target_pairs={{0,8},{8,16},{16,24},{1,9},{9,17},{17,25},{2,10},{10,18},{18,26},{... | collective-permute-start | bytes 1544 | tf_op jit(solution)/shard_map/while/body/eval_jaxpr/ppermute | solution.py:20
  55.3 1.6 collective-permute-done.1
  57.0 1.3 collective-permute-start.2
  58.3 5.5 %collective-permute-start.3 = (f32[4,1,130]{2,1,0:T(1,128)S(1)}, f32[4,1,130]{2,1,0:T(1,128)S(1)}, u32[]{:S(2)}, u32[]{:S(2)}) collective-permute-start(f32[4,1,130]{2,1,0:T(1,128)S(1)} %get-tuple-element.212), channel_id=1, source_target_pairs={{0,1},{1,2},{2,3},{3,4},{4,5},{5,6},{6,7},{8,9},{9,10},{10,11},{11... | collective-permute-start | bytes 6248 | tf_op jit(solution)/shard_map/while/body/eval_jaxpr/ppermute | solution.py:20
  67.1 4.6 %collective-permute-start.1 = (f32[4,32,1]{2,1,0:T(8,128)S(1)}, f32[4,32,1]{2,1,0:T(8,128)S(1)}, u32[]{:S(2)}, u32[]{:S(2)}) collective-permute-start(f32[4,32,1]{2,1,0:T(8,128)S(1)} %get-tuple-element.210), channel_id=1, source_target_pairs={{0,8},{8,16},{16,24},{1,9},{9,17},{17,25},{2,10},{10,18},{18,26},{... | collective-permute-start | bytes 1544 | tf_op jit(solution)/shard_map/while/body/eval_jaxpr/ppermute | solution.py:20
  72.0 1.6 collective-permute-done.1
  73.7 1.3 collective-permute-start.2
  75.0 5.3 %collective-permute-start.3 = (f32[4,1,130]{2,1,0:T(1,128)S(1)}, f32[4,1,130]{2,1,0:T(1,128)S(1)}, u32[]{:S(2)}, u32[]{:S(2)}) collective-permute-start(f32[4,1,130]{2,1,0:T(1,128)S(1)} %get-tuple-element.212), channel_id=1, source_target_pairs={{0,1},{1,2},{2,3},{3,4},{4,5},{5,6},{6,7},{8,9},{9,10},{10,11},{11... | collective-permute-start | bytes 6248 | tf_op jit(solution)/shard_map/while/body/eval_jaxpr/ppermute | solution.py:20
  83.6 4.6 %collective-permute-start.1 = (f32[4,32,1]{2,1,0:T(8,128)S(1)}, f32[4,32,1]{2,1,0:T(8,128)S(1)}, u32[]{:S(2)}, u32[]{:S(2)}) collective-permute-start(f32[4,32,1]{2,1,0:T(8,128)S(1)} %get-tuple-element.210), channel_id=1, source_target_pairs={{0,8},{8,16},{16,24},{1,9},{9,17},{17,25},{2,10},{10,18},{18,26},{... | collective-permute-start | bytes 1544 | tf_op jit(solution)/shard_map/while/body/eval_jaxpr/ppermute | solution.py:20
  88.5 1.6 collective-permute-done.1
  90.2 1.3 collective-permute-start.2
  91.5 5.0 %collective-permute-start.3 = (f32[4,1,130]{2,1,0:T(1,128)S(1)}, f32[4,1,130]{2,1,0:T(1,128)S(1)}, u32[]{:S(2)}, u32[]{:S(2)}) collective-permute-start(f32[4,1,130]{2,1,0:T(1,128)S(1)} %get-tuple-element.212), channel_id=1, source_target_pairs={{0,1},{1,2},{2,3},{3,4},{4,5},{5,6},{6,7},{8,9},{9,10},{10,11},{11... | collective-permute-start | bytes 6248 | tf_op jit(solution)/shard_map/while/body/eval_jaxpr/ppermute | solution.py:20
  99.8 4.6 %collective-permute-start.1 = (f32[4,32,1]{2,1,0:T(8,128)S(1)}, f32[4,32,1]{2,1,0:T(8,128)S(1)}, u32[]{:S(2)}, u32[]{:S(2)}) collective-permute-start(f32[4,32,1]{2,1,0:T(8,128)S(1)} %get-tuple-element.210), channel_id=1, source_target_pairs={{0,8},{8,16},{16,24},{1,9},{9,17},{17,25},{2,10},{10,18},{18,26},{... | collective-permute-start | bytes 1544 | tf_op jit(solution)/shard_map/while/body/eval_jaxpr/ppermute | solution.py:20
  104.7 1.6 collective-permute-done.1
  106.4 1.3 collective-permute-start.2
  107.7 5.0 %collective-permute-start.3 = (f32[4,1,130]{2,1,0:T(1,128)S(1)}, f32[4,1,130]{2,1,0:T(1,128)S(1)}, u32[]{:S(2)}, u32[]{:S(2)}) collective-permute-start(f32[4,1,130]{2,1,0:T(1,128)S(1)} %get-tuple-element.212), channel_id=1, source_target_pairs={{0,1},{1,2},{2,3},{3,4},{4,5},{5,6},{6,7},{8,9},{9,10},{10,11},{11... | collective-permute-start | bytes 6248 | tf_op jit(solution)/shard_map/while/body/eval_jaxpr/ppermute | solution.py:20
  116.0 4.6 %collective-permute-start.1 = (f32[4,32,1]{2,1,0:T(8,128)S(1)}, f32[4,32,1]{2,1,0:T(8,128)S(1)}, u32[]{:S(2)}, u32[]{:S(2)}) collective-permute-start(f32[4,32,1]{2,1,0:T(8,128)S(1)} %get-tuple-element.210), channel_id=1, source_target_pairs={{0,8},{8,16},{16,24},{1,9},{9,17},{17,25},{2,10},{10,18},{18,26},{... | collective-permute-start | bytes 1544 | tf_op jit(solution)/shard_map/while/body/eval_jaxpr/ppermute | solution.py:20
  120.9 1.6 collective-permute-done.1
  122.6 1.3 collective-permute-start.2
  123.9 5.0 %collective-permute-start.3 = (f32[4,1,130]{2,1,0:T(1,128)S(1)}, f32[4,1,130]{2,1,0:T(1,128)S(1)}, u32[]{:S(2)}, u32[]{:S(2)}) collective-permute-start(f32[4,1,130]{2,1,0:T(1,128)S(1)} %get-tuple-element.212), channel_id=1, source_target_pairs={{0,1},{1,2},{2,3},{3,4},{4,5},{5,6},{6,7},{8,9},{9,10},{10,11},{11... | collective-permute-start | bytes 6248 | tf_op jit(solution)/shard_map/while/body/eval_jaxpr/ppermute | solution.py:20
  132.2 4.6 %collective-permute-start.1 = (f32[4,32,1]{2,1,0:T(8,128)S(1)}, f32[4,32,1]{2,1,0:T(8,128)S(1)}, u32[]{:S(2)}, u32[]{:S(2)}) collective-permute-start(f32[4,32,1]{2,1,0:T(8,128)S(1)} %get-tuple-element.210), channel_id=1, source_target_pairs={{0,8},{8,16},{16,24},{1,9},{9,17},{17,25},{2,10},{10,18},{18,26},{... | collective-permute-start | bytes 1544 | tf_op jit(solution)/shard_map/while/body/eval_jaxpr/ppermute | solution.py:20
  137.1 1.6 collective-permute-done.1
  138.8 1.3 collective-permute-start.2
  140.1 5.6 %collective-permute-start.3 = (f32[4,1,130]{2,1,0:T(1,128)S(1)}, f32[4,1,130]{2,1,0:T(1,128)S(1)}, u32[]{:S(2)}, u32[]{:S(2)}) collective-permute-start(f32[4,1,130]{2,1,0:T(1,128)S(1)} %get-tuple-element.212), channel_id=1, source_target_pairs={{0,1},{1,2},{2,3},{3,4},{4,5},{5,6},{6,7},{8,9},{9,10},{10,11},{11... | collective-permute-start | bytes 6248 | tf_op jit(solution)/shard_map/while/body/eval_jaxpr/ppermute | solution.py:20
  149.0 4.6 %collective-permute-start.1 = (f32[4,32,1]{2,1,0:T(8,128)S(1)}, f32[4,32,1]{2,1,0:T(8,128)S(1)}, u32[]{:S(2)}, u32[]{:S(2)}) collective-permute-start(f32[4,32,1]{2,1,0:T(8,128)S(1)} %get-tuple-element.210), channel_id=1, source_target_pairs={{0,8},{8,16},{16,24},{1,9},{9,17},{17,25},{2,10},{10,18},{18,26},{... | collective-permute-start | bytes 1544 | tf_op jit(solution)/shard_map/while/body/eval_jaxpr/ppermute | solution.py:20
  153.9 1.6 collective-permute-done.1
  155.5 1.3 collective-permute-start.2
  156.8 5.9 %collective-permute-start.3 = (f32[4,1,130]{2,1,0:T(1,128)S(1)}, f32[4,1,130]{2,1,0:T(1,128)S(1)}, u32[]{:S(2)}, u32[]{:S(2)}) collective-permute-start(f32[4,1,130]{2,1,0:T(1,128)S(1)} %get-tuple-element.212), channel_id=1, source_target_pairs={{0,1},{1,2},{2,3},{3,4},{4,5},{5,6},{6,7},{8,9},{9,10},{10,11},{11... | collective-permute-start | bytes 6248 | tf_op jit(solution)/shard_map/while/body/eval_jaxpr/ppermute | solution.py:20
  166.1 4.6 %collective-permute-start.1 = (f32[4,32,1]{2,1,0:T(8,128)S(1)}, f32[4,32,1]{2,1,0:T(8,128)S(1)}, u32[]{:S(2)}, u32[]{:S(2)}) collective-permute-start(f32[4,32,1]{2,1,0:T(8,128)S(1)} %get-tuple-element.210), channel_id=1, source_target_pairs={{0,8},{8,16},{16,24},{1,9},{9,17},{17,25},{2,10},{10,18},{18,26},{... | collective-permute-start | bytes 1544 | tf_op jit(solution)/shard_map/while/body/eval_jaxpr/ppermute | solution.py:20
  171.0 1.6 collective-permute-done.1
  172.6 1.3 collective-permute-start.2
  173.9 5.9 %collective-permute-start.3 = (f32[4,1,130]{2,1,0:T(1,128)S(1)}, f32[4,1,130]{2,1,0:T(1,128)S(1)}, u32[]{:S(2)}, u32[]{:S(2)}) collective-permute-start(f32[4,1,130]{2,1,0:T(1,128)S(1)} %get-tuple-element.212), channel_id=1, source_target_pairs={{0,1},{1,2},{2,3},{3,4},{4,5},{5,6},{6,7},{8,9},{9,10},{10,11},{11... | collective-permute-start | bytes 6248 | tf_op jit(solution)/shard_map/while/body/eval_jaxpr/ppermute | solution.py:20
  183.2 4.6 %collective-permute-start.1 = (f32[4,32,1]{2,1,0:T(8,128)S(1)}, f32[4,32,1]{2,1,0:T(8,128)S(1)}, u32[]{:S(2)}, u32[]{:S(2)}) collective-permute-start(f32[4,32,1]{2,1,0:T(8,128)S(1)} %get-tuple-element.210), channel_id=1, source_target_pairs={{0,8},{8,16},{16,24},{1,9},{9,17},{17,25},{2,10},{10,18},{18,26},{... | collective-permute-start | bytes 1544 | tf_op jit(solution)/shard_map/while/body/eval_jaxpr/ppermute | solution.py:20
  188.1 1.6 collective-permute-done.1
  189.7 1.3 collective-permute-start.2
  191.0 5.9 %collective-permute-start.3 = (f32[4,1,130]{2,1,0:T(1,128)S(1)}, f32[4,1,130]{2,1,0:T(1,128)S(1)}, u32[]{:S(2)}, u32[]{:S(2)}) collective-permute-start(f32[4,1,130]{2,1,0:T(1,128)S(1)} %get-tuple-element.212), channel_id=1, source_target_pairs={{0,1},{1,2},{2,3},{3,4},{4,5},{5,6},{6,7},{8,9},{9,10},{10,11},{11... | collective-permute-start | bytes 6248 | tf_op jit(solution)/shard_map/while/body/eval_jaxpr/ppermute | solution.py:20
  200.3 4.6 %collective-permute-start.1 = (f32[4,32,1]{2,1,0:T(8,128)S(1)}, f32[4,32,1]{2,1,0:T(8,128)S(1)}, u32[]{:S(2)}, u32[]{:S(2)}) collective-permute-start(f32[4,32,1]{2,1,0:T(8,128)S(1)} %get-tuple-element.210), channel_id=1, source_target_pairs={{0,8},{8,16},{16,24},{1,9},{9,17},{17,25},{2,10},{10,18},{18,26},{... | collective-permute-start | bytes 1544 | tf_op jit(solution)/shard_map/while/body/eval_jaxpr/ppermute | solution.py:20
  205.2 1.6 collective-permute-done.1
  206.9 1.3 collective-permute-start.2
  208.2 5.9 %collective-permute-start.3 = (f32[4,1,130]{2,1,0:T(1,128)S(1)}, f32[4,1,130]{2,1,0:T(1,128)S(1)}, u32[]{:S(2)}, u32[]{:S(2)}) collective-permute-start(f32[4,1,130]{2,1,0:T(1,128)S(1)} %get-tuple-element.212), channel_id=1, source_target_pairs={{0,1},{1,2},{2,3},{3,4},{4,5},{5,6},{6,7},{8,9},{9,10},{10,11},{11... | collective-permute-start | bytes 6248 | tf_op jit(solution)/shard_map/while/body/eval_jaxpr/ppermute | solution.py:20
  218.6 4.6 %collective-permute-start.8 = (f32[8,1]{1,0:T(8,128)S(1)}, f32[8,1]{1,0:T(8,128)S(1)}, u32[]{:S(2)}, u32[]{:S(2)}) collective-permute-start(f32[8,1]{1,0:T(8,128)S(1)} %get-tuple-element.151), channel_id=1, source_target_pairs={{0,8},{8,16},{16,24},{1,9},{9,17},{17,25},{2,10},{10,18},{18,26},{... | collective-permute-start | bytes 104 | tf_op jit(solution)/shard_map/ppermute | solution.py:20
  223.2 1.3 collective-permute-done.8
  225.9 5.9 %collective-permute-start.11 = (f32[1,34]{1,0:T(1,128)S(1)}, f32[1,34]{1,0:T(1,128)S(1)}, u32[]{:S(2)}, u32[]{:S(2)}) collective-permute-start(f32[1,34]{1,0:T(1,128)S(1)} %get-tuple-element.147), channel_id=1, source_target_pairs={{0,1},{1,2},{2,3},{3,4},{4,5},{5,6},{6,7},{8,9},{9,10},{10,11},{11... | collective-permute-start | bytes 416 | tf_op jit(solution)/shard_map/ppermute | solution.py:20
  233.3 51.7 %all-reduce.10 = (f32[]{:T(128)}, f32[]{:T(128)}) all-reduce(f32[]{:T(128)} %get-tuple-element.90, f32[]{:T(128)} %get-tuple-element.89), channel_id=1, replica_groups=mesh['gx'=4,'gy'=8] {'gx','gy'}, use_global_device_ids=true, to_apply=%region_4.5 | all-reduce | flops 2 | bytes 16 | tf_op jit(solution)/shard_map/psum | solution.py:59
  287.6 42.3 %psum.30 = f32[]{:T(128)} all-reduce(f32[]{:T(128)} %multiply_reduce_fusion), channel_id=1, replica_groups=mesh['gx'=4,'gy'=8] {'gx','gy'}, use_global_device_ids=true, to_apply=%region_8.9 | all-reduce | flops 1 | bytes 8 | tf_op jit(solution)/shard_map/psum | solution.py:59
  331.4 1.9 collective-permute-start.12
  333.3 1.3 collective-permute-start.13
  334.6 4.2 %collective-permute-done.13 = f32[8,1]{1,0:T(8,128)S(1)} collective-permute-done((f32[8,1]{1,0:T(8,128)S(1)}, f32[8,1]{1,0:T(8,128)S(1)}, u32[]{:S(2)}, u32[]{:S(2)}) %collective-permute-start.13) | collective-permute-done | bytes 64 | tf_op jit(solution)/shard_map/ppermute | solution.py:23
  340.2 3.0 collective-permute-start.15
  345.4 43.0 %psum.31 = f32[]{:T(128)} all-reduce(f32[]{:T(128)} %fusion.15), channel_id=1, replica_groups=mesh['gx'=4,'gy'=8] {'gx','gy'}, use_global_device_ids=true, to_apply=%region_10.11 | all-reduce | flops 1 | bytes 8 | tf_op jit(solution)/shard_map/psum | solution.py:97
  (250 shorter events, 57.9 us)
Async XLA Ops:
  0.6 0.8 copy-start.2
  0.6 0.8 copy-start.4
  2.2 6.7 %collective-permute-start.4 = (f32[3,32,1]{2,1,0:T(8,128)S(1)}, f32[3,32,1]{2,1,0:T(8,128)S(1)}, u32[]{:S(2)}, u32[]{:S(2)}) collective-permute-start(f32[3,32,1]{2,1,0:T(8,128)S(1)} %get-tuple-element.136), channel_id=1, source_target_pairs={{0,8},{8,16},{16,24},{1,9},{9,17},{17,25},{2,10},{10,18},{18,26},{... | collective-permute-start | bytes 1160 | tf_op jit(solution)/shard_map/ppermute | solution.py:20
  7.2 8.8 %copy-start.3 = (f32[3,32,128]{2,1,0:T(8,128)S(1)}, f32[3,32,128]{2,1,0:T(8,128)}, u32[]{:S(2)}) copy-start(f32[3,32,128]{2,1,0:T(8,128)} %param.12) | copy-start | bytes 147460
  7.2 6.1 %collective-permute-start.5 = (f32[3,32,1]{2,1,0:T(8,128)S(1)}, f32[3,32,1]{2,1,0:T(8,128)S(1)}, u32[]{:S(2)}, u32[]{:S(2)}) collective-permute-start(f32[3,32,1]{2,1,0:T(8,128)S(1)} %get-tuple-element.137), channel_id=1, source_target_pairs={{8,0},{16,8},{24,16},{9,1},{17,9},{25,17},{10,2},{18,10},{26,18},{... | collective-permute-start | bytes 1160 | tf_op jit(solution)/shard_map/ppermute | solution.py:23
  13.3 2.7 copy-start.5
  13.4 3.4 collective-permute-start.6
  14.7 4.8 %collective-permute-start.7 = (f32[3,1,130]{2,1,0:T(1,128)S(1)}, f32[3,1,130]{2,1,0:T(1,128)S(1)}, u32[]{:S(2)}, u32[]{:S(2)}) collective-permute-start(f32[3,1,130]{2,1,0:T(1,128)S(1)} %get-tuple-element.135), channel_id=1, source_target_pairs={{1,0},{2,1},{3,2},{4,3},{5,4},{6,5},{7,6},{9,8},{10,9},{11,10},{12... | collective-permute-start | bytes 4688 | tf_op jit(solution)/shard_map/ppermute | solution.py:23
  19.7 6.2 %collective-permute-start = (f32[4,32,1]{2,1,0:T(8,128)S(1)}, f32[4,32,1]{2,1,0:T(8,128)S(1)}, u32[]{:S(2)}, u32[]{:S(2)}) collective-permute-start(f32[4,32,1]{2,1,0:T(8,128)S(1)} %get-tuple-element.209), channel_id=1, source_target_pairs={{8,0},{16,8},{24,16},{9,1},{17,9},{25,17},{10,2},{18,10},{26,18},{... | collective-permute-start | bytes 1544 | tf_op jit(solution)/shard_map/while/body/eval_jaxpr/ppermute | solution.py:23
  21.0 6.4 %collective-permute-start.1 = (f32[4,32,1]{2,1,0:T(8,128)S(1)}, f32[4,32,1]{2,1,0:T(8,128)S(1)}, u32[]{:S(2)}, u32[]{:S(2)}) collective-permute-start(f32[4,32,1]{2,1,0:T(8,128)S(1)} %get-tuple-element.210), channel_id=1, source_target_pairs={{0,8},{8,16},{16,24},{1,9},{9,17},{17,25},{2,10},{10,18},{18,26},{... | collective-permute-start | bytes 1544 | tf_op jit(solution)/shard_map/while/body/eval_jaxpr/ppermute | solution.py:20
  27.5 5.1 %collective-permute-start.2 = (f32[4,1,130]{2,1,0:T(1,128)S(1)}, f32[4,1,130]{2,1,0:T(1,128)S(1)}, u32[]{:S(2)}, u32[]{:S(2)}) collective-permute-start(f32[4,1,130]{2,1,0:T(1,128)S(1)} %get-tuple-element.211), channel_id=1, source_target_pairs={{1,0},{2,1},{3,2},{4,3},{5,4},{6,5},{7,6},{9,8},{10,9},{11,10},{12... | collective-permute-start | bytes 6248 | tf_op jit(solution)/shard_map/while/body/eval_jaxpr/ppermute | solution.py:23
  28.8 4.6 %collective-permute-start.3 = (f32[4,1,130]{2,1,0:T(1,128)S(1)}, f32[4,1,130]{2,1,0:T(1,128)S(1)}, u32[]{:S(2)}, u32[]{:S(2)}) collective-permute-start(f32[4,1,130]{2,1,0:T(1,128)S(1)} %get-tuple-element.212), channel_id=1, source_target_pairs={{0,1},{1,2},{2,3},{3,4},{4,5},{5,6},{6,7},{8,9},{9,10},{10,11},{11... | collective-permute-start | bytes 6248 | tf_op jit(solution)/shard_map/while/body/eval_jaxpr/ppermute | solution.py:20
  34.6 6.2 %collective-permute-start = (f32[4,32,1]{2,1,0:T(8,128)S(1)}, f32[4,32,1]{2,1,0:T(8,128)S(1)}, u32[]{:S(2)}, u32[]{:S(2)}) collective-permute-start(f32[4,32,1]{2,1,0:T(8,128)S(1)} %get-tuple-element.209), channel_id=1, source_target_pairs={{8,0},{16,8},{24,16},{9,1},{17,9},{25,17},{10,2},{18,10},{26,18},{... | collective-permute-start | bytes 1544 | tf_op jit(solution)/shard_map/while/body/eval_jaxpr/ppermute | solution.py:23
  35.9 6.5 %collective-permute-start.1 = (f32[4,32,1]{2,1,0:T(8,128)S(1)}, f32[4,32,1]{2,1,0:T(8,128)S(1)}, u32[]{:S(2)}, u32[]{:S(2)}) collective-permute-start(f32[4,32,1]{2,1,0:T(8,128)S(1)} %get-tuple-element.210), channel_id=1, source_target_pairs={{0,8},{8,16},{16,24},{1,9},{9,17},{17,25},{2,10},{10,18},{18,26},{... | collective-permute-start | bytes 1544 | tf_op jit(solution)/shard_map/while/body/eval_jaxpr/ppermute | solution.py:20
  42.4 4.7 %collective-permute-start.2 = (f32[4,1,130]{2,1,0:T(1,128)S(1)}, f32[4,1,130]{2,1,0:T(1,128)S(1)}, u32[]{:S(2)}, u32[]{:S(2)}) collective-permute-start(f32[4,1,130]{2,1,0:T(1,128)S(1)} %get-tuple-element.211), channel_id=1, source_target_pairs={{1,0},{2,1},{3,2},{4,3},{5,4},{6,5},{7,6},{9,8},{10,9},{11,10},{12... | collective-permute-start | bytes 6248 | tf_op jit(solution)/shard_map/while/body/eval_jaxpr/ppermute | solution.py:23
  43.7 4.2 %collective-permute-start.3 = (f32[4,1,130]{2,1,0:T(1,128)S(1)}, f32[4,1,130]{2,1,0:T(1,128)S(1)}, u32[]{:S(2)}, u32[]{:S(2)}) collective-permute-start(f32[4,1,130]{2,1,0:T(1,128)S(1)} %get-tuple-element.212), channel_id=1, source_target_pairs={{0,1},{1,2},{2,3},{3,4},{4,5},{5,6},{6,7},{8,9},{9,10},{10,11},{11... | collective-permute-start | bytes 6248 | tf_op jit(solution)/shard_map/while/body/eval_jaxpr/ppermute | solution.py:20
  49.1 6.2 %collective-permute-start = (f32[4,32,1]{2,1,0:T(8,128)S(1)}, f32[4,32,1]{2,1,0:T(8,128)S(1)}, u32[]{:S(2)}, u32[]{:S(2)}) collective-permute-start(f32[4,32,1]{2,1,0:T(8,128)S(1)} %get-tuple-element.209), channel_id=1, source_target_pairs={{8,0},{16,8},{24,16},{9,1},{17,9},{25,17},{10,2},{18,10},{26,18},{... | collective-permute-start | bytes 1544 | tf_op jit(solution)/shard_map/while/body/eval_jaxpr/ppermute | solution.py:23
  50.4 6.5 %collective-permute-start.1 = (f32[4,32,1]{2,1,0:T(8,128)S(1)}, f32[4,32,1]{2,1,0:T(8,128)S(1)}, u32[]{:S(2)}, u32[]{:S(2)}) collective-permute-start(f32[4,32,1]{2,1,0:T(8,128)S(1)} %get-tuple-element.210), channel_id=1, source_target_pairs={{0,8},{8,16},{16,24},{1,9},{9,17},{17,25},{2,10},{10,18},{18,26},{... | collective-permute-start | bytes 1544 | tf_op jit(solution)/shard_map/while/body/eval_jaxpr/ppermute | solution.py:20
  57.0 6.9 %collective-permute-start.2 = (f32[4,1,130]{2,1,0:T(1,128)S(1)}, f32[4,1,130]{2,1,0:T(1,128)S(1)}, u32[]{:S(2)}, u32[]{:S(2)}) collective-permute-start(f32[4,1,130]{2,1,0:T(1,128)S(1)} %get-tuple-element.211), channel_id=1, source_target_pairs={{1,0},{2,1},{3,2},{4,3},{5,4},{6,5},{7,6},{9,8},{10,9},{11,10},{12... | collective-permute-start | bytes 6248 | tf_op jit(solution)/shard_map/while/body/eval_jaxpr/ppermute | solution.py:23
  58.3 6.4 %collective-permute-start.3 = (f32[4,1,130]{2,1,0:T(1,128)S(1)}, f32[4,1,130]{2,1,0:T(1,128)S(1)}, u32[]{:S(2)}, u32[]{:S(2)}) collective-permute-start(f32[4,1,130]{2,1,0:T(1,128)S(1)} %get-tuple-element.212), channel_id=1, source_target_pairs={{0,1},{1,2},{2,3},{3,4},{4,5},{5,6},{6,7},{8,9},{9,10},{10,11},{11... | collective-permute-start | bytes 6248 | tf_op jit(solution)/shard_map/while/body/eval_jaxpr/ppermute | solution.py:20
  65.8 6.2 %collective-permute-start = (f32[4,32,1]{2,1,0:T(8,128)S(1)}, f32[4,32,1]{2,1,0:T(8,128)S(1)}, u32[]{:S(2)}, u32[]{:S(2)}) collective-permute-start(f32[4,32,1]{2,1,0:T(8,128)S(1)} %get-tuple-element.209), channel_id=1, source_target_pairs={{8,0},{16,8},{24,16},{9,1},{17,9},{25,17},{10,2},{18,10},{26,18},{... | collective-permute-start | bytes 1544 | tf_op jit(solution)/shard_map/while/body/eval_jaxpr/ppermute | solution.py:23
  67.1 6.5 %collective-permute-start.1 = (f32[4,32,1]{2,1,0:T(8,128)S(1)}, f32[4,32,1]{2,1,0:T(8,128)S(1)}, u32[]{:S(2)}, u32[]{:S(2)}) collective-permute-start(f32[4,32,1]{2,1,0:T(8,128)S(1)} %get-tuple-element.210), channel_id=1, source_target_pairs={{0,8},{8,16},{16,24},{1,9},{9,17},{17,25},{2,10},{10,18},{18,26},{... | collective-permute-start | bytes 1544 | tf_op jit(solution)/shard_map/while/body/eval_jaxpr/ppermute | solution.py:20
  73.7 6.6 %collective-permute-start.2 = (f32[4,1,130]{2,1,0:T(1,128)S(1)}, f32[4,1,130]{2,1,0:T(1,128)S(1)}, u32[]{:S(2)}, u32[]{:S(2)}) collective-permute-start(f32[4,1,130]{2,1,0:T(1,128)S(1)} %get-tuple-element.211), channel_id=1, source_target_pairs={{1,0},{2,1},{3,2},{4,3},{5,4},{6,5},{7,6},{9,8},{10,9},{11,10},{12... | collective-permute-start | bytes 6248 | tf_op jit(solution)/shard_map/while/body/eval_jaxpr/ppermute | solution.py:23
  75.0 6.1 %collective-permute-start.3 = (f32[4,1,130]{2,1,0:T(1,128)S(1)}, f32[4,1,130]{2,1,0:T(1,128)S(1)}, u32[]{:S(2)}, u32[]{:S(2)}) collective-permute-start(f32[4,1,130]{2,1,0:T(1,128)S(1)} %get-tuple-element.212), channel_id=1, source_target_pairs={{0,1},{1,2},{2,3},{3,4},{4,5},{5,6},{6,7},{8,9},{9,10},{10,11},{11... | collective-permute-start | bytes 6248 | tf_op jit(solution)/shard_map/while/body/eval_jaxpr/ppermute | solution.py:20
  82.3 6.2 %collective-permute-start = (f32[4,32,1]{2,1,0:T(8,128)S(1)}, f32[4,32,1]{2,1,0:T(8,128)S(1)}, u32[]{:S(2)}, u32[]{:S(2)}) collective-permute-start(f32[4,32,1]{2,1,0:T(8,128)S(1)} %get-tuple-element.209), channel_id=1, source_target_pairs={{8,0},{16,8},{24,16},{9,1},{17,9},{25,17},{10,2},{18,10},{26,18},{... | collective-permute-start | bytes 1544 | tf_op jit(solution)/shard_map/while/body/eval_jaxpr/ppermute | solution.py:23
  83.6 6.5 %collective-permute-start.1 = (f32[4,32,1]{2,1,0:T(8,128)S(1)}, f32[4,32,1]{2,1,0:T(8,128)S(1)}, u32[]{:S(2)}, u32[]{:S(2)}) collective-permute-start(f32[4,32,1]{2,1,0:T(8,128)S(1)} %get-tuple-element.210), channel_id=1, source_target_pairs={{0,8},{8,16},{16,24},{1,9},{9,17},{17,25},{2,10},{10,18},{18,26},{... | collective-permute-start | bytes 1544 | tf_op jit(solution)/shard_map/while/body/eval_jaxpr/ppermute | solution.py:20
  90.2 6.3 %collective-permute-start.2 = (f32[4,1,130]{2,1,0:T(1,128)S(1)}, f32[4,1,130]{2,1,0:T(1,128)S(1)}, u32[]{:S(2)}, u32[]{:S(2)}) collective-permute-start(f32[4,1,130]{2,1,0:T(1,128)S(1)} %get-tuple-element.211), channel_id=1, source_target_pairs={{1,0},{2,1},{3,2},{4,3},{5,4},{6,5},{7,6},{9,8},{10,9},{11,10},{12... | collective-permute-start | bytes 6248 | tf_op jit(solution)/shard_map/while/body/eval_jaxpr/ppermute | solution.py:23
  91.5 5.8 %collective-permute-start.3 = (f32[4,1,130]{2,1,0:T(1,128)S(1)}, f32[4,1,130]{2,1,0:T(1,128)S(1)}, u32[]{:S(2)}, u32[]{:S(2)}) collective-permute-start(f32[4,1,130]{2,1,0:T(1,128)S(1)} %get-tuple-element.212), channel_id=1, source_target_pairs={{0,1},{1,2},{2,3},{3,4},{4,5},{5,6},{6,7},{8,9},{9,10},{10,11},{11... | collective-permute-start | bytes 6248 | tf_op jit(solution)/shard_map/while/body/eval_jaxpr/ppermute | solution.py:20
  98.5 6.2 %collective-permute-start = (f32[4,32,1]{2,1,0:T(8,128)S(1)}, f32[4,32,1]{2,1,0:T(8,128)S(1)}, u32[]{:S(2)}, u32[]{:S(2)}) collective-permute-start(f32[4,32,1]{2,1,0:T(8,128)S(1)} %get-tuple-element.209), channel_id=1, source_target_pairs={{8,0},{16,8},{24,16},{9,1},{17,9},{25,17},{10,2},{18,10},{26,18},{... | collective-permute-start | bytes 1544 | tf_op jit(solution)/shard_map/while/body/eval_jaxpr/ppermute | solution.py:23
  99.8 6.5 %collective-permute-start.1 = (f32[4,32,1]{2,1,0:T(8,128)S(1)}, f32[4,32,1]{2,1,0:T(8,128)S(1)}, u32[]{:S(2)}, u32[]{:S(2)}) collective-permute-start(f32[4,32,1]{2,1,0:T(8,128)S(1)} %get-tuple-element.210), channel_id=1, source_target_pairs={{0,8},{8,16},{16,24},{1,9},{9,17},{17,25},{2,10},{10,18},{18,26},{... | collective-permute-start | bytes 1544 | tf_op jit(solution)/shard_map/while/body/eval_jaxpr/ppermute | solution.py:20
  106.4 6.3 %collective-permute-start.2 = (f32[4,1,130]{2,1,0:T(1,128)S(1)}, f32[4,1,130]{2,1,0:T(1,128)S(1)}, u32[]{:S(2)}, u32[]{:S(2)}) collective-permute-start(f32[4,1,130]{2,1,0:T(1,128)S(1)} %get-tuple-element.211), channel_id=1, source_target_pairs={{1,0},{2,1},{3,2},{4,3},{5,4},{6,5},{7,6},{9,8},{10,9},{11,10},{12... | collective-permute-start | bytes 6248 | tf_op jit(solution)/shard_map/while/body/eval_jaxpr/ppermute | solution.py:23
  107.7 5.8 %collective-permute-start.3 = (f32[4,1,130]{2,1,0:T(1,128)S(1)}, f32[4,1,130]{2,1,0:T(1,128)S(1)}, u32[]{:S(2)}, u32[]{:S(2)}) collective-permute-start(f32[4,1,130]{2,1,0:T(1,128)S(1)} %get-tuple-element.212), channel_id=1, source_target_pairs={{0,1},{1,2},{2,3},{3,4},{4,5},{5,6},{6,7},{8,9},{9,10},{10,11},{11... | collective-permute-start | bytes 6248 | tf_op jit(solution)/shard_map/while/body/eval_jaxpr/ppermute | solution.py:20
  114.7 6.2 %collective-permute-start = (f32[4,32,1]{2,1,0:T(8,128)S(1)}, f32[4,32,1]{2,1,0:T(8,128)S(1)}, u32[]{:S(2)}, u32[]{:S(2)}) collective-permute-start(f32[4,32,1]{2,1,0:T(8,128)S(1)} %get-tuple-element.209), channel_id=1, source_target_pairs={{8,0},{16,8},{24,16},{9,1},{17,9},{25,17},{10,2},{18,10},{26,18},{... | collective-permute-start | bytes 1544 | tf_op jit(solution)/shard_map/while/body/eval_jaxpr/ppermute | solution.py:23
  116.0 6.5 %collective-permute-start.1 = (f32[4,32,1]{2,1,0:T(8,128)S(1)}, f32[4,32,1]{2,1,0:T(8,128)S(1)}, u32[]{:S(2)}, u32[]{:S(2)}) collective-permute-start(f32[4,32,1]{2,1,0:T(8,128)S(1)} %get-tuple-element.210), channel_id=1, source_target_pairs={{0,8},{8,16},{16,24},{1,9},{9,17},{17,25},{2,10},{10,18},{18,26},{... | collective-permute-start | bytes 1544 | tf_op jit(solution)/shard_map/while/body/eval_jaxpr/ppermute | solution.py:20
  122.6 6.3 %collective-permute-start.2 = (f32[4,1,130]{2,1,0:T(1,128)S(1)}, f32[4,1,130]{2,1,0:T(1,128)S(1)}, u32[]{:S(2)}, u32[]{:S(2)}) collective-permute-start(f32[4,1,130]{2,1,0:T(1,128)S(1)} %get-tuple-element.211), channel_id=1, source_target_pairs={{1,0},{2,1},{3,2},{4,3},{5,4},{6,5},{7,6},{9,8},{10,9},{11,10},{12... | collective-permute-start | bytes 6248 | tf_op jit(solution)/shard_map/while/body/eval_jaxpr/ppermute | solution.py:23
  123.9 5.8 %collective-permute-start.3 = (f32[4,1,130]{2,1,0:T(1,128)S(1)}, f32[4,1,130]{2,1,0:T(1,128)S(1)}, u32[]{:S(2)}, u32[]{:S(2)}) collective-permute-start(f32[4,1,130]{2,1,0:T(1,128)S(1)} %get-tuple-element.212), channel_id=1, source_target_pairs={{0,1},{1,2},{2,3},{3,4},{4,5},{5,6},{6,7},{8,9},{9,10},{10,11},{11... | collective-permute-start | bytes 6248 | tf_op jit(solution)/shard_map/while/body/eval_jaxpr/ppermute | solution.py:20
  130.9 6.2 %collective-permute-start = (f32[4,32,1]{2,1,0:T(8,128)S(1)}, f32[4,32,1]{2,1,0:T(8,128)S(1)}, u32[]{:S(2)}, u32[]{:S(2)}) collective-permute-start(f32[4,32,1]{2,1,0:T(8,128)S(1)} %get-tuple-element.209), channel_id=1, source_target_pairs={{8,0},{16,8},{24,16},{9,1},{17,9},{25,17},{10,2},{18,10},{26,18},{... | collective-permute-start | bytes 1544 | tf_op jit(solution)/shard_map/while/body/eval_jaxpr/ppermute | solution.py:23
  132.2 6.5 %collective-permute-start.1 = (f32[4,32,1]{2,1,0:T(8,128)S(1)}, f32[4,32,1]{2,1,0:T(8,128)S(1)}, u32[]{:S(2)}, u32[]{:S(2)}) collective-permute-start(f32[4,32,1]{2,1,0:T(8,128)S(1)} %get-tuple-element.210), channel_id=1, source_target_pairs={{0,8},{8,16},{16,24},{1,9},{9,17},{17,25},{2,10},{10,18},{18,26},{... | collective-permute-start | bytes 1544 | tf_op jit(solution)/shard_map/while/body/eval_jaxpr/ppermute | solution.py:20
  138.8 6.9 %collective-permute-start.2 = (f32[4,1,130]{2,1,0:T(1,128)S(1)}, f32[4,1,130]{2,1,0:T(1,128)S(1)}, u32[]{:S(2)}, u32[]{:S(2)}) collective-permute-start(f32[4,1,130]{2,1,0:T(1,128)S(1)} %get-tuple-element.211), channel_id=1, source_target_pairs={{1,0},{2,1},{3,2},{4,3},{5,4},{6,5},{7,6},{9,8},{10,9},{11,10},{12... | collective-permute-start | bytes 6248 | tf_op jit(solution)/shard_map/while/body/eval_jaxpr/ppermute | solution.py:23
  140.1 6.4 %collective-permute-start.3 = (f32[4,1,130]{2,1,0:T(1,128)S(1)}, f32[4,1,130]{2,1,0:T(1,128)S(1)}, u32[]{:S(2)}, u32[]{:S(2)}) collective-permute-start(f32[4,1,130]{2,1,0:T(1,128)S(1)} %get-tuple-element.212), channel_id=1, source_target_pairs={{0,1},{1,2},{2,3},{3,4},{4,5},{5,6},{6,7},{8,9},{9,10},{10,11},{11... | collective-permute-start | bytes 6248 | tf_op jit(solution)/shard_map/while/body/eval_jaxpr/ppermute | solution.py:20
  147.7 6.2 %collective-permute-start = (f32[4,32,1]{2,1,0:T(8,128)S(1)}, f32[4,32,1]{2,1,0:T(8,128)S(1)}, u32[]{:S(2)}, u32[]{:S(2)}) collective-permute-start(f32[4,32,1]{2,1,0:T(8,128)S(1)} %get-tuple-element.209), channel_id=1, source_target_pairs={{8,0},{16,8},{24,16},{9,1},{17,9},{25,17},{10,2},{18,10},{26,18},{... | collective-permute-start | bytes 1544 | tf_op jit(solution)/shard_map/while/body/eval_jaxpr/ppermute | solution.py:23
  149.0 6.5 %collective-permute-start.1 = (f32[4,32,1]{2,1,0:T(8,128)S(1)}, f32[4,32,1]{2,1,0:T(8,128)S(1)}, u32[]{:S(2)}, u32[]{:S(2)}) collective-permute-start(f32[4,32,1]{2,1,0:T(8,128)S(1)} %get-tuple-element.210), channel_id=1, source_target_pairs={{0,8},{8,16},{16,24},{1,9},{9,17},{17,25},{2,10},{10,18},{18,26},{... | collective-permute-start | bytes 1544 | tf_op jit(solution)/shard_map/while/body/eval_jaxpr/ppermute | solution.py:20
  155.5 7.3 %collective-permute-start.2 = (f32[4,1,130]{2,1,0:T(1,128)S(1)}, f32[4,1,130]{2,1,0:T(1,128)S(1)}, u32[]{:S(2)}, u32[]{:S(2)}) collective-permute-start(f32[4,1,130]{2,1,0:T(1,128)S(1)} %get-tuple-element.211), channel_id=1, source_target_pairs={{1,0},{2,1},{3,2},{4,3},{5,4},{6,5},{7,6},{9,8},{10,9},{11,10},{12... | collective-permute-start | bytes 6248 | tf_op jit(solution)/shard_map/while/body/eval_jaxpr/ppermute | solution.py:23
  156.8 6.8 %collective-permute-start.3 = (f32[4,1,130]{2,1,0:T(1,128)S(1)}, f32[4,1,130]{2,1,0:T(1,128)S(1)}, u32[]{:S(2)}, u32[]{:S(2)}) collective-permute-start(f32[4,1,130]{2,1,0:T(1,128)S(1)} %get-tuple-element.212), channel_id=1, source_target_pairs={{0,1},{1,2},{2,3},{3,4},{4,5},{5,6},{6,7},{8,9},{9,10},{10,11},{11... | collective-permute-start | bytes 6248 | tf_op jit(solution)/shard_map/while/body/eval_jaxpr/ppermute | solution.py:20
  164.8 6.2 %collective-permute-start = (f32[4,32,1]{2,1,0:T(8,128)S(1)}, f32[4,32,1]{2,1,0:T(8,128)S(1)}, u32[]{:S(2)}, u32[]{:S(2)}) collective-permute-start(f32[4,32,1]{2,1,0:T(8,128)S(1)} %get-tuple-element.209), channel_id=1, source_target_pairs={{8,0},{16,8},{24,16},{9,1},{17,9},{25,17},{10,2},{18,10},{26,18},{... | collective-permute-start | bytes 1544 | tf_op jit(solution)/shard_map/while/body/eval_jaxpr/ppermute | solution.py:23
  166.1 6.5 %collective-permute-start.1 = (f32[4,32,1]{2,1,0:T(8,128)S(1)}, f32[4,32,1]{2,1,0:T(8,128)S(1)}, u32[]{:S(2)}, u32[]{:S(2)}) collective-permute-start(f32[4,32,1]{2,1,0:T(8,128)S(1)} %get-tuple-element.210), channel_id=1, source_target_pairs={{0,8},{8,16},{16,24},{1,9},{9,17},{17,25},{2,10},{10,18},{18,26},{... | collective-permute-start | bytes 1544 | tf_op jit(solution)/shard_map/while/body/eval_jaxpr/ppermute | solution.py:20
  172.6 7.3 %collective-permute-start.2 = (f32[4,1,130]{2,1,0:T(1,128)S(1)}, f32[4,1,130]{2,1,0:T(1,128)S(1)}, u32[]{:S(2)}, u32[]{:S(2)}) collective-permute-start(f32[4,1,130]{2,1,0:T(1,128)S(1)} %get-tuple-element.211), channel_id=1, source_target_pairs={{1,0},{2,1},{3,2},{4,3},{5,4},{6,5},{7,6},{9,8},{10,9},{11,10},{12... | collective-permute-start | bytes 6248 | tf_op jit(solution)/shard_map/while/body/eval_jaxpr/ppermute | solution.py:23
  173.9 6.8 %collective-permute-start.3 = (f32[4,1,130]{2,1,0:T(1,128)S(1)}, f32[4,1,130]{2,1,0:T(1,128)S(1)}, u32[]{:S(2)}, u32[]{:S(2)}) collective-permute-start(f32[4,1,130]{2,1,0:T(1,128)S(1)} %get-tuple-element.212), channel_id=1, source_target_pairs={{0,1},{1,2},{2,3},{3,4},{4,5},{5,6},{6,7},{8,9},{9,10},{10,11},{11... | collective-permute-start | bytes 6248 | tf_op jit(solution)/shard_map/while/body/eval_jaxpr/ppermute | solution.py:20
  181.9 6.2 %collective-permute-start = (f32[4,32,1]{2,1,0:T(8,128)S(1)}, f32[4,32,1]{2,1,0:T(8,128)S(1)}, u32[]{:S(2)}, u32[]{:S(2)}) collective-permute-start(f32[4,32,1]{2,1,0:T(8,128)S(1)} %get-tuple-element.209), channel_id=1, source_target_pairs={{8,0},{16,8},{24,16},{9,1},{17,9},{25,17},{10,2},{18,10},{26,18},{... | collective-permute-start | bytes 1544 | tf_op jit(solution)/shard_map/while/body/eval_jaxpr/ppermute | solution.py:23
  183.2 6.5 %collective-permute-start.1 = (f32[4,32,1]{2,1,0:T(8,128)S(1)}, f32[4,32,1]{2,1,0:T(8,128)S(1)}, u32[]{:S(2)}, u32[]{:S(2)}) collective-permute-start(f32[4,32,1]{2,1,0:T(8,128)S(1)} %get-tuple-element.210), channel_id=1, source_target_pairs={{0,8},{8,16},{16,24},{1,9},{9,17},{17,25},{2,10},{10,18},{18,26},{... | collective-permute-start | bytes 1544 | tf_op jit(solution)/shard_map/while/body/eval_jaxpr/ppermute | solution.py:20
  189.7 7.3 %collective-permute-start.2 = (f32[4,1,130]{2,1,0:T(1,128)S(1)}, f32[4,1,130]{2,1,0:T(1,128)S(1)}, u32[]{:S(2)}, u32[]{:S(2)}) collective-permute-start(f32[4,1,130]{2,1,0:T(1,128)S(1)} %get-tuple-element.211), channel_id=1, source_target_pairs={{1,0},{2,1},{3,2},{4,3},{5,4},{6,5},{7,6},{9,8},{10,9},{11,10},{12... | collective-permute-start | bytes 6248 | tf_op jit(solution)/shard_map/while/body/eval_jaxpr/ppermute | solution.py:23
  191.0 6.8 %collective-permute-start.3 = (f32[4,1,130]{2,1,0:T(1,128)S(1)}, f32[4,1,130]{2,1,0:T(1,128)S(1)}, u32[]{:S(2)}, u32[]{:S(2)}) collective-permute-start(f32[4,1,130]{2,1,0:T(1,128)S(1)} %get-tuple-element.212), channel_id=1, source_target_pairs={{0,1},{1,2},{2,3},{3,4},{4,5},{5,6},{6,7},{8,9},{9,10},{10,11},{11... | collective-permute-start | bytes 6248 | tf_op jit(solution)/shard_map/while/body/eval_jaxpr/ppermute | solution.py:20
  199.0 6.2 %collective-permute-start = (f32[4,32,1]{2,1,0:T(8,128)S(1)}, f32[4,32,1]{2,1,0:T(8,128)S(1)}, u32[]{:S(2)}, u32[]{:S(2)}) collective-permute-start(f32[4,32,1]{2,1,0:T(8,128)S(1)} %get-tuple-element.209), channel_id=1, source_target_pairs={{8,0},{16,8},{24,16},{9,1},{17,9},{25,17},{10,2},{18,10},{26,18},{... | collective-permute-start | bytes 1544 | tf_op jit(solution)/shard_map/while/body/eval_jaxpr/ppermute | solution.py:23
  200.3 6.5 %collective-permute-start.1 = (f32[4,32,1]{2,1,0:T(8,128)S(1)}, f32[4,32,1]{2,1,0:T(8,128)S(1)}, u32[]{:S(2)}, u32[]{:S(2)}) collective-permute-start(f32[4,32,1]{2,1,0:T(8,128)S(1)} %get-tuple-element.210), channel_id=1, source_target_pairs={{0,8},{8,16},{16,24},{1,9},{9,17},{17,25},{2,10},{10,18},{18,26},{... | collective-permute-start | bytes 1544 | tf_op jit(solution)/shard_map/while/body/eval_jaxpr/ppermute | solution.py:20
  206.9 7.3 %collective-permute-start.2 = (f32[4,1,130]{2,1,0:T(1,128)S(1)}, f32[4,1,130]{2,1,0:T(1,128)S(1)}, u32[]{:S(2)}, u32[]{:S(2)}) collective-permute-start(f32[4,1,130]{2,1,0:T(1,128)S(1)} %get-tuple-element.211), channel_id=1, source_target_pairs={{1,0},{2,1},{3,2},{4,3},{5,4},{6,5},{7,6},{9,8},{10,9},{11,10},{12... | collective-permute-start | bytes 6248 | tf_op jit(solution)/shard_map/while/body/eval_jaxpr/ppermute | solution.py:23
  208.2 6.8 %collective-permute-start.3 = (f32[4,1,130]{2,1,0:T(1,128)S(1)}, f32[4,1,130]{2,1,0:T(1,128)S(1)}, u32[]{:S(2)}, u32[]{:S(2)}) collective-permute-start(f32[4,1,130]{2,1,0:T(1,128)S(1)} %get-tuple-element.212), channel_id=1, source_target_pairs={{0,1},{1,2},{2,3},{3,4},{4,5},{5,6},{6,7},{8,9},{9,10},{10,11},{11... | collective-permute-start | bytes 6248 | tf_op jit(solution)/shard_map/while/body/eval_jaxpr/ppermute | solution.py:20
  217.3 5.9 %collective-permute-start.9 = (f32[8,1]{1,0:T(8,128)S(1)}, f32[8,1]{1,0:T(8,128)S(1)}, u32[]{:S(2)}, u32[]{:S(2)}) collective-permute-start(f32[8,1]{1,0:T(8,128)S(1)} %get-tuple-element.150), channel_id=1, source_target_pairs={{8,0},{16,8},{24,16},{9,1},{17,9},{25,17},{10,2},{18,10},{26,18},{... | collective-permute-start | bytes 104 | tf_op jit(solution)/shard_map/ppermute | solution.py:23
  218.6 5.9 %collective-permute-start.8 = (f32[8,1]{1,0:T(8,128)S(1)}, f32[8,1]{1,0:T(8,128)S(1)}, u32[]{:S(2)}, u32[]{:S(2)}) collective-permute-start(f32[8,1]{1,0:T(8,128)S(1)} %get-tuple-element.151), channel_id=1, source_target_pairs={{0,8},{8,16},{16,24},{1,9},{9,17},{17,25},{2,10},{10,18},{18,26},{... | collective-permute-start | bytes 104 | tf_op jit(solution)/shard_map/ppermute | solution.py:20
  224.6 7.3 %collective-permute-start.10 = (f32[1,34]{1,0:T(1,128)S(1)}, f32[1,34]{1,0:T(1,128)S(1)}, u32[]{:S(2)}, u32[]{:S(2)}) collective-permute-start(f32[1,34]{1,0:T(1,128)S(1)} %get-tuple-element.146), channel_id=1, source_target_pairs={{1,0},{2,1},{3,2},{4,3},{5,4},{6,5},{7,6},{9,8},{10,9},{11,10},{12... | collective-permute-start | bytes 416 | tf_op jit(solution)/shard_map/ppermute | solution.py:23
  225.9 6.7 %collective-permute-start.11 = (f32[1,34]{1,0:T(1,128)S(1)}, f32[1,34]{1,0:T(1,128)S(1)}, u32[]{:S(2)}, u32[]{:S(2)}) collective-permute-start(f32[1,34]{1,0:T(1,128)S(1)} %get-tuple-element.147), channel_id=1, source_target_pairs={{0,1},{1,2},{2,3},{3,4},{4,5},{5,6},{6,7},{8,9},{9,10},{10,11},{11... | collective-permute-start | bytes 416 | tf_op jit(solution)/shard_map/ppermute | solution.py:20
  331.4 3.2 collective-permute-start.12
  333.3 5.5 %collective-permute-start.13 = (f32[8,1]{1,0:T(8,128)S(1)}, f32[8,1]{1,0:T(8,128)S(1)}, u32[]{:S(2)}, u32[]{:S(2)}) collective-permute-start(f32[8,1]{1,0:T(8,128)S(1)} %get-tuple-element.145), channel_id=1, source_target_pairs={{8,0},{16,8},{24,16},{9,1},{17,9},{25,17},{10,2},{18,10},{26,18},{... | collective-permute-start | bytes 104 | tf_op jit(solution)/shard_map/ppermute | solution.py:23
  338.9 4.4 %collective-permute-start.14 = (f32[1,34]{1,0:T(1,128)S(1)}, f32[1,34]{1,0:T(1,128)S(1)}, u32[]{:S(2)}, u32[]{:S(2)}) collective-permute-start(f32[1,34]{1,0:T(1,128)S(1)} %get-tuple-element.142), channel_id=1, source_target_pairs={{1,0},{2,1},{3,2},{4,3},{5,4},{6,5},{7,6},{9,8},{10,9},{11,10},{12... | collective-permute-start | bytes 416 | tf_op jit(solution)/shard_map/ppermute | solution.py:23
  340.2 3.8 collective-permute-start.15
  (5 other events, 3.5 us)
where the time goes:
time: 393 us; the launch traced here: 390 us
  starting transfers between devices  178 us (45%)
  blocking collectives  137 us (35%)
  waiting for transfers between devices  45.5 us (12%)
  other arithmetic  16 us (4%)
  local copies, waits for them, and re-layouts  7.25 us (2%)
  between operations  4.9 us (1%)
    ppermute x30, starting transfers between devices, with_halo(): lax.ppermute(lax.slice_in_dim(block, block.shape[dim] - width, None, axis...  139 us
    psum x2, blocking collectives, weighted_total(): return lax.psum(jnp.sum(resid * precond), ('gx', 'gy'))  94 us
    psum x1, blocking collectives, shards(): step_size = weighted / lax.psum(jnp.sum(direction * image), ('gx', 'gy'))  43 us
    ppermute x30, starting transfers between devices, with_halo(): lax.ppermute(lax.slice_in_dim(block, 0, width, axis=dim), axis, backward)  38.8 us
    ppermute x30, waiting for transfers between devices, with_halo(): lax.ppermute(lax.slice_in_dim(block, block.shape[dim] - width, None, axis...  31.4 us
    ppermute x30, waiting for transfers between devices, with_halo(): lax.ppermute(lax.slice_in_dim(block, 0, width, axis=dim), axis, backward)  14.1 us
  transfers between devices with their start and end apart: 60, of which 43 were waited for; matrix products, arithmetic and copies ran while one was open for 0% of the time, Pallas kernels for 0%

commit v1 on v0

v1 whole, which is shorter than its diff:
```python
import functools

import jax
import jax.numpy as jnp
from jax import lax
from jax.experimental import pallas as pl
from jax.experimental.pallas import tpu as pltpu
from jax.sharding import PartitionSpec as P

SUBSTEPS = 12
TIME_STEP = 0.2
INFILTRATION = 0.05
MOVES = ((-1, -1), (-1, 0), (-1, 1), (0, -1), (0, 1), (1, -1), (1, 0), (1, 1))
AXES = ("gx", "gy")

WIDE = 20
SLIM = 12
LANES = 128
SLOTS = ((0, WIDE), (WIDE, WIDE), (2 * WIDE, WIDE), (3 * WIDE, WIDE)) + tuple(
    (4 * WIDE + k * SLIM, SLIM) for k in range(3)
)
EAST_AT = 4 * WIDE + 3 * SLIM
WEST_AT = EAST_AT + WIDE
COARSE_AT = WEST_AT + WIDE
STRIP = 168
F32 = jnp.float32


def whole(count):
    return [pl.BlockSpec(memory_space=pltpu.VMEM)] * count


def lane_ids(rows):
    return lax.broadcasted_iota(jnp.int32, (rows, LANES), 1)


def pack_columns(depth, tracers, rain, rough, codes, land_mask, leak, pump, active, own, first, last, coarse):
    land = land_mask[...].astype(F32)
    fields = [
        depth[...] * land,
        rain[...] * land * TIME_STEP,
        rough[...] * land * TIME_STEP,
        codes[...].astype(F32),
        tracers[0] * land,
        tracers[1] * land,
        tracers[2] * land,
    ]
    rows = land.shape[0]
    ids = lane_ids(rows)
    head = jnp.zeros((rows, LANES), F32)
    tail = jnp.zeros((rows, LANES), F32)
    for field, (at, width) in zip(fields, SLOTS):
        spot = (ids >= at) & (ids < at + width)
        head = jnp.where(spot, pltpu.roll(field, at, 1) if at else field, head)
        tail = jnp.where(spot, pltpu.roll(field, (at + width) % LANES, 1), tail)
    for k, field in enumerate(fields):
        own[k] = field
    act = active[...].astype(F32)
    weight = act / (act * (4.0 + leak[...]) + (1.0 - act))
    both = jnp.concatenate([weight, pump[...], jnp.zeros((act.shape[0], LANES - 2 * act.shape[1]), F32)], axis=1)
    coarse[...] = both
    first[0:rows] = head
    last[0:rows] = tail
    first[rows : rows + act.shape[0]] = both
    last[rows : rows + act.shape[0]] = both


def pack_rows(own, east, west, coarse, first, last):
    rows = own.shape[1]
    crows = coarse.shape[0]
    for k, (at, width) in enumerate(SLOTS):
        first[at : at + width] = own[k, 0:width]
        last[at : at + width] = own[k, rows - width : rows]
    for at, side in ((EAST_AT, east), (WEST_AT, west)):
        first[at : at + WIDE] = side[0:WIDE]
        last[at : at + WIDE] = side[rows - WIDE : rows]
    for at, part in ((COARSE_AT, coarse), (COARSE_AT + 2, east.at[rows : rows + crows]), (COARSE_AT + 4, west.at[rows : rows + crows])):
        first[at : at + 2] = part[0:2]
        last[at : at + 2] = part[crows - 2 : crows]
    first[COARSE_AT + 6 : STRIP] = jnp.zeros((STRIP - COARSE_AT - 6, LANES), F32)
    last[COARSE_AT + 6 : STRIP] = jnp.zeros((STRIP - COARSE_AT - 6, LANES), F32)


def inside(counts):
    col = lax.axis_index("gx")
    row = lax.axis_index("gy")
    return row > 0, row < counts[1] - 1, col < counts[0] - 1, col > 0


def gather_fields(kinds, halo, own, east, west, north, south, flags, stage):
    has_north, has_south, has_east, has_west = flags
    rows = own.shape[1]
    total = rows + 2 * halo
    chunk = total // 8

    def lay(slot, at, width, middle):
        stage[slot, 0:halo] = jnp.where(has_north, north[at + width - halo : at + width], 0.0)
        stage[slot, halo : halo + rows] = middle
        stage[slot, halo + rows : total] = jnp.where(has_south, south[at : at + halo], 0.0)

    def read(slot):
        return [stage[slot, pl.ds(i, 8, stride=chunk)] for i in range(chunk)]

    for k in kinds:
        at, width = SLOTS[k]
        lay(k, at, width, own[k])
    lay(7, EAST_AT, WIDE, east[0:rows])
    lay(8, WEST_AT, WIDE, west[0:rows])
    east_parts = read(7)
    west_parts = read(8)
    ids = lane_ids(8)
    fields = []
    for k in kinds:
        at, width = SLOTS[k]
        in_east = ids < jnp.where(has_east, width, 0)
        in_west = ids >= jnp.where(has_west, LANES - width, LANES)
        parts = []
        for main, e, w in zip(read(k), east_parts, west_parts):
            e = pltpu.roll(e, (LANES - at) % LANES, 1) if at else e
            w = pltpu.roll(w, (2 * LANES - width - at) % LANES, 1)
            side = jnp.where(in_east, e, jnp.where(in_west, w, 0.0))
            parts.append(jnp.concatenate([main, side], axis=1)[None])
        fields.append(jnp.concatenate(parts, axis=0))
    return fields


def from_left(field):
    return pltpu.roll(field, 1, 2)


def from_right(field):
    return pltpu.roll(field, field.shape[2] - 1, 2)


def from_above(field):
    return jnp.concatenate([pltpu.roll(field[-1], 1, 0)[None], field[:-1]], axis=0)


def from_below(field):
    return jnp.concatenate([field[1:], pltpu.roll(field[0], 7, 0)[None]], axis=0)


def move_masks(codes, coef, masks):
    land = coef > 0.0
    sides = {-1: from_right(codes), 0: codes, 1: from_left(codes)}
    for k, (drow, dcol) in enumerate(MOVES):
        seen = sides[dcol]
        if drow == 1:
            seen = from_above(seen)
        elif drow == -1:
            seen = from_below(seen)
        masks[k] = jnp.where(land & (seen == float(k)), 1.0, 0.0)


def inflow(flux, masks):
    sides = {-1: from_right(flux), 0: flux, 1: from_left(flux)}
    total = None
    for dcol in (0, 1, -1):
        side = sides[dcol]
        for drow, seen in ((0, side), (1, from_above(side)), (-1, from_below(side))):
            if (drow, dcol) == (0, 0):
                continue
            term = masks[MOVES.index((drow, dcol))] * seen
            total = term if total is None else total + term
    return total


def speed(depth, coef):
    return coef * jnp.exp(jnp.log(jnp.abs(depth)) * (2.0 / 3.0))


KEEP = 1.0 - TIME_STEP * INFILTRATION


def depth_kernel(counts, own, east, west, north, south, coarse, sums, zc, uc, stage, masks, cst):
    flags = inside(counts)
    depth, rain, coef, codes = gather_fields((0, 1, 2, 3), WIDE, own, east, west, north, south, flags, stage)
    move_masks(codes, coef, masks)

    def step(_, carry):
        now, total = carry
        flux = speed(now, coef) * now
        return now * KEEP - flux + rain + inflow(flux, masks), total + now

    now, total = lax.fori_loop(0, SUBSTEPS - 1, step, (depth, jnp.zeros_like(depth)))
    total = total + now
    chunk = total.shape[0]
    for i in range(chunk):
        stage[0, pl.ds(i, 8, stride=chunk)] = total[i, :, :LANES]
        stage[1, pl.ds(i, 8, stride=chunk)] = total[i, :, LANES:]
    blocks = []
    for b in range(2):
        quads = [stage[b, pl.ds(8 + j, 16, stride=4)] for j in range(4)]
        blocks.append((quads[0] + quads[1]) + (quads[2] + quads[3]))
    pooled = jnp.concatenate(blocks, axis=1)
    crows, ccols = zc.shape[0], LANES // 4
    fine = lax.broadcasted_iota(jnp.int32, (2 * LANES, LANES), 0)
    cell = lax.broadcasted_iota(jnp.int32, (2 * LANES, LANES), 1)
    place = lax.shift_right_logical(fine, 2)
    near = fine < LANES + 8
    far = fine >= 2 * LANES - 8
    hit = (near & (place == cell)) | (far & (place - (2 * LANES // 4 - 2) == cell - (LANES - 2)))
    rc = jnp.dot(
        pooled,
        jnp.where(hit, 1.0, 0.0),
        precision=lax.Precision.HIGHEST,
        preferred_element_type=F32,
    ) * (INFILTRATION * TIME_STEP)

    has_north, has_south, has_east, has_west = flags
    rows = own.shape[1]
    for k, middle in enumerate((coarse[...], east[rows : rows + crows], west[rows : rows + crows])):
        at = COARSE_AT + 2 * k
        cst[k] = jnp.zeros((16, LANES), F32)
        cst[k, 1:3] = jnp.where(has_north, north[at : at + 2], 0.0)
        cst[k, 3 : 3 + crows] = middle
        cst[k, 3 + crows : 5 + crows] = jnp.where(has_south, south[at : at + 2], 0.0)
    ids = lane_ids(16)
    e_here = (ids >= ccols) & (ids < jnp.where(has_east, ccols + 2, ccols))
    w_here = ids >= jnp.where(has_west, LANES - 2, LANES)
    pair = []
    for shift in (0, ccols):
        main = pltpu.roll(cst[0], LANES - shift, 1) if shift else cst[0]
        e = pltpu.roll(cst[1], (LANES + ccols - shift) % LANES, 1) if shift != ccols else cst[1]
        w = pltpu.roll(cst[2], (2 * LANES - ccols - shift) % LANES, 1)
        pair.append(jnp.where(ids < ccols, main, jnp.where(e_here, e, jnp.where(w_here, w, 0.0))))
    weight, pump = pair

    def beside(v):
        return (pltpu.roll(v, 1, 1) + pltpu.roll(v, LANES - 1, 1)) + (pltpu.roll(v, 1, 0) + pltpu.roll(v, 15, 0))

    drive = rc - pump
    z = weight * drive
    nz = beside(z)
    u = weight * nz
    nu = beside(u)
    mine = (ids < ccols)[3 : 3 + crows]
    cut = lambda v: v[3 : 3 + crows]
    z, nz, u, nu, drive = cut(z), cut(nz), cut(u), cut(nu), cut(drive)
    z = jnp.where(mine, z, 0.0)
    u = jnp.where(mine, u, 0.0)
    lines = [jnp.sum(a * b, axis=0, keepdims=True) for a, b in ((drive, z), (z, nz), (u, nz), (u, nu))]
    sums[...] = jnp.concatenate(lines + [jnp.zeros((4, LANES), F32)], axis=0)
    zc[...] = z
    uc[...] = u


def state_kernel(counts, own, east, west, north, south, depth_out, tracers_out, stage, masks):
    flags = inside(counts)
    depth, rain, coef, codes, *species = gather_fields(
        (0, 1, 2, 3, 4, 5, 6), SLIM, own, east, west, north, south, flags, stage
    )
    move_masks(codes, coef, masks)

    def step(_, carry):
        now = carry[0]
        rate = speed(now, coef)
        flux = rate * now
        new = [now * KEEP - flux + rain + inflow(flux, masks)]
        for held in carry[1:]:
            flux = rate * held
            new.append(held * KEEP - flux + inflow(flux, masks))
        return tuple(new)

    final = lax.fori_loop(0, SUBSTEPS, step, (depth, *species))
    chunk = depth.shape[0]
    rows = own.shape[1]
    for k, field in enumerate(final):
        for i in range(chunk):
            stage[k, pl.ds(i, 8, stride=chunk)] = field[i, :, :LANES]
        if k == 0:
            depth_out[...] = stage[k, SLIM : SLIM + rows]
        else:
            tracers_out[k - 1] = stage[k, SLIM : SLIM + rows]


def head_kernel(sums, zc, uc, head):
    n = jnp.sum(sums[...], axis=1, keepdims=True)
    n0, n1, n2, n3 = n[0:1], n[1:2], n[2:3], n[3:4]
    pq = n0 - n1
    a0 = n0 / pq
    ratio = (n0 * n2 - n1 * n1) / (pq * pq)
    slope = (n1 - n2) / pq
    below = (n2 - n3) - slope * (n1 - n2)
    a1 = jnp.where(below > 0.0, n0 * ratio / jnp.where(below > 0.0, below, 1.0), 0.0) / a0
    wide = head.shape[1]
    head[...] = ((a0 - a1 * slope) * zc[...] + a1 * uc[...])[:, :wide]


def ring(shift, axis, counts):
    size = counts[AXES.index(axis)]
    return [(i, (i + shift) % size) for i in range(size)]


def exchange(first, last, axis, counts):
    after = lax.ppermute(first, axis, ring(-1, axis, counts))
    before = lax.ppermute(last, axis, ring(1, axis, counts))
    return after, before


def everywhere(value, counts):
    size = counts[0] * counts[1]
    if size & (size - 1):
        return lax.psum(value, AXES)
    bit = 1
    while bit < size:
        value = value + lax.ppermute(value, AXES, [(i, i ^ bit) for i in range(size)])
        bit *= 2
    return value


def shards(counts, water_depth, tracers, rainfall, roughness, flow_codes, land_mask, leakance, pumping, active):
    rows, cols = water_depth.shape
    crows, ccols = leakance.shape
    shape = lambda *dims: jax.ShapeDtypeStruct(dims, F32)
    own, first, last, coarse = pl.pallas_call(
        pack_columns,
        out_shape=(shape(7, rows, cols), shape(rows + crows, LANES), shape(rows + crows, LANES), shape(crows, LANES)),
        in_specs=whole(9),
        out_specs=tuple(whole(4)),
        name="pack_columns",
    )(water_depth, tracers, rainfall, roughness, flow_codes, land_mask, leakance, pumping, active)
    east, west = exchange(first, last, "gx", counts)
    first, last = pl.pallas_call(
        pack_rows,
        out_shape=(shape(STRIP, LANES), shape(STRIP, LANES)),
        in_specs=whole(4),
        out_specs=tuple(whole(2)),
        name="pack_rows",
    )(own, east, west, coarse)
    south, north = exchange(first, last, "gy", counts)
    deep = rows + 2 * WIDE
    sums, zc, uc = pl.pallas_call(
        functools.partial(depth_kernel, counts),
        out_shape=(shape(8, LANES), shape(crows, LANES), shape(crows, LANES)),
        in_specs=whole(6),
        out_specs=tuple(whole(3)),
        scratch_shapes=[
            pltpu.VMEM((9, deep, LANES), F32),
            pltpu.VMEM((8, deep // 8, 8, 2 * LANES), F32),
            pltpu.VMEM((3, 16, LANES), F32),
        ],
        name="depth_and_moments",
    )(own, east, west, north, south, coarse)
    low = rows + 2 * SLIM
    depth_out, tracers_out = pl.pallas_call(
        functools.partial(state_kernel, counts),
        out_shape=(shape(rows, cols), shape(3, rows, cols)),
        in_specs=whole(5),
        out_specs=tuple(whole(2)),
        scratch_shapes=[
            pltpu.VMEM((9, low, LANES), F32),
            pltpu.VMEM((8, low // 8, 8, 2 * LANES), F32),
        ],
        cost_estimate=pl.CostEstimate(flops=20_000_000, bytes_accessed=20_000_000, transcendentals=0),
        name="all_channels",
    )(own, east, west, north, south)
    sums = everywhere(sums, counts)
    head = pl.pallas_call(
        head_kernel,
        out_shape=shape(crows, ccols),
        in_specs=whole(3),
        out_specs=pl.BlockSpec(memory_space=pltpu.VMEM),
        name="combine_head",
    )(sums, zc, uc)
    return depth_out, tracers_out, head


def solution(mesh):
    counts = (mesh.shape["gx"], mesh.shape["gy"])
    tile = P("gy", "gx")
    deep = P(None, "gy", "gx")
    return jax.shard_map(
        functools.partial(shards, counts),
        mesh=mesh,
        in_specs=(tile, deep) + (tile,) * 7,
        out_specs=(tile, deep, tile),
        check_vma=False,
    )
```

time: 393 us -> 45.6 us (0.12)
  starting transfers between devices: 178 us -> 11.5 us
  blocking collectives: 137 us -> 0 us
  waiting for transfers between devices: 45.5 us -> 16.7 us
  other arithmetic: 16 us -> 1.3 us
  Pallas kernels: 0 us -> 13.3 us
  local copies, waits for them, and re-layouts: 7.25 us -> 1.82 us
  between operations: 4.9 us -> 0.65 us
    ppermute x60 -> x9, starting transfers between devices: 178 us -> 11.5 us  [the longest x2 7.69 us: exchange(): after = lax.ppermute(first, axis, ring(-1, axis, counts))]
    psum x3 -> x0, blocking collectives: 137 us -> none  [the longest x2 94 us: weighted_total(): return lax.psum(jnp.sum(resid * precond), ('gx', 'gy'))]
    ppermute x60 -> x9, waiting for transfers between devices: 45.5 us -> 16.7 us  [the longest x5 8.47 us: everywhere(): lax.ppermute(value, AXES, [(i, i ^ bit) for i in range(size)])]
    pallas_call x0 -> x5, Pallas kernels: none -> 13.3 us  [the longest x1 4.89 us: shards(): pl.pallas_call(functools.partial(state_kernel, counts), out_shape=(shape(...]
    slice x42 -> x0, local copies, waits for them, and re-layouts: 4.06 us -> none  [the longest x12 1.35 us: shift_into(): lax.slice(padded, (0, 1 - drow, 1 - dcol), (field.shape[0], 1 - drow + he...]
  transfers between devices with their start and end apart: 60 -> 9, of which waited for: 43 -> 7; matrix products, arithmetic and copies ran while one was open for 0% -> 0% of each run, Pallas kernels for 0% -> 11%
where the time goes in v1:
time: 45.6 us; the launch traced here: 45.2 us
  waiting for transfers between devices  16.7 us (37%)
  Pallas kernels  13.3 us (29%)
  starting transfers between devices  11.5 us (25%)
  local copies, waits for them, and re-layouts  1.82 us (4%)
  other arithmetic  1.3 us (3%)
  between operations  0.65 us (1%)
    ppermute x5, waiting for transfers between devices, everywhere(): lax.ppermute(value, AXES, [(i, i ^ bit) for i in range(size)])  8.47 us
    ppermute x2, starting transfers between devices, exchange(): after = lax.ppermute(first, axis, ring(-1, axis, counts))  7.69 us
    ppermute x2, waiting for transfers between devices, exchange(): before = lax.ppermute(last, axis, ring(1, axis, counts))  6.47 us
    pallas_call x1, Pallas kernels, shards(): pl.pallas_call(functools.partial(state_kernel, counts), out_shape=(shape(...  4.89 us
    ppermute x5, starting transfers between devices, everywhere(): lax.ppermute(value, AXES, [(i, i ^ bit) for i in range(size)])  3.83 us
    pallas_call x1, Pallas kernels, shards(): pl.pallas_call(functools.partial(depth_kernel, counts), out_shape=(shape(...  3.8 us
    unnamed x8, local copies, waits for them, and re-layouts  1.82 us
    ppermute x2, waiting for transfers between devices, exchange(): after = lax.ppermute(first, axis, ring(-1, axis, counts))  1.73 us
  transfers between devices with their start and end apart: 9, of which 7 were waited for; matrix products, arithmetic and copies ran while one was open for 0% of the time, Pallas kernels for 11%

profile of v1, /device:TPU:0, one launch (start us, length us, event | category | flops | bytes accessed | tf_op | source)
XLA Modules:
  0.0 45.2 jit_solution(4485950106471612452)
XLA Ops:
  0.6 1.6 %pack_columns.1 = (f32[7,32,128]{2,1,0:T(8,128)}, f32[40,128]{1,0:T(8,128)}, f32[40,128]{1,0:T(8,128)}, f32[8,128]{1,0:T(8,128)}) custom-call(f32[32,128]{1,0:T(8,128)} %depth.1, f32[3,32,128]{2,1,0:T(8,128)} %tracers.1, f32[32,128]{1,0:T(8,128)} %rain.1, f32[32,128]{1,0:T(8,128)} %rough.1, s32[32,128]{1,0:T(8,128)} %codes.1, s32[32,128]{1,0:T(8,128)} %land_mask.1, ...), custom_call_target="tpu_custom_call" | custom-call | tf_op jit(solution)/shard_map/pack_columns/pallas_call | solution.py:316
  2.2 5.0 %collective-permute-start = (f32[40,128]{1,0:T(8,128)}, f32[40,128]{1,0:T(8,128)S(1)}, u32[]{:S(2)}, u32[]{:S(2)}) collective-permute-start(f32[40,128]{1,0:T(8,128)} %get-tuple-element.15), channel_id=1, source_target_pairs={{0,24},{8,0},{16,8},{24,16},{1,25},{9,1},{17,9},{25,17},{2,26},{10... | collective-permute-start | bytes 61448 | tf_op jit(solution)/shard_map/ppermute | solution.py:296
  7.2 0.0 collective-permute-start.1
  7.2 1.7 %collective-permute-done.east = f32[40,128]{1,0:T(8,128)S(1)} collective-permute-done((f32[40,128]{1,0:T(8,128)}, f32[40,128]{1,0:T(8,128)S(1)}, u32[]{:S(2)}, u32[]{:S(2)}) %collective-permute-start) | collective-permute-done | bytes 20512 | tf_op jit(solution)/shard_map/ppermute | solution.py:296
  8.9 0.0 copy-start.2
  8.9 4.1 %collective-permute-done.1.west = f32[40,128]{1,0:T(8,128)S(1)} collective-permute-done((f32[40,128]{1,0:T(8,128)}, f32[40,128]{1,0:T(8,128)S(1)}, u32[]{:S(2)}, u32[]{:S(2)}) %collective-permute-start.1) | collective-permute-done | bytes 20512 | tf_op jit(solution)/shard_map/ppermute | solution.py:297
  13.0 0.0 copy-start.3
  13.0 0.0 copy-done.2
  13.0 0.6 %copy-done.3 = f32[40,128]{1,0:T(8,128)} copy-done((f32[40,128]{1,0:T(8,128)}, f32[40,128]{1,0:T(8,128)S(1)}, u32[]{:S(2)}) %copy-start.3) | copy-done | bytes 20504
  13.6 1.6 %pack_rows.1 = (f32[168,128]{1,0:T(8,128)}, f32[168,128]{1,0:T(8,128)}) custom-call(f32[7,32,128]{2,1,0:T(8,128)} %get-tuple-element.14.own, f32[40,128]{1,0:T(8,128)} %copy-done.2, f32[40,128]{1,0:T(8,128)} %copy-done.3, f32[8,128]{1,0:T(8,128)} %get-tuple-element.17.coarse), custom_call_target="tpu_custom_call" | custom-call | tf_op jit(solution)/shard_map/pack_rows/pallas_call | solution.py:324
  15.2 0.0 collective-permute-start.2
  15.2 2.6 %collective-permute-start.3 = (f32[168,128]{1,0:T(8,128)}, f32[168,128]{1,0:T(8,128)S(1)}, u32[]{:S(2)}, u32[]{:S(2)}) collective-permute-start(f32[168,128]{1,0:T(8,128)} %get-tuple-element.19), channel_id=1, source_target_pairs={{0,7},{1,0},{2,1},{3,2},{4,3},{5,4},{6,5},{7,6},{8,15},{9,8},{10,9... | collective-permute-start | bytes 258056 | tf_op jit(solution)/shard_map/ppermute | solution.py:296
  17.9 2.4 %collective-permute-done.2.north = f32[168,128]{1,0:T(8,128)S(1)} collective-permute-done((f32[168,128]{1,0:T(8,128)}, f32[168,128]{1,0:T(8,128)S(1)}, u32[]{:S(2)}, u32[]{:S(2)}) %collective-permute-start.2) | collective-permute-done | bytes 86048 | tf_op jit(solution)/shard_map/ppermute | solution.py:297
  20.3 0.0 copy-start
  20.3 0.0 collective-permute-done.3.south
  20.3 0.6 %copy-done = f32[168,128]{1,0:T(8,128)} copy-done((f32[168,128]{1,0:T(8,128)}, f32[168,128]{1,0:T(8,128)S(1)}, u32[]{:S(2)}) %copy-start) | copy-done | bytes 86040
  20.9 0.0 copy-start.1
  20.9 0.6 %copy-done.1 = f32[168,128]{1,0:T(8,128)} copy-done((f32[168,128]{1,0:T(8,128)}, f32[168,128]{1,0:T(8,128)S(1)}, u32[]{:S(2)}) %copy-start.1) | copy-done | bytes 86040
  21.5 3.8 %depth_and_moments.1 = (f32[8,128]{1,0:T(8,128)}, f32[8,128]{1,0:T(8,128)}, f32[8,128]{1,0:T(8,128)}) custom-call(f32[7,32,128]{2,1,0:T(8,128)} %get-tuple-element.14.own, f32[40,128]{1,0:T(8,128)} %copy-done.2, f32[40,128]{1,0:T(8,128)} %copy-done.3, f32[168,128]{1,0:T(8,128)} %copy-done, f32[168,128]{1,0:T(8,128)} %copy-done.1, ...), custom_call_target="tpu_custom_call" | custom-call | tf_op jit(solution)/shard_map/depth_and_moments/pallas_call | solution.py:333
  25.3 0.2 collective-permute-start.4
  25.5 1.2 %collective-permute-done.4 = f32[8,128]{1,0:T(8,128)S(1)} collective-permute-done((f32[8,128]{1,0:T(8,128)}, f32[8,128]{1,0:T(8,128)S(1)}, u32[]{:S(2)}, u32[]{:S(2)}) %collective-permute-start.4) | collective-permute-done | bytes 4128 | tf_op jit(solution)/shard_map/ppermute | solution.py:307
  26.7 0.7 %add.15 = f32[8,128]{1,0:T(8,128)S(1)} add(f32[8,128]{1,0:T(8,128)} %get-tuple-element.22, f32[8,128]{1,0:T(8,128)S(1)} %collective-permute-done.4) | non-fusion elementwise | flops 1024 | bytes 12288 | tf_op jit(solution)/shard_map/add | solution.py:307
  27.4 2.1 %collective-permute-start.5 = (f32[8,128]{1,0:T(8,128)S(1)}, f32[8,128]{1,0:T(8,128)S(1)}, u32[]{:S(2)}, u32[]{:S(2)}) collective-permute-start(f32[8,128]{1,0:T(8,128)S(1)} %add.15), channel_id=1, source_target_pairs={{0,2},{1,3},{2,0},{3,1},{4,6},{5,7},{6,4},{7,5},{8,10},{9,11},{10,... | collective-permute-start | bytes 12296 | tf_op jit(solution)/shard_map/ppermute | solution.py:307
  29.5 1.6 %collective-permute-done.5 = f32[8,128]{1,0:T(8,128)S(1)} collective-permute-done((f32[8,128]{1,0:T(8,128)S(1)}, f32[8,128]{1,0:T(8,128)S(1)}, u32[]{:S(2)}, u32[]{:S(2)}) %collective-permute-start.5) | collective-permute-done | bytes 4128 | tf_op jit(solution)/shard_map/ppermute | solution.py:307
  31.1 1.5 %collective-permute-start.6 = (f32[8,128]{1,0:T(8,128)S(1)}, f32[8,128]{1,0:T(8,128)S(1)}, u32[]{:S(2)}, u32[]{:S(2)}) collective-permute-start(f32[8,128]{1,0:T(8,128)S(1)} %add.16), channel_id=1, source_target_pairs={{0,4},{1,5},{2,6},{3,7},{4,0},{5,1},{6,2},{7,3},{8,12},{9,13},{10,... | collective-permute-start | bytes 12296 | tf_op jit(solution)/shard_map/ppermute | solution.py:307
  32.6 2.1 %collective-permute-done.6 = f32[8,128]{1,0:T(8,128)S(1)} collective-permute-done((f32[8,128]{1,0:T(8,128)S(1)}, f32[8,128]{1,0:T(8,128)S(1)}, u32[]{:S(2)}, u32[]{:S(2)}) %collective-permute-start.6) | collective-permute-done | bytes 4128 | tf_op jit(solution)/shard_map/ppermute | solution.py:307
  34.7 0.0 collective-permute-start.7
  34.7 3.6 %collective-permute-done.7 = f32[8,128]{1,0:T(8,128)S(1)} collective-permute-done((f32[8,128]{1,0:T(8,128)S(1)}, f32[8,128]{1,0:T(8,128)S(1)}, u32[]{:S(2)}, u32[]{:S(2)}) %collective-permute-start.7) | collective-permute-done | bytes 4128 | tf_op jit(solution)/shard_map/ppermute | solution.py:307
  38.3 0.0 collective-permute-start.8
  38.3 4.9 %all_channels.1 = (f32[32,128]{1,0:T(8,128)}, f32[3,32,128]{2,1,0:T(8,128)}) custom-call(f32[7,32,128]{2,1,0:T(8,128)} %get-tuple-element.14.own, f32[40,128]{1,0:T(8,128)} %copy-done.2, f32[40,128]{1,0:T(8,128)} %copy-done.3, f32[168,128]{1,0:T(8,128)} %copy-done, f32[168,128]{1,0:T(8,128)} %copy-done.1), custom_call_target="tpu_custom_call" | custom-call | flops 20000000 | bytes 20000000 | tf_op jit(solution)/shard_map/all_channels/pallas_call | solution.py:346
  43.2 0.0 collective-permute-done.8
  43.2 0.6 %add.19.sums = f32[8,128]{1,0:T(8,128)} add(f32[8,128]{1,0:T(8,128)S(1)} %add.18, f32[8,128]{1,0:T(8,128)S(1)} %collective-permute-done.8) | non-fusion elementwise | flops 1024 | bytes 12288 | tf_op jit(solution)/shard_map/add | solution.py:307
  43.8 1.4 %combine_head.1 = f32[8,32]{1,0:T(8,128)} custom-call(f32[8,128]{1,0:T(8,128)} %add.19.sums, f32[8,128]{1,0:T(8,128)} %get-tuple-element.23.zc, f32[8,128]{1,0:T(8,128)} %get-tuple-element.24.uc), custom_call_target="tpu_custom_call" | custom-call | tf_op jit(solution)/shard_map/combine_head/pallas_call | solution.py:359
  (3 shorter events, 0.0 us)
Async XLA Ops:
  2.2 6.7 %collective-permute-start = (f32[40,128]{1,0:T(8,128)}, f32[40,128]{1,0:T(8,128)S(1)}, u32[]{:S(2)}, u32[]{:S(2)}) collective-permute-start(f32[40,128]{1,0:T(8,128)} %get-tuple-element.15), channel_id=1, source_target_pairs={{0,24},{8,0},{16,8},{24,16},{1,25},{9,1},{17,9},{25,17},{2,26},{10... | collective-permute-start | bytes 61448 | tf_op jit(solution)/shard_map/ppermute | solution.py:296
  7.2 5.8 %collective-permute-start.1 = (f32[40,128]{1,0:T(8,128)}, f32[40,128]{1,0:T(8,128)S(1)}, u32[]{:S(2)}, u32[]{:S(2)}) collective-permute-start(f32[40,128]{1,0:T(8,128)} %get-tuple-element.16), channel_id=1, source_target_pairs={{0,8},{8,16},{16,24},{24,0},{1,9},{9,17},{17,25},{25,1},{2,10},{10... | collective-permute-start | bytes 61448 | tf_op jit(solution)/shard_map/ppermute | solution.py:297
  8.9 4.1 %copy-start.2 = (f32[40,128]{1,0:T(8,128)}, f32[40,128]{1,0:T(8,128)S(1)}, u32[]{:S(2)}) copy-start(f32[40,128]{1,0:T(8,128)S(1)} %collective-permute-done.east) | copy-start | bytes 61444
  13.0 0.6 %copy-start.3 = (f32[40,128]{1,0:T(8,128)}, f32[40,128]{1,0:T(8,128)S(1)}, u32[]{:S(2)}) copy-start(f32[40,128]{1,0:T(8,128)S(1)} %collective-permute-done.1.west) | copy-start | bytes 61444
  15.2 5.0 %collective-permute-start.2 = (f32[168,128]{1,0:T(8,128)}, f32[168,128]{1,0:T(8,128)S(1)}, u32[]{:S(2)}, u32[]{:S(2)}) collective-permute-start(f32[168,128]{1,0:T(8,128)} %get-tuple-element.18), channel_id=1, source_target_pairs={{0,1},{1,2},{2,3},{3,4},{4,5},{5,6},{6,7},{7,0},{8,9},{9,10},{10,1... | collective-permute-start | bytes 258056 | tf_op jit(solution)/shard_map/ppermute | solution.py:297
  15.2 5.1 %collective-permute-start.3 = (f32[168,128]{1,0:T(8,128)}, f32[168,128]{1,0:T(8,128)S(1)}, u32[]{:S(2)}, u32[]{:S(2)}) collective-permute-start(f32[168,128]{1,0:T(8,128)} %get-tuple-element.19), channel_id=1, source_target_pairs={{0,7},{1,0},{2,1},{3,2},{4,3},{5,4},{6,5},{7,6},{8,15},{9,8},{10,9... | collective-permute-start | bytes 258056 | tf_op jit(solution)/shard_map/ppermute | solution.py:296
  20.3 0.6 %copy-start = (f32[168,128]{1,0:T(8,128)}, f32[168,128]{1,0:T(8,128)S(1)}, u32[]{:S(2)}) copy-start(f32[168,128]{1,0:T(8,128)S(1)} %collective-permute-done.2.north) | copy-start | bytes 258052
  20.9 0.6 %copy-start.1 = (f32[168,128]{1,0:T(8,128)}, f32[168,128]{1,0:T(8,128)S(1)}, u32[]{:S(2)}) copy-start(f32[168,128]{1,0:T(8,128)S(1)} %collective-permute-done.3.south) | copy-start | bytes 258052
  25.3 1.4 %collective-permute-start.4 = (f32[8,128]{1,0:T(8,128)}, f32[8,128]{1,0:T(8,128)S(1)}, u32[]{:S(2)}, u32[]{:S(2)}) collective-permute-start(f32[8,128]{1,0:T(8,128)} %get-tuple-element.22), channel_id=1, source_target_pairs={{0,1},{1,0},{2,3},{3,2},{4,5},{5,4},{6,7},{7,6},{8,9},{9,8},{10,11... | collective-permute-start | bytes 12296 | tf_op jit(solution)/shard_map/ppermute | solution.py:307
  27.4 3.7 %collective-permute-start.5 = (f32[8,128]{1,0:T(8,128)S(1)}, f32[8,128]{1,0:T(8,128)S(1)}, u32[]{:S(2)}, u32[]{:S(2)}) collective-permute-start(f32[8,128]{1,0:T(8,128)S(1)} %add.15), channel_id=1, source_target_pairs={{0,2},{1,3},{2,0},{3,1},{4,6},{5,7},{6,4},{7,5},{8,10},{9,11},{10,... | collective-permute-start | bytes 12296 | tf_op jit(solution)/shard_map/ppermute | solution.py:307
  31.1 3.6 %collective-permute-start.6 = (f32[8,128]{1,0:T(8,128)S(1)}, f32[8,128]{1,0:T(8,128)S(1)}, u32[]{:S(2)}, u32[]{:S(2)}) collective-permute-start(f32[8,128]{1,0:T(8,128)S(1)} %add.16), channel_id=1, source_target_pairs={{0,4},{1,5},{2,6},{3,7},{4,0},{5,1},{6,2},{7,3},{8,12},{9,13},{10,... | collective-permute-start | bytes 12296 | tf_op jit(solution)/shard_map/ppermute | solution.py:307
  34.7 3.6 %collective-permute-start.7 = (f32[8,128]{1,0:T(8,128)S(1)}, f32[8,128]{1,0:T(8,128)S(1)}, u32[]{:S(2)}, u32[]{:S(2)}) collective-permute-start(f32[8,128]{1,0:T(8,128)S(1)} %add.17), channel_id=1, source_target_pairs={{0,8},{1,9},{2,10},{3,11},{4,12},{5,13},{6,14},{7,15},{8,0},{9,1},... | collective-permute-start | bytes 12296 | tf_op jit(solution)/shard_map/ppermute | solution.py:307
  38.3 4.9 %collective-permute-start.8 = (f32[8,128]{1,0:T(8,128)S(1)}, f32[8,128]{1,0:T(8,128)S(1)}, u32[]{:S(2)}, u32[]{:S(2)}) collective-permute-start(f32[8,128]{1,0:T(8,128)S(1)} %add.18), channel_id=1, source_target_pairs={{0,16},{1,17},{2,18},{3,19},{4,20},{5,21},{6,22},{7,23},{8,24},{9,... | collective-permute-start | bytes 12296 | tf_op jit(solution)/shard_map/ppermute | solution.py:307

commit v2 on v1

--- a/solution.py
+++ b/solution.py
@@ -24,6 +24,8 @@
 COARSE_AT = WEST_AT + WIDE
 STRIP = 168
 F32 = jnp.float32
+SMALL = pltpu.CompilerParams(vmem_limit_bytes=2 << 20)
+ROOMY = pltpu.CompilerParams(vmem_limit_bytes=6 << 20)
 
 
 def whole(count):
@@ -34,7 +36,14 @@
     return lax.broadcasted_iota(jnp.int32, (rows, LANES), 1)
 
 
-def pack_columns(depth, tracers, rain, rough, codes, land_mask, leak, pump, active, own, first, last, coarse):
+def pack_columns(*refs):
+    sources, (own, first, last, coarse), buffers, done = refs[:9], refs[9:13], refs[13:22], refs[22]
+    copies = [pltpu.make_async_copy(a, b, done.at[k]) for k, (a, b) in enumerate(zip(sources, buffers))]
+    for copy in copies:
+        copy.start()
+    for copy in copies:
+        copy.wait()
+    depth, tracers, rain, rough, codes, land_mask, leak, pump, active = buffers
     land = land_mask[...].astype(F32)
     fields = [
         depth[...] * land,
@@ -239,8 +248,12 @@
     z, nz, u, nu, drive = cut(z), cut(nz), cut(u), cut(nu), cut(drive)
     z = jnp.where(mine, z, 0.0)
     u = jnp.where(mine, u, 0.0)
-    lines = [jnp.sum(a * b, axis=0, keepdims=True) for a, b in ((drive, z), (z, nz), (u, nz), (u, nu))]
-    sums[...] = jnp.concatenate(lines + [jnp.zeros((4, LANES), F32)], axis=0)
+    row = jnp.zeros((crows, LANES), F32)
+    for k, (a, b) in enumerate(((drive, z), (z, nz), (u, nz), (u, nu))):
+        part = a * b
+        row = row + (pltpu.roll(part, k * ccols, 1) if k else part)
+    row = jnp.sum(row, axis=0, keepdims=True)
+    sums[...] = jnp.broadcast_to(row, sums.shape)
     zc[...] = z
     uc[...] = u
 
@@ -275,8 +288,13 @@
 
 
 def head_kernel(sums, zc, uc, head):
-    n = jnp.sum(sums[...], axis=1, keepdims=True)
-    n0, n1, n2, n3 = n[0:1], n[1:2], n[2:3], n[3:4]
+    total = jnp.sum(sums[...], axis=0, keepdims=True)
+    run = LANES // 4
+    ids = lane_ids(1)
+    n0, n1, n2, n3 = (
+        jnp.sum(jnp.where((ids >= k * run) & (ids < (k + 1) * run), total, 0.0), axis=1, keepdims=True)
+        for k in range(4)
+    )
     pq = n0 - n1
     a0 = n0 / pq
     ratio = (n0 * n2 - n1 * n1) / (pq * pq)
@@ -298,41 +316,33 @@
     return after, before
 
 
-def everywhere(value, counts):
-    size = counts[0] * counts[1]
-    if size & (size - 1):
-        return lax.psum(value, AXES)
-    bit = 1
-    while bit < size:
-        value = value + lax.ppermute(value, AXES, [(i, i ^ bit) for i in range(size)])
-        bit *= 2
-    return value
-
-
-def shards(counts, water_depth, tracers, rainfall, roughness, flow_codes, land_mask, leakance, pumping, active):
-    rows, cols = water_depth.shape
-    crows, ccols = leakance.shape
+def shards(counts, *inputs):
+    rows, cols = inputs[0].shape
+    crows, ccols = inputs[6].shape
     shape = lambda *dims: jax.ShapeDtypeStruct(dims, F32)
     own, first, last, coarse = pl.pallas_call(
         pack_columns,
         out_shape=(shape(7, rows, cols), shape(rows + crows, LANES), shape(rows + crows, LANES), shape(crows, LANES)),
-        in_specs=whole(9),
+        in_specs=[pl.BlockSpec(memory_space=pltpu.MemorySpace.HBM)] * 9,
         out_specs=tuple(whole(4)),
+        scratch_shapes=[pltpu.VMEM(a.shape, a.dtype) for a in inputs] + [pltpu.SemaphoreType.DMA((9,))],
+        compiler_params=SMALL,
         name="pack_columns",
-    )(water_depth, tracers, rainfall, roughness, flow_codes, land_mask, leakance, pumping, active)
+    )(*[pltpu.with_memory_space_constraint(a, pltpu.MemorySpace.HBM) for a in inputs])
     east, west = exchange(first, last, "gx", counts)
     first, last = pl.pallas_call(
         pack_rows,
         out_shape=(shape(STRIP, LANES), shape(STRIP, LANES)),
         in_specs=whole(4),
         out_specs=tuple(whole(2)),
+        compiler_params=SMALL,
         name="pack_rows",
     )(own, east, west, coarse)
     south, north = exchange(first, last, "gy", counts)
     deep = rows + 2 * WIDE
     sums, zc, uc = pl.pallas_call(
         functools.partial(depth_kernel, counts),
-        out_shape=(shape(8, LANES), shape(crows, LANES), shape(crows, LANES)),
+        out_shape=(shape(counts[0] * counts[1], LANES), shape(crows, LANES), shape(crows, LANES)),
         in_specs=whole(6),
         out_specs=tuple(whole(3)),
         scratch_shapes=[
@@ -340,6 +350,7 @@
             pltpu.VMEM((8, deep // 8, 8, 2 * LANES), F32),
             pltpu.VMEM((3, 16, LANES), F32),
         ],
+        compiler_params=ROOMY,
         name="depth_and_moments",
     )(own, east, west, north, south, coarse)
     low = rows + 2 * SLIM
@@ -353,14 +364,16 @@
             pltpu.VMEM((8, low // 8, 8, 2 * LANES), F32),
         ],
         cost_estimate=pl.CostEstimate(flops=20_000_000, bytes_accessed=20_000_000, transcendentals=0),
+        compiler_params=ROOMY,
         name="all_channels",
     )(own, east, west, north, south)
-    sums = everywhere(sums, counts)
+    sums = lax.all_to_all(sums, AXES, 0, 0, tiled=True)
     head = pl.pallas_call(
         head_kernel,
         out_shape=shape(crows, ccols),
         in_specs=whole(3),
         out_specs=pl.BlockSpec(memory_space=pltpu.VMEM),
+        compiler_params=SMALL,
         name="combine_head",
     )(sums, zc, uc)
     return depth_out, tracers_out, head

time: 45.6 us -> 31.3 us (0.69)
  waiting for transfers between devices: 16.7 us -> 11 us
  Pallas kernels: 13.3 us -> 8.49 us
  local copies, waits for them, and re-layouts: 1.82 us -> 0 us
  other arithmetic: 1.3 us -> 0 us
  starting transfers between devices: 11.5 us -> 10.9 us
    ppermute x5 -> x0, waiting for transfers between devices: 8.47 us -> none  [everywhere(): lax.ppermute(value, AXES, [(i, i ^ bit) for i in range(size)])]
    ppermute x5 -> x0, starting transfers between devices: 3.83 us -> none  [everywhere(): lax.ppermute(value, AXES, [(i, i ^ bit) for i in range(size)])]
    all_to_all x0 -> x1, waiting for transfers between devices: none -> 3.27 us  [shards(): sums = lax.all_to_all(sums, AXES, 0, 0, tiled=True)]
    all_to_all x0 -> x1, starting transfers between devices: none -> 3.06 us  [shards(): sums = lax.all_to_all(sums, AXES, 0, 0, tiled=True)]
    unnamed x8 -> x0, local copies, waits for them, and re-layouts: 1.82 us -> none
    pallas_call x1, Pallas kernels: 1.6 us -> 0.02 us  [shards(): pl.pallas_call(pack_rows, out_shape=(shape(STRIP, LANES), shape(STRIP, LA...]
    add x5 -> x0, other arithmetic: 1.3 us -> none  [everywhere(): value + lax.ppermute(value, AXES, [(i, i ^ bit) for i in range(size)])]
    pallas_call x1, Pallas kernels: 4.89 us -> 3.88 us  [shards(): pl.pallas_call(functools.partial(state_kernel, counts), out_shape=(shape(...]
  transfers between devices with their start and end apart: 9 -> 5, of which waited for: 7 -> 4; matrix products, arithmetic and copies ran while one was open for 0% -> 0% of each run, Pallas kernels for 11% -> 13%
where the time goes in v2:
time: 31.3 us; the launch traced here: 31 us
  waiting for transfers between devices  11 us (35%)
  starting transfers between devices  10.9 us (35%)
  Pallas kernels  8.49 us (27%)
  between operations  0.67 us (2%)
    ppermute x2, starting transfers between devices, exchange(): after = lax.ppermute(first, axis, ring(-1, axis, counts))  7.73 us
    ppermute x2, waiting for transfers between devices, exchange(): before = lax.ppermute(last, axis, ring(1, axis, counts))  6.26 us
    pallas_call x1, Pallas kernels, shards(): pl.pallas_call(functools.partial(state_kernel, counts), out_shape=(shape(...  3.88 us
    all_to_all x1, waiting for transfers between devices, shards(): sums = lax.all_to_all(sums, AXES, 0, 0, tiled=True)  3.27 us
    all_to_all x1, starting transfers between devices, shards(): sums = lax.all_to_all(sums, AXES, 0, 0, tiled=True)  3.06 us
    pallas_call x1, Pallas kernels, shards(): pl.pallas_call(functools.partial(depth_kernel, counts), out_shape=(shape(...  2.86 us
    ppermute x2, waiting for transfers between devices, exchange(): after = lax.ppermute(first, axis, ring(-1, axis, counts))  1.48 us
    pallas_call x1, Pallas kernels, shards(): pl.pallas_call(pack_columns, out_shape=(shape(7, rows, cols), shape(rows...  1.03 us
  transfers between devices with their start and end apart: 5, of which 4 were waited for; matrix products, arithmetic and copies ran while one was open for 0% of the time, Pallas kernels for 13%

profile of v2, /device:TPU:0, one launch (start us, length us, event | category | flops | bytes accessed | tf_op | source)
XLA Modules:
  0.0 31.0 jit_solution(16973841430168139805)
XLA Ops:
  0.6 1.0 %pack_columns.1 = (f32[7,32,128]{2,1,0:T(8,128)S(1)}, f32[40,128]{1,0:T(8,128)S(1)}, f32[40,128]{1,0:T(8,128)S(1)}, f32[8,128]{1,0:T(8,128)S(1)}) custom-call(f32[32,128]{1,0:T(8,128)} %refs_0_.1, f32[3,32,128]{2,1,0:T(8,128)} %refs_1_.1, f32[32,128]{1,0:T(8,128)} %refs_2_.1, f32[32,128]{1,0:T(8,128)} %refs_3_.1, s32[32,128]{1,0:T(8,128)} %refs_4_.1, ...), custom_call_target="tpu_custom_call" | custom-call | tf_op jit(solution)/shard_map/pack_columns/pallas_call | solution.py:323
  1.7 5.1 %collective-permute-start = (f32[40,128]{1,0:T(8,128)S(1)}, f32[40,128]{1,0:T(8,128)S(1)}, u32[]{:S(2)}, u32[]{:S(2)}) collective-permute-start(f32[40,128]{1,0:T(8,128)S(1)} %get-tuple-element.15), channel_id=1, source_target_pairs={{0,24},{8,0},{16,8},{24,16},{1,25},{9,1},{17,9},{25,17},{2,26},{10... | collective-permute-start | bytes 61448 | tf_op jit(solution)/shard_map/ppermute | solution.py:314
  6.8 0.0 collective-permute-start.1
  6.8 1.5 %collective-permute-done.east = f32[40,128]{1,0:T(8,128)S(1)} collective-permute-done((f32[40,128]{1,0:T(8,128)S(1)}, f32[40,128]{1,0:T(8,128)S(1)}, u32[]{:S(2)}, u32[]{:S(2)}) %collective-permute-start) | collective-permute-done | bytes 20512 | tf_op jit(solution)/shard_map/ppermute | solution.py:314
  8.3 4.1 %collective-permute-done.1.west = f32[40,128]{1,0:T(8,128)S(1)} collective-permute-done((f32[40,128]{1,0:T(8,128)S(1)}, f32[40,128]{1,0:T(8,128)S(1)}, u32[]{:S(2)}, u32[]{:S(2)}) %collective-permute-start.1) | collective-permute-done | bytes 20512 | tf_op jit(solution)/shard_map/ppermute | solution.py:315
  12.4 0.1 collective-permute-start.2
  12.4 2.6 %collective-permute-start.3 = (f32[168,128]{1,0:T(8,128)S(1)}, f32[168,128]{1,0:T(8,128)S(1)}, u32[]{:S(2)}, u32[]{:S(2)}) collective-permute-start(f32[168,128]{1,0:T(8,128)S(1)} %get-tuple-element.19), channel_id=1, source_target_pairs={{0,7},{1,0},{2,1},{3,2},{4,3},{5,4},{6,5},{7,6},{8,15},{9,8},{10,9... | collective-permute-start | bytes 258056 | tf_op jit(solution)/shard_map/ppermute | solution.py:314
  15.1 2.2 %collective-permute-done.2.north = f32[168,128]{1,0:T(8,128)S(1)} collective-permute-done((f32[168,128]{1,0:T(8,128)S(1)}, f32[168,128]{1,0:T(8,128)S(1)}, u32[]{:S(2)}, u32[]{:S(2)}) %collective-permute-start.2) | collective-permute-done | bytes 86048 | tf_op jit(solution)/shard_map/ppermute | solution.py:315
  17.2 0.0 collective-permute-done.3.south
  17.2 2.9 %depth_and_moments.1 = (f32[32,128]{1,0:T(8,128)}, f32[8,128]{1,0:T(8,128)S(1)}, f32[8,128]{1,0:T(8,128)S(1)}) custom-call(f32[7,32,128]{2,1,0:T(8,128)S(1)} %get-tuple-element.14.own, f32[40,128]{1,0:T(8,128)S(1)} %collective-permute-done.east, f32[40,128]{1,0:T(8,128)S(1)} %collective-permute-done.1.west, f32[168,128]{1,0:T(8,128)S(1)} %collective-permute-done.2.north, ...), custom_call_target="tpu_custom_call" | custom-call | tf_op jit(solution)/shard_map/depth_and_moments/pallas_call | solution.py:343
  20.1 3.1 %all-to-all-start = ((f32[32,1,128]{2,1,0:T(1,128)}), f32[32,1,128]{2,1,0:T(1,128)S(1)}, u32[]{:S(2)}, u32[]{:S(2)}) async-start(f32[32,1,128]{2,1,0:T(1,128)} %bitcast.1), calls=%async_computation | async-start | bytes 32768 | tf_op jit(solution)/shard_map/all_to_all | solution.py:370
  23.2 3.9 %all_channels.1 = (f32[32,128]{1,0:T(8,128)}, f32[3,32,128]{2,1,0:T(8,128)}) custom-call(f32[7,32,128]{2,1,0:T(8,128)S(1)} %get-tuple-element.14.own, f32[40,128]{1,0:T(8,128)S(1)} %collective-permute-done.east, f32[40,128]{1,0:T(8,128)S(1)} %collective-permute-done.1.west, f32[168,128]{1,0:T(8,128)S(1)} %collective-permute-done.2.north, ...), custom_call_target="tpu_custom_call" | custom-call | flops 20000000 | bytes 20000000 | tf_op jit(solution)/shard_map/all_channels/pallas_call | solution.py:357
  27.0 3.3 %all-to-all-done = f32[32,1,128]{2,1,0:T(1,128)S(1)} async-done(((f32[32,1,128]{2,1,0:T(1,128)}), f32[32,1,128]{2,1,0:T(1,128)S(1)}, u32[]{:S(2)}, u32[]{:S(2)}) %all-to-all-start) | async-done | bytes 16416 | tf_op jit(solution)/shard_map/all_to_all | solution.py:370
  30.3 0.7 %combine_head.1 = f32[8,32]{1,0:T(8,128)} custom-call(f32[32,128]{1,0:T(8,128)S(1)} %bitcast.4, f32[8,128]{1,0:T(8,128)S(1)} %get-tuple-element.23.zc, f32[8,128]{1,0:T(8,128)S(1)} %get-tuple-element.24.uc), custom_call_target="tpu_custom_call" | custom-call | tf_op jit(solution)/shard_map/combine_head/pallas_call | solution.py:371
  (1 shorter events, 0.0 us)
Async XLA Ops:
  1.7 6.6 %collective-permute-start = (f32[40,128]{1,0:T(8,128)S(1)}, f32[40,128]{1,0:T(8,128)S(1)}, u32[]{:S(2)}, u32[]{:S(2)}) collective-permute-start(f32[40,128]{1,0:T(8,128)S(1)} %get-tuple-element.15), channel_id=1, source_target_pairs={{0,24},{8,0},{16,8},{24,16},{1,25},{9,1},{17,9},{25,17},{2,26},{10... | collective-permute-start | bytes 61448 | tf_op jit(solution)/shard_map/ppermute | solution.py:314
  6.8 5.6 %collective-permute-start.1 = (f32[40,128]{1,0:T(8,128)S(1)}, f32[40,128]{1,0:T(8,128)S(1)}, u32[]{:S(2)}, u32[]{:S(2)}) collective-permute-start(f32[40,128]{1,0:T(8,128)S(1)} %get-tuple-element.16), channel_id=1, source_target_pairs={{0,8},{8,16},{16,24},{24,0},{1,9},{9,17},{17,25},{25,1},{2,10},{10... | collective-permute-start | bytes 61448 | tf_op jit(solution)/shard_map/ppermute | solution.py:315
  12.4 4.9 %collective-permute-start.2 = (f32[168,128]{1,0:T(8,128)S(1)}, f32[168,128]{1,0:T(8,128)S(1)}, u32[]{:S(2)}, u32[]{:S(2)}) collective-permute-start(f32[168,128]{1,0:T(8,128)S(1)} %get-tuple-element.18), channel_id=1, source_target_pairs={{0,1},{1,2},{2,3},{3,4},{4,5},{5,6},{6,7},{7,0},{8,9},{9,10},{10,1... | collective-permute-start | bytes 258056 | tf_op jit(solution)/shard_map/ppermute | solution.py:315
  12.4 4.8 %collective-permute-start.3 = (f32[168,128]{1,0:T(8,128)S(1)}, f32[168,128]{1,0:T(8,128)S(1)}, u32[]{:S(2)}, u32[]{:S(2)}) collective-permute-start(f32[168,128]{1,0:T(8,128)S(1)} %get-tuple-element.19), channel_id=1, source_target_pairs={{0,7},{1,0},{2,1},{3,2},{4,3},{5,4},{6,5},{7,6},{8,15},{9,8},{10,9... | collective-permute-start | bytes 258056 | tf_op jit(solution)/shard_map/ppermute | solution.py:314
  20.1 10.2 %all-to-all-start = ((f32[32,1,128]{2,1,0:T(1,128)}), f32[32,1,128]{2,1,0:T(1,128)S(1)}, u32[]{:S(2)}, u32[]{:S(2)}) async-start(f32[32,1,128]{2,1,0:T(1,128)} %bitcast.1), calls=%async_computation | async-start | bytes 32768 | tf_op jit(solution)/shard_map/all_to_all | solution.py:370

commit v3 on v2

--- a/solution.py
+++ b/solution.py
@@ -37,7 +37,7 @@
 
 
 def pack_columns(*refs):
-    sources, (own, first, last, coarse), buffers, done = refs[:9], refs[9:13], refs[13:22], refs[22]
+    sources, (own, near, far, coarse), buffers, done = refs[:9], refs[9:13], refs[13:22], refs[22]
     copies = [pltpu.make_async_copy(a, b, done.at[k]) for k, (a, b) in enumerate(zip(sources, buffers))]
     for copy in copies:
         copy.start()
@@ -68,26 +68,34 @@
     weight = act / (act * (4.0 + leak[...]) + (1.0 - act))
     both = jnp.concatenate([weight, pump[...], jnp.zeros((act.shape[0], LANES - 2 * act.shape[1]), F32)], axis=1)
     coarse[...] = both
-    first[0:rows] = head
-    last[0:rows] = tail
-    first[rows : rows + act.shape[0]] = both
-    last[rows : rows + act.shape[0]] = both
-
-
-def pack_rows(own, east, west, coarse, first, last):
+    odd = lax.axis_index("gx") % 2 == 1
+    near[0:rows] = jnp.where(odd, head, tail)
+    far[0:rows] = jnp.where(odd, tail, head)
+    near[rows : rows + act.shape[0]] = both
+    far[rows : rows + act.shape[0]] = both
+
+
+def pack_rows(own, side_near, side_far, coarse, near, far, east, west):
+    flip = lax.axis_index("gx") % 2 == 1
+    east[...] = jnp.where(flip, side_far[...], side_near[...])
+    west[...] = jnp.where(flip, side_near[...], side_far[...])
     rows = own.shape[1]
     crows = coarse.shape[0]
+    odd = lax.axis_index("gy") % 2 == 1
+
+    def put(at, top, bottom):
+        near[at : at + top.shape[0]] = jnp.where(odd, top, bottom)
+        far[at : at + top.shape[0]] = jnp.where(odd, bottom, top)
+
     for k, (at, width) in enumerate(SLOTS):
-        first[at : at + width] = own[k, 0:width]
-        last[at : at + width] = own[k, rows - width : rows]
+        put(at, own[k, 0:width], own[k, rows - width : rows])
     for at, side in ((EAST_AT, east), (WEST_AT, west)):
-        first[at : at + WIDE] = side[0:WIDE]
-        last[at : at + WIDE] = side[rows - WIDE : rows]
+        put(at, side[0:WIDE], side[rows - WIDE : rows])
     for at, part in ((COARSE_AT, coarse), (COARSE_AT + 2, east.at[rows : rows + crows]), (COARSE_AT + 4, west.at[rows : rows + crows])):
-        first[at : at + 2] = part[0:2]
-        last[at : at + 2] = part[crows - 2 : crows]
-    first[COARSE_AT + 6 : STRIP] = jnp.zeros((STRIP - COARSE_AT - 6, LANES), F32)
-    last[COARSE_AT + 6 : STRIP] = jnp.zeros((STRIP - COARSE_AT - 6, LANES), F32)
+        put(at, part[0:2], part[crows - 2 : crows])
+    rest = jnp.zeros((STRIP - COARSE_AT - 6, LANES), F32)
+    near[COARSE_AT + 6 : STRIP] = rest
+    far[COARSE_AT + 6 : STRIP] = rest
 
 
 def inside(counts):
@@ -96,16 +104,22 @@
     return row > 0, row < counts[1] - 1, col < counts[0] - 1, col > 0
 
 
-def gather_fields(kinds, halo, own, east, west, north, south, flags, stage):
+def rows_from(near, far, start, count, use_near, present):
+    got = jnp.where(use_near, near[start : start + count], far[start : start + count])
+    return jnp.where(present, got, 0.0)
+
+
+def gather_fields(kinds, halo, own, east, west, near, far, flags, stage):
     has_north, has_south, has_east, has_west = flags
     rows = own.shape[1]
     total = rows + 2 * halo
     chunk = total // 8
+    odd = lax.axis_index("gy") % 2 == 1
 
     def lay(slot, at, width, middle):
-        stage[slot, 0:halo] = jnp.where(has_north, north[at + width - halo : at + width], 0.0)
+        stage[slot, 0:halo] = rows_from(near, far, at + width - halo, halo, odd, has_north)
         stage[slot, halo : halo + rows] = middle
-        stage[slot, halo + rows : total] = jnp.where(has_south, south[at : at + halo], 0.0)
+        stage[slot, halo + rows : total] = rows_from(near, far, at, halo, ~odd, has_south)
 
     def read(slot):
         return [stage[slot, pl.ds(i, 8, stride=chunk)] for i in range(chunk)]
@@ -181,9 +195,9 @@
 KEEP = 1.0 - TIME_STEP * INFILTRATION
 
 
-def depth_kernel(counts, own, east, west, north, south, coarse, sums, zc, uc, stage, masks, cst):
+def depth_kernel(counts, own, east, west, near, far, coarse, sums, zc, uc, stage, masks, cst):
     flags = inside(counts)
-    depth, rain, coef, codes = gather_fields((0, 1, 2, 3), WIDE, own, east, west, north, south, flags, stage)
+    depth, rain, coef, codes = gather_fields((0, 1, 2, 3), WIDE, own, east, west, near, far, flags, stage)
     move_masks(codes, coef, masks)
 
     def step(_, carry):
@@ -206,9 +220,7 @@
     fine = lax.broadcasted_iota(jnp.int32, (2 * LANES, LANES), 0)
     cell = lax.broadcasted_iota(jnp.int32, (2 * LANES, LANES), 1)
     place = lax.shift_right_logical(fine, 2)
-    near = fine < LANES + 8
-    far = fine >= 2 * LANES - 8
-    hit = (near & (place == cell)) | (far & (place - (2 * LANES // 4 - 2) == cell - (LANES - 2)))
+    hit = ((fine < LANES + 8) & (place == cell)) | ((fine >= 2 * LANES - 8) & (place - (2 * LANES // 4 - 2) == cell - (LANES - 2)))
     rc = jnp.dot(
         pooled,
         jnp.where(hit, 1.0, 0.0),
@@ -218,12 +230,13 @@
 
     has_north, has_south, has_east, has_west = flags
     rows = own.shape[1]
+    odd = lax.axis_index("gy") % 2 == 1
     for k, middle in enumerate((coarse[...], east[rows : rows + crows], west[rows : rows + crows])):
         at = COARSE_AT + 2 * k
         cst[k] = jnp.zeros((16, LANES), F32)
-        cst[k, 1:3] = jnp.where(has_north, north[at : at + 2], 0.0)
+        cst[k, 1:3] = rows_from(near, far, at, 2, odd, has_north)
         cst[k, 3 : 3 + crows] = middle
-        cst[k, 3 + crows : 5 + crows] = jnp.where(has_south, south[at : at + 2], 0.0)
+        cst[k, 3 + crows : 5 + crows] = rows_from(near, far, at, 2, ~odd, has_south)
     ids = lane_ids(16)
     e_here = (ids >= ccols) & (ids < jnp.where(has_east, ccols + 2, ccols))
     w_here = ids >= jnp.where(has_west, LANES - 2, LANES)
@@ -258,10 +271,10 @@
     uc[...] = u
 
 
-def state_kernel(counts, own, east, west, north, south, depth_out, tracers_out, stage, masks):
+def state_kernel(counts, own, east, west, near, far, depth_out, tracers_out, stage, masks):
     flags = inside(counts)
     depth, rain, coef, codes, *species = gather_fields(
-        (0, 1, 2, 3, 4, 5, 6), SLIM, own, east, west, north, south, flags, stage
+        (0, 1, 2, 3, 4, 5, 6), SLIM, own, east, west, near, far, flags, stage
     )
     move_masks(codes, coef, masks)
 
@@ -305,22 +318,32 @@
     head[...] = ((a0 - a1 * slope) * zc[...] + a1 * uc[...])[:, :wide]
 
 
-def ring(shift, axis, counts):
-    size = counts[AXES.index(axis)]
-    return [(i, (i + shift) % size) for i in range(size)]
-
-
-def exchange(first, last, axis, counts):
-    after = lax.ppermute(first, axis, ring(-1, axis, counts))
-    before = lax.ppermute(last, axis, ring(1, axis, counts))
-    return after, before
+def swaps(axis, offset, counts):
+    pairs = []
+    for col in range(counts[0]):
+        for row in range(counts[1]):
+            spot = [col, row]
+            k = AXES.index(axis)
+            other = ((spot[k] + offset) ^ 1) - offset
+            if 0 <= other < counts[k]:
+                spot[k] = other
+            else:
+                spot[1 - k] ^= 1
+            pairs.append((col * counts[1] + row, spot[0] * counts[1] + spot[1]))
+    return pairs
+
+
+def exchange(near, far, axis, counts):
+    near = lax.ppermute(near, AXES, swaps(axis, 0, counts))
+    far = lax.ppermute(far, AXES, swaps(axis, 1, counts))
+    return near, far
 
 
 def shards(counts, *inputs):
     rows, cols = inputs[0].shape
     crows, ccols = inputs[6].shape
     shape = lambda *dims: jax.ShapeDtypeStruct(dims, F32)
-    own, first, last, coarse = pl.pallas_call(
+    own, near, far, coarse = pl.pallas_call(
         pack_columns,
         out_shape=(shape(7, rows, cols), shape(rows + crows, LANES), shape(rows + crows, LANES), shape(crows, LANES)),
         in_specs=[pl.BlockSpec(memory_space=pltpu.MemorySpace.HBM)] * 9,
@@ -329,16 +352,16 @@
         compiler_params=SMALL,
         name="pack_columns",
     )(*[pltpu.with_memory_space_constraint(a, pltpu.MemorySpace.HBM) for a in inputs])
-    east, west = exchange(first, last, "gx", counts)
-    first, last = pl.pallas_call(
+    near, far = exchange(near, far, "gx", counts)
+    near, far, east, west = pl.pallas_call(
         pack_rows,
-        out_shape=(shape(STRIP, LANES), shape(STRIP, LANES)),
+        out_shape=(shape(STRIP, LANES), shape(STRIP, LANES), shape(rows + crows, LANES), shape(rows + crows, LANES)),
         in_specs=whole(4),
-        out_specs=tuple(whole(2)),
+        out_specs=tuple(whole(4)),
         compiler_params=SMALL,
         name="pack_rows",
-    )(own, east, west, coarse)
-    south, north = exchange(first, last, "gy", counts)
+    )(own, near, far, coarse)
+    near, far = exchange(near, far, "gy", counts)
     deep = rows + 2 * WIDE
     sums, zc, uc = pl.pallas_call(
         functools.partial(depth_kernel, counts),
@@ -352,7 +375,7 @@
         ],
         compiler_params=ROOMY,
         name="depth_and_moments",
-    )(own, east, west, north, south, coarse)
+    )(own, east, west, near, far, coarse)
     low = rows + 2 * SLIM
     depth_out, tracers_out = pl.pallas_call(
         functools.partial(state_kernel, counts),
@@ -366,7 +389,7 @@
         cost_estimate=pl.CostEstimate(flops=20_000_000, bytes_accessed=20_000_000, transcendentals=0),
         compiler_params=ROOMY,
         name="all_channels",
-    )(own, east, west, north, south)
+    )(own, east, west, near, far)
     sums = lax.all_to_all(sums, AXES, 0, 0, tiled=True)
     head = pl.pallas_call(
         head_kernel,

time: 31.3 us -> 29 us (0.927)
  waiting for transfers between devices: 11 us -> 7.48 us
  starting transfers between devices: 10.9 us -> 12.1 us
    ppermute x4, waiting for transfers between devices: 7.74 us -> 4.23 us  [the longest x2 2.46 us: exchange(): far = lax.ppermute(far, AXES, swaps(axis, 1, counts))]
    all_to_all x1, starting transfers between devices: 3.06 us -> 5.7 us  [shards(): sums = lax.all_to_all(sums, AXES, 0, 0, tiled=True)]
    ppermute x4, starting transfers between devices: 7.79 us -> 6.37 us  [the longest x2 3.21 us: exchange(): far = lax.ppermute(far, AXES, swaps(axis, 1, counts))]
  transfers between devices with their start and end apart: 5 -> 5, of which waited for: 4 -> 3; matrix products, arithmetic and copies ran while one was open for 0% -> 0% of each run, Pallas kernels for 13% -> 14%
where the time goes in v3:
time: 29 us; the launch traced here: 28.7 us
  starting transfers between devices  12.1 us (42%)
  Pallas kernels  8.52 us (29%)
  waiting for transfers between devices  7.48 us (26%)
  between operations  0.67 us (2%)
    all_to_all x1, starting transfers between devices, shards(): sums = lax.all_to_all(sums, AXES, 0, 0, tiled=True)  5.7 us
    pallas_call x1, Pallas kernels, shards(): pl.pallas_call(functools.partial(state_kernel, counts), out_shape=(shape(...  3.89 us
    all_to_all x1, waiting for transfers between devices, shards(): sums = lax.all_to_all(sums, AXES, 0, 0, tiled=True)  3.26 us
    ppermute x2, starting transfers between devices, exchange(): far = lax.ppermute(far, AXES, swaps(axis, 1, counts))  3.21 us
    ppermute x2, starting transfers between devices, exchange(): near = lax.ppermute(near, AXES, swaps(axis, 0, counts))  3.16 us
    pallas_call x1, Pallas kernels, shards(): pl.pallas_call(functools.partial(depth_kernel, counts), out_shape=(shape(...  2.86 us
    ppermute x2, waiting for transfers between devices, exchange(): far = lax.ppermute(far, AXES, swaps(axis, 1, counts))  2.46 us
    ppermute x2, waiting for transfers between devices, exchange(): near = lax.ppermute(near, AXES, swaps(axis, 0, counts))  1.76 us
  transfers between devices with their start and end apart: 5, of which 3 were waited for; matrix products, arithmetic and copies ran while one was open for 0% of the time, Pallas kernels for 14%

profile of v3, /device:TPU:0, one launch (start us, length us, event | category | flops | bytes accessed | tf_op | source)
XLA Modules:
  0.0 28.7 jit_solution(11754995564565618149)
XLA Ops:
  0.6 1.0 %pack_columns.1 = (f32[7,32,128]{2,1,0:T(8,128)S(1)}, f32[40,128]{1,0:T(8,128)S(1)}, f32[40,128]{1,0:T(8,128)S(1)}, f32[8,128]{1,0:T(8,128)S(1)}) custom-call(f32[32,128]{1,0:T(8,128)} %refs_0_.1, f32[3,32,128]{2,1,0:T(8,128)} %refs_1_.1, f32[32,128]{1,0:T(8,128)} %refs_2_.1, f32[32,128]{1,0:T(8,128)} %refs_3_.1, s32[32,128]{1,0:T(8,128)} %refs_4_.1, ...), custom_call_target="tpu_custom_call" | custom-call | tf_op jit(solution)/shard_map/pack_columns/pallas_call | solution.py:346
  1.7 3.1 %collective-permute-start = (f32[40,128]{1,0:T(8,128)S(1)}, f32[40,128]{1,0:T(8,128)S(1)}, u32[]{:S(2)}, u32[]{:S(2)}) collective-permute-start(f32[40,128]{1,0:T(8,128)S(1)} %get-tuple-element.17), channel_id=1, source_target_pairs={{0,8},{1,9},{2,10},{3,11},{4,12},{5,13},{6,14},{7,15},{8,0},{9,1},... | collective-permute-start | bytes 61448 | tf_op jit(solution)/shard_map/ppermute | solution.py:337
  4.8 0.0 collective-permute-start.1
  4.8 1.8 %collective-permute-done.side_near = f32[40,128]{1,0:T(8,128)S(1)} collective-permute-done((f32[40,128]{1,0:T(8,128)S(1)}, f32[40,128]{1,0:T(8,128)S(1)}, u32[]{:S(2)}, u32[]{:S(2)}) %collective-permute-start) | collective-permute-done | bytes 20512 | tf_op jit(solution)/shard_map/ppermute | solution.py:337
  6.5 0.0 collective-permute-done.1.side_far
  6.6 0.1 collective-permute-start.2
  6.7 3.2 %collective-permute-start.3 = (f32[168,128]{1,0:T(8,128)S(1)}, f32[168,128]{1,0:T(8,128)S(1)}, u32[]{:S(2)}, u32[]{:S(2)}) collective-permute-start(f32[168,128]{1,0:T(8,128)S(1)} %get-tuple-element.23), channel_id=1, source_target_pairs={{0,8},{1,2},{2,1},{3,4},{4,3},{5,6},{6,5},{7,15},{8,0},{9,10},{10,... | collective-permute-start | bytes 258056 | tf_op jit(solution)/shard_map/ppermute | solution.py:338
  9.9 0.0 collective-permute-done.2.near
  9.9 2.5 %collective-permute-done.3.far = f32[168,128]{1,0:T(8,128)S(1)} collective-permute-done((f32[168,128]{1,0:T(8,128)S(1)}, f32[168,128]{1,0:T(8,128)S(1)}, u32[]{:S(2)}, u32[]{:S(2)}) %collective-permute-start.3) | collective-permute-done | bytes 86048 | tf_op jit(solution)/shard_map/ppermute | solution.py:338
  12.3 2.9 %depth_and_moments.1 = (f32[32,128]{1,0:T(8,128)}, f32[8,128]{1,0:T(8,128)S(1)}, f32[8,128]{1,0:T(8,128)S(1)}) custom-call(f32[7,32,128]{2,1,0:T(8,128)S(1)} %get-tuple-element.16.own, f32[40,128]{1,0:T(8,128)S(1)} %get-tuple-element.20.east, f32[40,128]{1,0:T(8,128)S(1)} %get-tuple-element.21.west, f32[168,128]{1,0:T(8,128)S(1)} %collective-permute-done.2.near, ...), custom_call_target="tpu_custom_call" | custom-call | tf_op jit(solution)/shard_map/depth_and_moments/pallas_call | solution.py:366
  15.2 5.7 %all-to-all-start = ((f32[32,1,128]{2,1,0:T(1,128)}), f32[32,1,128]{2,1,0:T(1,128)S(1)}, u32[]{:S(2)}, u32[]{:S(2)}) async-start(f32[32,1,128]{2,1,0:T(1,128)} %bitcast.1), calls=%async_computation | async-start | bytes 32768 | tf_op jit(solution)/shard_map/all_to_all | solution.py:393
  20.9 3.9 %all_channels.1 = (f32[32,128]{1,0:T(8,128)}, f32[3,32,128]{2,1,0:T(8,128)}) custom-call(f32[7,32,128]{2,1,0:T(8,128)S(1)} %get-tuple-element.16.own, f32[40,128]{1,0:T(8,128)S(1)} %get-tuple-element.20.east, f32[40,128]{1,0:T(8,128)S(1)} %get-tuple-element.21.west, f32[168,128]{1,0:T(8,128)S(1)} %collective-permute-done.2.near, ...), custom_call_target="tpu_custom_call" | custom-call | flops 20000000 | bytes 20000000 | tf_op jit(solution)/shard_map/all_channels/pallas_call | solution.py:380
  24.8 3.3 %all-to-all-done = f32[32,1,128]{2,1,0:T(1,128)S(1)} async-done(((f32[32,1,128]{2,1,0:T(1,128)}), f32[32,1,128]{2,1,0:T(1,128)S(1)}, u32[]{:S(2)}, u32[]{:S(2)}) %all-to-all-start) | async-done | bytes 16416 | tf_op jit(solution)/shard_map/all_to_all | solution.py:393
  28.0 0.7 %combine_head.1 = f32[8,32]{1,0:T(8,128)} custom-call(f32[32,128]{1,0:T(8,128)S(1)} %bitcast.4, f32[8,128]{1,0:T(8,128)S(1)} %get-tuple-element.27.zc, f32[8,128]{1,0:T(8,128)S(1)} %get-tuple-element.28.uc), custom_call_target="tpu_custom_call" | custom-call | tf_op jit(solution)/shard_map/combine_head/pallas_call | solution.py:394
  (1 shorter events, 0.0 us)
Async XLA Ops:
  1.7 4.9 %collective-permute-start = (f32[40,128]{1,0:T(8,128)S(1)}, f32[40,128]{1,0:T(8,128)S(1)}, u32[]{:S(2)}, u32[]{:S(2)}) collective-permute-start(f32[40,128]{1,0:T(8,128)S(1)} %get-tuple-element.17), channel_id=1, source_target_pairs={{0,8},{1,9},{2,10},{3,11},{4,12},{5,13},{6,14},{7,15},{8,0},{9,1},... | collective-permute-start | bytes 61448 | tf_op jit(solution)/shard_map/ppermute | solution.py:337
  4.8 1.8 %collective-permute-start.1 = (f32[40,128]{1,0:T(8,128)S(1)}, f32[40,128]{1,0:T(8,128)S(1)}, u32[]{:S(2)}, u32[]{:S(2)}) collective-permute-start(f32[40,128]{1,0:T(8,128)S(1)} %get-tuple-element.18), channel_id=1, source_target_pairs={{0,1},{1,0},{2,3},{3,2},{4,5},{5,4},{6,7},{7,6},{8,16},{9,17},{10,... | collective-permute-start | bytes 61448 | tf_op jit(solution)/shard_map/ppermute | solution.py:338
  6.6 3.3 %collective-permute-start.2 = (f32[168,128]{1,0:T(8,128)S(1)}, f32[168,128]{1,0:T(8,128)S(1)}, u32[]{:S(2)}, u32[]{:S(2)}) collective-permute-start(f32[168,128]{1,0:T(8,128)S(1)} %get-tuple-element.22), channel_id=1, source_target_pairs={{0,1},{1,0},{2,3},{3,2},{4,5},{5,4},{6,7},{7,6},{8,9},{9,8},{10,11... | collective-permute-start | bytes 258056 | tf_op jit(solution)/shard_map/ppermute | solution.py:337
  6.7 5.7 %collective-permute-start.3 = (f32[168,128]{1,0:T(8,128)S(1)}, f32[168,128]{1,0:T(8,128)S(1)}, u32[]{:S(2)}, u32[]{:S(2)}) collective-permute-start(f32[168,128]{1,0:T(8,128)S(1)} %get-tuple-element.23), channel_id=1, source_target_pairs={{0,8},{1,2},{2,1},{3,4},{4,3},{5,6},{6,5},{7,15},{8,0},{9,10},{10,... | collective-permute-start | bytes 258056 | tf_op jit(solution)/shard_map/ppermute | solution.py:338
  15.2 12.9 %all-to-all-start = ((f32[32,1,128]{2,1,0:T(1,128)}), f32[32,1,128]{2,1,0:T(1,128)S(1)}, u32[]{:S(2)}, u32[]{:S(2)}) async-start(f32[32,1,128]{2,1,0:T(1,128)} %bitcast.1), calls=%async_computation | async-start | bytes 32768 | tf_op jit(solution)/shard_map/all_to_all | solution.py:393

commit v4 on v3

--- a/solution.py
+++ b/solution.py
@@ -75,7 +75,7 @@
     far[rows : rows + act.shape[0]] = both
 
 
-def pack_rows(own, side_near, side_far, coarse, near, far, east, west):
+def pack_rows(own, side_far, side_near, coarse, near, far, east, west):
     flip = lax.axis_index("gx") % 2 == 1
     east[...] = jnp.where(flip, side_far[...], side_near[...])
     west[...] = jnp.where(flip, side_near[...], side_far[...])
@@ -195,39 +195,17 @@
 KEEP = 1.0 - TIME_STEP * INFILTRATION
 
 
-def depth_kernel(counts, own, east, west, near, far, coarse, sums, zc, uc, stage, masks, cst):
+def depth_kernel(counts, own, east, west, far, near, coarse, sums, zc, uc, stage, masks, cst):
     flags = inside(counts)
     depth, rain, coef, codes = gather_fields((0, 1, 2, 3), WIDE, own, east, west, near, far, flags, stage)
     move_masks(codes, coef, masks)
 
-    def step(_, carry):
-        now, total = carry
-        flux = speed(now, coef) * now
-        return now * KEEP - flux + rain + inflow(flux, masks), total + now
-
-    now, total = lax.fori_loop(0, SUBSTEPS - 1, step, (depth, jnp.zeros_like(depth)))
-    total = total + now
-    chunk = total.shape[0]
-    for i in range(chunk):
-        stage[0, pl.ds(i, 8, stride=chunk)] = total[i, :, :LANES]
-        stage[1, pl.ds(i, 8, stride=chunk)] = total[i, :, LANES:]
-    blocks = []
-    for b in range(2):
-        quads = [stage[b, pl.ds(8 + j, 16, stride=4)] for j in range(4)]
-        blocks.append((quads[0] + quads[1]) + (quads[2] + quads[3]))
-    pooled = jnp.concatenate(blocks, axis=1)
     crows, ccols = zc.shape[0], LANES // 4
     fine = lax.broadcasted_iota(jnp.int32, (2 * LANES, LANES), 0)
     cell = lax.broadcasted_iota(jnp.int32, (2 * LANES, LANES), 1)
     place = lax.shift_right_logical(fine, 2)
     hit = ((fine < LANES + 8) & (place == cell)) | ((fine >= 2 * LANES - 8) & (place - (2 * LANES // 4 - 2) == cell - (LANES - 2)))
-    rc = jnp.dot(
-        pooled,
-        jnp.where(hit, 1.0, 0.0),
-        precision=lax.Precision.HIGHEST,
-        preferred_element_type=F32,
-    ) * (INFILTRATION * TIME_STEP)
-
+    pick = jnp.where(hit, 1.0, 0.0)
     has_north, has_south, has_east, has_west = flags
     rows = own.shape[1]
     odd = lax.axis_index("gy") % 2 == 1
@@ -248,6 +226,30 @@
         pair.append(jnp.where(ids < ccols, main, jnp.where(e_here, e, jnp.where(w_here, w, 0.0))))
     weight, pump = pair
 
+
+    def step(_, carry):
+        now, total = carry
+        flux = speed(now, coef) * now
+        return now * KEEP - flux + rain + inflow(flux, masks), total + now
+
+    now, total = lax.fori_loop(0, SUBSTEPS - 1, step, (depth, jnp.zeros_like(depth)), unroll=True)
+    total = total + now
+    chunk = total.shape[0]
+    for i in range(chunk):
+        stage[0, pl.ds(i, 8, stride=chunk)] = total[i, :, :LANES]
+        stage[1, pl.ds(i, 8, stride=chunk)] = total[i, :, LANES:]
+    blocks = []
+    for b in range(2):
+        quads = [stage[b, pl.ds(8 + j, 16, stride=4)] for j in range(4)]
+        blocks.append((quads[0] + quads[1]) + (quads[2] + quads[3]))
+    pooled = jnp.concatenate(blocks, axis=1)
+    rc = jnp.dot(
+        pooled,
+        pick,
+        precision=lax.Precision.HIGHEST,
+        preferred_element_type=F32,
+    ) * (INFILTRATION * TIME_STEP)
+
     def beside(v):
         return (pltpu.roll(v, 1, 1) + pltpu.roll(v, LANES - 1, 1)) + (pltpu.roll(v, 1, 0) + pltpu.roll(v, 15, 0))
 
@@ -271,7 +273,7 @@
     uc[...] = u
 
 
-def state_kernel(counts, own, east, west, near, far, depth_out, tracers_out, stage, masks):
+def state_kernel(counts, own, east, west, far, near, depth_out, tracers_out, stage, masks):
     flags = inside(counts)
     depth, rain, coef, codes, *species = gather_fields(
         (0, 1, 2, 3, 4, 5, 6), SLIM, own, east, west, near, far, flags, stage
@@ -288,7 +290,7 @@
             new.append(held * KEEP - flux + inflow(flux, masks))
         return tuple(new)
 
-    final = lax.fori_loop(0, SUBSTEPS, step, (depth, *species))
+    final = lax.fori_loop(0, SUBSTEPS, step, (depth, *species), unroll=4)
     chunk = depth.shape[0]
     rows = own.shape[1]
     for k, field in enumerate(final):
@@ -360,7 +362,7 @@
         out_specs=tuple(whole(4)),
         compiler_params=SMALL,
         name="pack_rows",
-    )(own, near, far, coarse)
+    )(own, far, near, coarse)
     near, far = exchange(near, far, "gy", counts)
     deep = rows + 2 * WIDE
     sums, zc, uc = pl.pallas_call(
@@ -375,7 +377,7 @@
         ],
         compiler_params=ROOMY,
         name="depth_and_moments",
-    )(own, east, west, near, far, coarse)
+    )(own, east, west, far, near, coarse)
     low = rows + 2 * SLIM
     depth_out, tracers_out = pl.pallas_call(
         functools.partial(state_kernel, counts),
@@ -389,7 +391,7 @@
         cost_estimate=pl.CostEstimate(flops=20_000_000, bytes_accessed=20_000_000, transcendentals=0),
         compiler_params=ROOMY,
         name="all_channels",
-    )(own, east, west, near, far)
+    )(own, east, west, far, near)
     sums = lax.all_to_all(sums, AXES, 0, 0, tiled=True)
     head = pl.pallas_call(
         head_kernel,

time: 29 us -> 28.1 us (0.969)
  starting transfers between devices: 12.1 us -> 11.3 us
  Pallas kernels: 8.52 us -> 7.94 us
  waiting for transfers between devices: 7.48 us -> 7.87 us
    all_to_all x1, starting transfers between devices: 5.7 us -> 4.56 us  [shards(): sums = lax.all_to_all(sums, AXES, 0, 0, tiled=True)]
    ppermute x2, starting transfers between devices: 3.16 us -> 4.15 us  [exchange(): near = lax.ppermute(near, AXES, swaps(axis, 0, counts))]
    ppermute x2, starting transfers between devices: 3.21 us -> 2.61 us  [exchange(): far = lax.ppermute(far, AXES, swaps(axis, 1, counts))]
    all_to_all x1, waiting for transfers between devices: 3.26 us -> 3.65 us  [shards(): sums = lax.all_to_all(sums, AXES, 0, 0, tiled=True)]
    pallas_call x1, Pallas kernels: 3.89 us -> 3.49 us  [shards(): pl.pallas_call(functools.partial(state_kernel, counts), out_shape=(shape(...]
  transfers between devices with their start and end apart: 5 -> 5, of which waited for: 3 -> 3; matrix products, arithmetic and copies ran while one was open for 0% -> 0% of each run, Pallas kernels for 14% -> 13%
where the time goes in v4:
time: 28.1 us; the launch traced here: 27.8 us
  starting transfers between devices  11.3 us (40%)
  Pallas kernels  7.94 us (28%)
  waiting for transfers between devices  7.87 us (28%)
  between operations  0.66 us (2%)
    all_to_all x1, starting transfers between devices, shards(): sums = lax.all_to_all(sums, AXES, 0, 0, tiled=True)  4.56 us
    ppermute x2, starting transfers between devices, exchange(): near = lax.ppermute(near, AXES, swaps(axis, 0, counts))  4.15 us
    all_to_all x1, waiting for transfers between devices, shards(): sums = lax.all_to_all(sums, AXES, 0, 0, tiled=True)  3.65 us
    pallas_call x1, Pallas kernels, shards(): pl.pallas_call(functools.partial(state_kernel, counts), out_shape=(shape(...  3.49 us
    pallas_call x1, Pallas kernels, shards(): pl.pallas_call(functools.partial(depth_kernel, counts), out_shape=(shape(...  2.67 us
    ppermute x2, starting transfers between devices, exchange(): far = lax.ppermute(far, AXES, swaps(axis, 1, counts))  2.61 us
    ppermute x2, waiting for transfers between devices, exchange(): far = lax.ppermute(far, AXES, swaps(axis, 1, counts))  2.46 us
    ppermute x2, waiting for transfers between devices, exchange(): near = lax.ppermute(near, AXES, swaps(axis, 0, counts))  1.76 us
  transfers between devices with their start and end apart: 5, of which 3 were waited for; matrix products, arithmetic and copies ran while one was open for 0% of the time, Pallas kernels for 13%

profile of v4, /device:TPU:0, one launch (start us, length us, event | category | flops | bytes accessed | tf_op | source)
XLA Modules:
  0.0 27.8 jit_solution(13102873665576504426)
XLA Ops:
  0.6 1.0 %pack_columns.1 = (f32[7,32,128]{2,1,0:T(8,128)S(1)}, f32[40,128]{1,0:T(8,128)S(1)}, f32[40,128]{1,0:T(8,128)S(1)}, f32[8,128]{1,0:T(8,128)S(1)}) custom-call(f32[32,128]{1,0:T(8,128)} %refs_0_.1, f32[3,32,128]{2,1,0:T(8,128)} %refs_1_.1, f32[32,128]{1,0:T(8,128)} %refs_2_.1, f32[32,128]{1,0:T(8,128)} %refs_3_.1, s32[32,128]{1,0:T(8,128)} %refs_4_.1, ...), custom_call_target="tpu_custom_call" | custom-call | tf_op jit(solution)/shard_map/pack_columns/pallas_call | solution.py:348
  1.7 0.5 %collective-permute-start = (f32[40,128]{1,0:T(8,128)S(1)}, f32[40,128]{1,0:T(8,128)S(1)}, u32[]{:S(2)}, u32[]{:S(2)}) collective-permute-start(f32[40,128]{1,0:T(8,128)S(1)} %get-tuple-element.17), channel_id=1, source_target_pairs={{0,1},{1,0},{2,3},{3,2},{4,5},{5,4},{6,7},{7,6},{8,16},{9,17},{10,... | collective-permute-start | bytes 61448 | tf_op jit(solution)/shard_map/ppermute | solution.py:340
  2.2 4.1 %collective-permute-start.1 = (f32[40,128]{1,0:T(8,128)S(1)}, f32[40,128]{1,0:T(8,128)S(1)}, u32[]{:S(2)}, u32[]{:S(2)}) collective-permute-start(f32[40,128]{1,0:T(8,128)S(1)} %get-tuple-element.18), channel_id=1, source_target_pairs={{0,8},{1,9},{2,10},{3,11},{4,12},{5,13},{6,14},{7,15},{8,0},{9,1},... | collective-permute-start | bytes 61448 | tf_op jit(solution)/shard_map/ppermute | solution.py:339
  6.3 0.0 collective-permute-done.side_far
  6.3 1.8 %collective-permute-done.1.side_near = f32[40,128]{1,0:T(8,128)S(1)} collective-permute-done((f32[40,128]{1,0:T(8,128)S(1)}, f32[40,128]{1,0:T(8,128)S(1)}, u32[]{:S(2)}, u32[]{:S(2)}) %collective-permute-start.1) | collective-permute-done | bytes 20512 | tf_op jit(solution)/shard_map/ppermute | solution.py:339
  8.1 2.1 %collective-permute-start.2 = (f32[168,128]{1,0:T(8,128)S(1)}, f32[168,128]{1,0:T(8,128)S(1)}, u32[]{:S(2)}, u32[]{:S(2)}) collective-permute-start(f32[168,128]{1,0:T(8,128)S(1)} %get-tuple-element.22), channel_id=1, source_target_pairs={{0,8},{1,2},{2,1},{3,4},{4,3},{5,6},{6,5},{7,15},{8,0},{9,10},{10,... | collective-permute-start | bytes 258056 | tf_op jit(solution)/shard_map/ppermute | solution.py:340
  10.2 0.0 collective-permute-start.3
  10.2 2.5 %collective-permute-done.2.far = f32[168,128]{1,0:T(8,128)S(1)} collective-permute-done((f32[168,128]{1,0:T(8,128)S(1)}, f32[168,128]{1,0:T(8,128)S(1)}, u32[]{:S(2)}, u32[]{:S(2)}) %collective-permute-start.2) | collective-permute-done | bytes 86048 | tf_op jit(solution)/shard_map/ppermute | solution.py:340
  12.7 0.0 collective-permute-done.3.near
  12.7 2.7 %depth_and_moments.1 = (f32[32,128]{1,0:T(8,128)}, f32[8,128]{1,0:T(8,128)S(1)}, f32[8,128]{1,0:T(8,128)S(1)}) custom-call(f32[7,32,128]{2,1,0:T(8,128)S(1)} %get-tuple-element.16.own, f32[40,128]{1,0:T(8,128)S(1)} %get-tuple-element.20.east, f32[40,128]{1,0:T(8,128)S(1)} %get-tuple-element.21.west, f32[168,128]{1,0:T(8,128)S(1)} %collective-permute-done.2.far, ...), custom_call_target="tpu_custom_call" | custom-call | tf_op jit(solution)/shard_map/depth_and_moments/pallas_call | solution.py:368
  15.4 4.6 %all-to-all-start = ((f32[32,1,128]{2,1,0:T(1,128)}), f32[32,1,128]{2,1,0:T(1,128)S(1)}, u32[]{:S(2)}, u32[]{:S(2)}) async-start(f32[32,1,128]{2,1,0:T(1,128)} %bitcast.1), calls=%async_computation | async-start | bytes 32768 | tf_op jit(solution)/shard_map/all_to_all | solution.py:395
  19.9 3.5 %all_channels.1 = (f32[32,128]{1,0:T(8,128)}, f32[3,32,128]{2,1,0:T(8,128)}) custom-call(f32[7,32,128]{2,1,0:T(8,128)S(1)} %get-tuple-element.16.own, f32[40,128]{1,0:T(8,128)S(1)} %get-tuple-element.20.east, f32[40,128]{1,0:T(8,128)S(1)} %get-tuple-element.21.west, f32[168,128]{1,0:T(8,128)S(1)} %collective-permute-done.2.far, ...), custom_call_target="tpu_custom_call" | custom-call | flops 20000000 | bytes 20000000 | tf_op jit(solution)/shard_map/all_channels/pallas_call | solution.py:382
  23.4 3.7 %all-to-all-done = f32[32,1,128]{2,1,0:T(1,128)S(1)} async-done(((f32[32,1,128]{2,1,0:T(1,128)}), f32[32,1,128]{2,1,0:T(1,128)S(1)}, u32[]{:S(2)}, u32[]{:S(2)}) %all-to-all-start) | async-done | bytes 16416 | tf_op jit(solution)/shard_map/all_to_all | solution.py:395
  27.1 0.7 %combine_head.1 = f32[8,32]{1,0:T(8,128)} custom-call(f32[32,128]{1,0:T(8,128)S(1)} %bitcast.4, f32[8,128]{1,0:T(8,128)S(1)} %get-tuple-element.27.zc, f32[8,128]{1,0:T(8,128)S(1)} %get-tuple-element.28.uc), custom_call_target="tpu_custom_call" | custom-call | tf_op jit(solution)/shard_map/combine_head/pallas_call | solution.py:396
  (1 shorter events, 0.0 us)
Async XLA Ops:
  1.7 4.7 %collective-permute-start = (f32[40,128]{1,0:T(8,128)S(1)}, f32[40,128]{1,0:T(8,128)S(1)}, u32[]{:S(2)}, u32[]{:S(2)}) collective-permute-start(f32[40,128]{1,0:T(8,128)S(1)} %get-tuple-element.17), channel_id=1, source_target_pairs={{0,1},{1,0},{2,3},{3,2},{4,5},{5,4},{6,7},{7,6},{8,16},{9,17},{10,... | collective-permute-start | bytes 61448 | tf_op jit(solution)/shard_map/ppermute | solution.py:340
  2.2 5.9 %collective-permute-start.1 = (f32[40,128]{1,0:T(8,128)S(1)}, f32[40,128]{1,0:T(8,128)S(1)}, u32[]{:S(2)}, u32[]{:S(2)}) collective-permute-start(f32[40,128]{1,0:T(8,128)S(1)} %get-tuple-element.18), channel_id=1, source_target_pairs={{0,8},{1,9},{2,10},{3,11},{4,12},{5,13},{6,14},{7,15},{8,0},{9,1},... | collective-permute-start | bytes 61448 | tf_op jit(solution)/shard_map/ppermute | solution.py:339
  8.1 4.6 %collective-permute-start.2 = (f32[168,128]{1,0:T(8,128)S(1)}, f32[168,128]{1,0:T(8,128)S(1)}, u32[]{:S(2)}, u32[]{:S(2)}) collective-permute-start(f32[168,128]{1,0:T(8,128)S(1)} %get-tuple-element.22), channel_id=1, source_target_pairs={{0,8},{1,2},{2,1},{3,4},{4,3},{5,6},{6,5},{7,15},{8,0},{9,10},{10,... | collective-permute-start | bytes 258056 | tf_op jit(solution)/shard_map/ppermute | solution.py:340
  10.2 2.5 %collective-permute-start.3 = (f32[168,128]{1,0:T(8,128)S(1)}, f32[168,128]{1,0:T(8,128)S(1)}, u32[]{:S(2)}, u32[]{:S(2)}) collective-permute-start(f32[168,128]{1,0:T(8,128)S(1)} %get-tuple-element.23), channel_id=1, source_target_pairs={{0,1},{1,0},{2,3},{3,2},{4,5},{5,4},{6,7},{7,6},{8,9},{9,8},{10,11... | collective-permute-start | bytes 258056 | tf_op jit(solution)/shard_map/ppermute | solution.py:339
  15.4 11.7 %all-to-all-start = ((f32[32,1,128]{2,1,0:T(1,128)}), f32[32,1,128]{2,1,0:T(1,128)S(1)}, u32[]{:S(2)}, u32[]{:S(2)}) async-start(f32[32,1,128]{2,1,0:T(1,128)} %bitcast.1), calls=%async_computation | async-start | bytes 32768 | tf_op jit(solution)/shard_map/all_to_all | solution.py:395

commit v5 on v4

--- a/solution.py
+++ b/solution.py
@@ -19,9 +19,11 @@
 SLOTS = ((0, WIDE), (WIDE, WIDE), (2 * WIDE, WIDE), (3 * WIDE, WIDE)) + tuple(
     (4 * WIDE + k * SLIM, SLIM) for k in range(3)
 )
-EAST_AT = 4 * WIDE + 3 * SLIM
+EAST_AT = 4 * WIDE
 WEST_AT = EAST_AT + WIDE
 COARSE_AT = WEST_AT + WIDE
+EARLY = 128
+ROWS_AT = (0, WIDE, 2 * WIDE, 3 * WIDE) + tuple(EARLY + k * SLIM for k in range(3))
 STRIP = 168
 F32 = jnp.float32
 SMALL = pltpu.CompilerParams(vmem_limit_bytes=2 << 20)
@@ -75,7 +77,7 @@
     far[rows : rows + act.shape[0]] = both
 
 
-def pack_rows(own, side_far, side_near, coarse, near, far, east, west):
+def pack_rows(own, side_far, side_near, coarse, near, far, near_late, far_late, east, west):
     flip = lax.axis_index("gx") % 2 == 1
     east[...] = jnp.where(flip, side_far[...], side_near[...])
     west[...] = jnp.where(flip, side_near[...], side_far[...])
@@ -84,18 +86,22 @@
     odd = lax.axis_index("gy") % 2 == 1
 
     def put(at, top, bottom):
-        near[at : at + top.shape[0]] = jnp.where(odd, top, bottom)
-        far[at : at + top.shape[0]] = jnp.where(odd, bottom, top)
-
-    for k, (at, width) in enumerate(SLOTS):
+        count = top.shape[0]
+        early = at < EARLY
+        at = at if early else at - EARLY
+        (near if early else near_late)[at : at + count] = jnp.where(odd, top, bottom)
+        (far if early else far_late)[at : at + count] = jnp.where(odd, bottom, top)
+
+    for k, at in enumerate(ROWS_AT):
+        width = SLOTS[k][1]
         put(at, own[k, 0:width], own[k, rows - width : rows])
     for at, side in ((EAST_AT, east), (WEST_AT, west)):
         put(at, side[0:WIDE], side[rows - WIDE : rows])
-    for at, part in ((COARSE_AT, coarse), (COARSE_AT + 2, east.at[rows : rows + crows]), (COARSE_AT + 4, west.at[rows : rows + crows])):
-        put(at, part[0:2], part[crows - 2 : crows])
-    rest = jnp.zeros((STRIP - COARSE_AT - 6, LANES), F32)
-    near[COARSE_AT + 6 : STRIP] = rest
-    far[COARSE_AT + 6 : STRIP] = rest
+    for k, part in enumerate((coarse, east.at[rows : rows + crows], west.at[rows : rows + crows])):
+        put(COARSE_AT + 2 * k, part[0:2], part[crows - 2 : crows])
+    for start, stop in ((COARSE_AT + 6, EARLY), (ROWS_AT[-1] + SLIM, STRIP)):
+        rest = jnp.zeros((stop - start, LANES), F32)
+        put(start, rest, rest)
 
 
 def inside(counts):
@@ -104,12 +110,14 @@
     return row > 0, row < counts[1] - 1, col < counts[0] - 1, col > 0
 
 
-def rows_from(near, far, start, count, use_near, present):
+def rows_from(near, far, late, start, count, use_near, present):
+    if start >= EARLY:
+        (near, far), start = late, start - EARLY
     got = jnp.where(use_near, near[start : start + count], far[start : start + count])
     return jnp.where(present, got, 0.0)
 
 
-def gather_fields(kinds, halo, own, east, west, near, far, flags, stage):
+def gather_fields(kinds, halo, own, east, west, near, far, late, flags, stage):
     has_north, has_south, has_east, has_west = flags
     rows = own.shape[1]
     total = rows + 2 * halo
@@ -117,16 +125,15 @@
     odd = lax.axis_index("gy") % 2 == 1
 
     def lay(slot, at, width, middle):
-        stage[slot, 0:halo] = rows_from(near, far, at + width - halo, halo, odd, has_north)
+        stage[slot, 0:halo] = rows_from(near, far, late, at + width - halo, halo, odd, has_north)
         stage[slot, halo : halo + rows] = middle
-        stage[slot, halo + rows : total] = rows_from(near, far, at, halo, ~odd, has_south)
+        stage[slot, halo + rows : total] = rows_from(near, far, late, at, halo, ~odd, has_south)
 
     def read(slot):
         return [stage[slot, pl.ds(i, 8, stride=chunk)] for i in range(chunk)]
 
     for k in kinds:
-        at, width = SLOTS[k]
-        lay(k, at, width, own[k])
+        lay(k, ROWS_AT[k], SLOTS[k][1], own[k])
     lay(7, EAST_AT, WIDE, east[0:rows])
     lay(8, WEST_AT, WIDE, west[0:rows])
     east_parts = read(7)
@@ -195,9 +202,9 @@
 KEEP = 1.0 - TIME_STEP * INFILTRATION
 
 
-def depth_kernel(counts, own, east, west, far, near, coarse, sums, zc, uc, stage, masks, cst):
+def depth_kernel(counts, own, east, west, near, far, coarse, sums, zc, uc, stage, masks, cst):
     flags = inside(counts)
-    depth, rain, coef, codes = gather_fields((0, 1, 2, 3), WIDE, own, east, west, near, far, flags, stage)
+    depth, rain, coef, codes = gather_fields((0, 1, 2, 3), WIDE, own, east, west, near, far, None, flags, stage)
     move_masks(codes, coef, masks)
 
     crows, ccols = zc.shape[0], LANES // 4
@@ -212,9 +219,9 @@
     for k, middle in enumerate((coarse[...], east[rows : rows + crows], west[rows : rows + crows])):
         at = COARSE_AT + 2 * k
         cst[k] = jnp.zeros((16, LANES), F32)
-        cst[k, 1:3] = rows_from(near, far, at, 2, odd, has_north)
+        cst[k, 1:3] = rows_from(near, far, None, at, 2, odd, has_north)
         cst[k, 3 : 3 + crows] = middle
-        cst[k, 3 + crows : 5 + crows] = rows_from(near, far, at, 2, ~odd, has_south)
+        cst[k, 3 + crows : 5 + crows] = rows_from(near, far, None, at, 2, ~odd, has_south)
     ids = lane_ids(16)
     e_here = (ids >= ccols) & (ids < jnp.where(has_east, ccols + 2, ccols))
     w_here = ids >= jnp.where(has_west, LANES - 2, LANES)
@@ -273,10 +280,10 @@
     uc[...] = u
 
 
-def state_kernel(counts, own, east, west, far, near, depth_out, tracers_out, stage, masks):
+def state_kernel(counts, own, east, west, far, near, far_late, near_late, depth_out, tracers_out, stage, masks):
     flags = inside(counts)
     depth, rain, coef, codes, *species = gather_fields(
-        (0, 1, 2, 3, 4, 5, 6), SLIM, own, east, west, near, far, flags, stage
+        (0, 1, 2, 3, 4, 5, 6), SLIM, own, east, west, near, far, (near_late, far_late), flags, stage
     )
     move_masks(codes, coef, masks)
 
@@ -355,15 +362,23 @@
         name="pack_columns",
     )(*[pltpu.with_memory_space_constraint(a, pltpu.MemorySpace.HBM) for a in inputs])
     near, far = exchange(near, far, "gx", counts)
-    near, far, east, west = pl.pallas_call(
+    near, far, near_late, far_late, east, west = pl.pallas_call(
         pack_rows,
-        out_shape=(shape(STRIP, LANES), shape(STRIP, LANES), shape(rows + crows, LANES), shape(rows + crows, LANES)),
+        out_shape=(
+            shape(EARLY, LANES),
+            shape(EARLY, LANES),
+            shape(STRIP - EARLY, LANES),
+            shape(STRIP - EARLY, LANES),
+            shape(rows + crows, LANES),
+            shape(rows + crows, LANES),
+        ),
         in_specs=whole(4),
-        out_specs=tuple(whole(4)),
+        out_specs=tuple(whole(6)),
         compiler_params=SMALL,
         name="pack_rows",
     )(own, far, near, coarse)
     near, far = exchange(near, far, "gy", counts)
+    near_late, far_late = exchange(near_late, far_late, "gy", counts)
     deep = rows + 2 * WIDE
     sums, zc, uc = pl.pallas_call(
         functools.partial(depth_kernel, counts),
@@ -376,13 +391,15 @@
             pltpu.VMEM((3, 16, LANES), F32),
         ],
         compiler_params=ROOMY,
+        cost_estimate=pl.CostEstimate(flops=20000000, bytes_accessed=20000000, transcendentals=0),
         name="depth_and_moments",
-    )(own, east, west, far, near, coarse)
+    )(own, east, west, near, far, coarse)
+    sums, near_late, far_late = lax.optimization_barrier((sums, near_late, far_late))
     low = rows + 2 * SLIM
     depth_out, tracers_out = pl.pallas_call(
         functools.partial(state_kernel, counts),
         out_shape=(shape(rows, cols), shape(3, rows, cols)),
-        in_specs=whole(5),
+        in_specs=whole(7),
         out_specs=tuple(whole(2)),
         scratch_shapes=[
             pltpu.VMEM((9, low, LANES), F32),
@@ -391,7 +408,7 @@
         cost_estimate=pl.CostEstimate(flops=20_000_000, bytes_accessed=20_000_000, transcendentals=0),
         compiler_params=ROOMY,
         name="all_channels",
-    )(own, east, west, far, near)
+    )(own, east, west, far, near, far_late, near_late)
     sums = lax.all_to_all(sums, AXES, 0, 0, tiled=True)
     head = pl.pallas_call(
         head_kernel,

time: 28.1 us -> 27.7 us (0.986)
  waiting for transfers between devices: 7.87 us -> 6.05 us
  starting transfers between devices: 11.3 us -> 12.7 us
    ppermute x2 -> x3, waiting for transfers between devices: 2.46 us -> 0.64 us  [exchange(): far = lax.ppermute(far, AXES, swaps(axis, 1, counts))]
    ppermute x2 -> x3, starting transfers between devices: 2.61 us -> 3.7 us  [exchange(): far = lax.ppermute(far, AXES, swaps(axis, 1, counts))]
    ppermute x2 -> x3, starting transfers between devices: 4.15 us -> 4.66 us  [exchange(): near = lax.ppermute(near, AXES, swaps(axis, 0, counts))]
    ppermute x2 -> x3, waiting for transfers between devices: 1.76 us -> 1.76 us  [exchange(): near = lax.ppermute(near, AXES, swaps(axis, 0, counts))]
  transfers between devices with their start and end apart: 5 -> 7, of which waited for: 3 -> 3; matrix products, arithmetic and copies ran while one was open for 0% -> 0% of each run, Pallas kernels for 13% -> 23%
where the time goes in v5:
time: 27.7 us; the launch traced here: 27.4 us
  starting transfers between devices  12.7 us (46%)
  Pallas kernels  7.94 us (29%)
  waiting for transfers between devices  6.05 us (22%)
  between operations  0.66 us (2%)
    ppermute x3, starting transfers between devices, exchange(): near = lax.ppermute(near, AXES, swaps(axis, 0, counts))  4.66 us
    all_to_all x1, starting transfers between devices, shards(): sums = lax.all_to_all(sums, AXES, 0, 0, tiled=True)  4.34 us
    ppermute x3, starting transfers between devices, exchange(): far = lax.ppermute(far, AXES, swaps(axis, 1, counts))  3.7 us
    all_to_all x1, waiting for transfers between devices, shards(): sums = lax.all_to_all(sums, AXES, 0, 0, tiled=True)  3.65 us
    pallas_call x1, Pallas kernels, shards(): pl.pallas_call(functools.partial(state_kernel, counts), out_shape=(shape(...  3.49 us
    pallas_call x1, Pallas kernels, shards(): pl.pallas_call(functools.partial(depth_kernel, counts), out_shape=(shape(...  2.67 us
    ppermute x3, waiting for transfers between devices, exchange(): near = lax.ppermute(near, AXES, swaps(axis, 0, counts))  1.76 us
    pallas_call x1, Pallas kernels, shards(): pl.pallas_call(pack_columns, out_shape=(shape(7, rows, cols), shape(rows...  1.04 us
  transfers between devices with their start and end apart: 7, of which 3 were waited for; matrix products, arithmetic and copies ran while one was open for 0% of the time, Pallas kernels for 23%

profile of v5, /device:TPU:0, one launch (start us, length us, event | category | flops | bytes accessed | tf_op | source)
XLA Modules:
  0.0 27.4 jit_solution(16020376572406806839)
XLA Ops:
  0.6 1.0 %pack_columns.1 = (f32[7,32,128]{2,1,0:T(8,128)S(1)}, f32[40,128]{1,0:T(8,128)S(1)}, f32[40,128]{1,0:T(8,128)S(1)}, f32[8,128]{1,0:T(8,128)S(1)}) custom-call(f32[32,128]{1,0:T(8,128)} %refs_0_.1, f32[3,32,128]{2,1,0:T(8,128)} %refs_1_.1, f32[32,128]{1,0:T(8,128)} %refs_2_.1, f32[32,128]{1,0:T(8,128)} %refs_3_.1, s32[32,128]{1,0:T(8,128)} %refs_4_.1, ...), custom_call_target="tpu_custom_call" | custom-call | tf_op jit(solution)/shard_map/pack_columns/pallas_call | solution.py:355
  1.7 0.5 %collective-permute-start = (f32[40,128]{1,0:T(8,128)S(1)}, f32[40,128]{1,0:T(8,128)S(1)}, u32[]{:S(2)}, u32[]{:S(2)}) collective-permute-start(f32[40,128]{1,0:T(8,128)S(1)} %get-tuple-element.22), channel_id=1, source_target_pairs={{0,1},{1,0},{2,3},{3,2},{4,5},{5,4},{6,7},{7,6},{8,16},{9,17},{10,... | collective-permute-start | bytes 61448 | tf_op jit(solution)/shard_map/ppermute | solution.py:347
  2.2 4.1 %collective-permute-start.1 = (f32[40,128]{1,0:T(8,128)S(1)}, f32[40,128]{1,0:T(8,128)S(1)}, u32[]{:S(2)}, u32[]{:S(2)}) collective-permute-start(f32[40,128]{1,0:T(8,128)S(1)} %get-tuple-element.23), channel_id=1, source_target_pairs={{0,8},{1,9},{2,10},{3,11},{4,12},{5,13},{6,14},{7,15},{8,0},{9,1},... | collective-permute-start | bytes 61448 | tf_op jit(solution)/shard_map/ppermute | solution.py:346
  6.3 0.0 collective-permute-done.side_far
  6.3 1.8 %collective-permute-done.1.side_near = f32[40,128]{1,0:T(8,128)S(1)} collective-permute-done((f32[40,128]{1,0:T(8,128)S(1)}, f32[40,128]{1,0:T(8,128)S(1)}, u32[]{:S(2)}, u32[]{:S(2)}) %collective-permute-start.1) | collective-permute-done | bytes 20512 | tf_op jit(solution)/shard_map/ppermute | solution.py:346
  8.1 2.1 %collective-permute-start.2 = (f32[128,128]{1,0:T(8,128)S(1)}, f32[128,128]{1,0:T(8,128)S(1)}, u32[]{:S(2)}, u32[]{:S(2)}) collective-permute-start(f32[128,128]{1,0:T(8,128)S(1)} %get-tuple-element.27), channel_id=1, source_target_pairs={{0,8},{1,2},{2,1},{3,4},{4,3},{5,6},{6,5},{7,15},{8,0},{9,10},{10,... | collective-permute-start | bytes 196616 | tf_op jit(solution)/shard_map/ppermute | solution.py:347
  10.2 0.0 collective-permute-start.3
  10.2 0.5 %collective-permute-start.4 = (f32[40,128]{1,0:T(8,128)S(1)}, f32[40,128]{1,0:T(8,128)S(1)}, u32[]{:S(2)}, u32[]{:S(2)}) collective-permute-start(f32[40,128]{1,0:T(8,128)S(1)} %get-tuple-element.30), channel_id=1, source_target_pairs={{0,1},{1,0},{2,3},{3,2},{4,5},{5,4},{6,7},{7,6},{8,9},{9,8},{10,11... | collective-permute-start | bytes 61448 | tf_op jit(solution)/shard_map/ppermute | solution.py:346
  10.7 1.1 %collective-permute-start.5 = (f32[40,128]{1,0:T(8,128)S(1)}, f32[40,128]{1,0:T(8,128)S(1)}, u32[]{:S(2)}, u32[]{:S(2)}) collective-permute-start(f32[40,128]{1,0:T(8,128)S(1)} %get-tuple-element.31), channel_id=1, source_target_pairs={{0,8},{1,2},{2,1},{3,4},{4,3},{5,6},{6,5},{7,15},{8,0},{9,10},{10,... | collective-permute-start | bytes 61448 | tf_op jit(solution)/shard_map/ppermute | solution.py:347
  11.8 0.6 %collective-permute-done.2.far = f32[128,128]{1,0:T(8,128)S(1)} collective-permute-done((f32[128,128]{1,0:T(8,128)S(1)}, f32[128,128]{1,0:T(8,128)S(1)}, u32[]{:S(2)}, u32[]{:S(2)}) %collective-permute-start.2) | collective-permute-done | bytes 65568 | tf_op jit(solution)/shard_map/ppermute | solution.py:347
  12.5 0.0 collective-permute-done.3.near
  12.5 2.7 %depth_and_moments.1 = (f32[32,128]{1,0:T(8,128)}, f32[8,128]{1,0:T(8,128)S(1)}, f32[8,128]{1,0:T(8,128)S(1)}) custom-call(f32[7,32,128]{2,1,0:T(8,128)S(1)} %get-tuple-element.21.own, f32[40,128]{1,0:T(8,128)S(1)} %get-tuple-element.25.east, f32[40,128]{1,0:T(8,128)S(1)} %get-tuple-element.26.west, f32[128,128]{1,0:T(8,128)S(1)} %collective-permute-done.3.near, ...), custom_call_target="tpu_custom_call" | custom-call | flops 20000000 | bytes 20000000 | tf_op jit(solution)/shard_map/depth_and_moments/pallas_call | solution.py:383
  15.2 0.0 collective-permute-done.4.near_late
  15.2 0.0 collective-permute-done.5.far_late
  15.2 4.3 %all-to-all-start = ((f32[32,1,128]{2,1,0:T(1,128)}), f32[32,1,128]{2,1,0:T(1,128)S(1)}, u32[]{:S(2)}, u32[]{:S(2)}) async-start(f32[32,1,128]{2,1,0:T(1,128)} %bitcast.1), calls=%async_computation | async-start | bytes 32768 | tf_op jit(solution)/shard_map/all_to_all | solution.py:412
  19.5 3.5 %all_channels.1 = (f32[32,128]{1,0:T(8,128)}, f32[3,32,128]{2,1,0:T(8,128)}) custom-call(f32[7,32,128]{2,1,0:T(8,128)S(1)} %get-tuple-element.21.own, f32[40,128]{1,0:T(8,128)S(1)} %get-tuple-element.25.east, f32[40,128]{1,0:T(8,128)S(1)} %get-tuple-element.26.west, f32[128,128]{1,0:T(8,128)S(1)} %collective-permute-done.2.far, ...), custom_call_target="tpu_custom_call" | custom-call | flops 20000000 | bytes 20000000 | tf_op jit(solution)/shard_map/all_channels/pallas_call | solution.py:399
  23.0 3.7 %all-to-all-done = f32[32,1,128]{2,1,0:T(1,128)S(1)} async-done(((f32[32,1,128]{2,1,0:T(1,128)}), f32[32,1,128]{2,1,0:T(1,128)S(1)}, u32[]{:S(2)}, u32[]{:S(2)}) %all-to-all-start) | async-done | bytes 16416 | tf_op jit(solution)/shard_map/all_to_all | solution.py:412
  26.7 0.7 %combine_head.1 = f32[8,32]{1,0:T(8,128)} custom-call(f32[32,128]{1,0:T(8,128)S(1)} %bitcast.4, f32[8,128]{1,0:T(8,128)S(1)} %get-tuple-element.37.zc, f32[8,128]{1,0:T(8,128)S(1)} %get-tuple-element.38.uc), custom_call_target="tpu_custom_call" | custom-call | tf_op jit(solution)/shard_map/combine_head/pallas_call | solution.py:413
  (1 shorter events, 0.0 us)
Async XLA Ops:
  1.7 4.7 %collective-permute-start = (f32[40,128]{1,0:T(8,128)S(1)}, f32[40,128]{1,0:T(8,128)S(1)}, u32[]{:S(2)}, u32[]{:S(2)}) collective-permute-start(f32[40,128]{1,0:T(8,128)S(1)} %get-tuple-element.22), channel_id=1, source_target_pairs={{0,1},{1,0},{2,3},{3,2},{4,5},{5,4},{6,7},{7,6},{8,16},{9,17},{10,... | collective-permute-start | bytes 61448 | tf_op jit(solution)/shard_map/ppermute | solution.py:347
  2.2 5.9 %collective-permute-start.1 = (f32[40,128]{1,0:T(8,128)S(1)}, f32[40,128]{1,0:T(8,128)S(1)}, u32[]{:S(2)}, u32[]{:S(2)}) collective-permute-start(f32[40,128]{1,0:T(8,128)S(1)} %get-tuple-element.23), channel_id=1, source_target_pairs={{0,8},{1,9},{2,10},{3,11},{4,12},{5,13},{6,14},{7,15},{8,0},{9,1},... | collective-permute-start | bytes 61448 | tf_op jit(solution)/shard_map/ppermute | solution.py:346
  8.1 4.3 %collective-permute-start.2 = (f32[128,128]{1,0:T(8,128)S(1)}, f32[128,128]{1,0:T(8,128)S(1)}, u32[]{:S(2)}, u32[]{:S(2)}) collective-permute-start(f32[128,128]{1,0:T(8,128)S(1)} %get-tuple-element.27), channel_id=1, source_target_pairs={{0,8},{1,2},{2,1},{3,4},{4,3},{5,6},{6,5},{7,15},{8,0},{9,10},{10,... | collective-permute-start | bytes 196616 | tf_op jit(solution)/shard_map/ppermute | solution.py:347
  10.2 2.2 %collective-permute-start.3 = (f32[128,128]{1,0:T(8,128)S(1)}, f32[128,128]{1,0:T(8,128)S(1)}, u32[]{:S(2)}, u32[]{:S(2)}) collective-permute-start(f32[128,128]{1,0:T(8,128)S(1)} %get-tuple-element.28), channel_id=1, source_target_pairs={{0,1},{1,0},{2,3},{3,2},{4,5},{5,4},{6,7},{7,6},{8,9},{9,8},{10,11... | collective-permute-start | bytes 196616 | tf_op jit(solution)/shard_map/ppermute | solution.py:346
  10.2 4.9 %collective-permute-start.4 = (f32[40,128]{1,0:T(8,128)S(1)}, f32[40,128]{1,0:T(8,128)S(1)}, u32[]{:S(2)}, u32[]{:S(2)}) collective-permute-start(f32[40,128]{1,0:T(8,128)S(1)} %get-tuple-element.30), channel_id=1, source_target_pairs={{0,1},{1,0},{2,3},{3,2},{4,5},{5,4},{6,7},{7,6},{8,9},{9,8},{10,11... | collective-permute-start | bytes 61448 | tf_op jit(solution)/shard_map/ppermute | solution.py:346
  10.7 4.4 %collective-permute-start.5 = (f32[40,128]{1,0:T(8,128)S(1)}, f32[40,128]{1,0:T(8,128)S(1)}, u32[]{:S(2)}, u32[]{:S(2)}) collective-permute-start(f32[40,128]{1,0:T(8,128)S(1)} %get-tuple-element.31), channel_id=1, source_target_pairs={{0,8},{1,2},{2,1},{3,4},{4,3},{5,6},{6,5},{7,15},{8,0},{9,10},{10,... | collective-permute-start | bytes 61448 | tf_op jit(solution)/shard_map/ppermute | solution.py:347
  15.2 11.5 %all-to-all-start = ((f32[32,1,128]{2,1,0:T(1,128)}), f32[32,1,128]{2,1,0:T(1,128)S(1)}, u32[]{:S(2)}, u32[]{:S(2)}) async-start(f32[32,1,128]{2,1,0:T(1,128)} %bitcast.1), calls=%async_computation | async-start | bytes 32768 | tf_op jit(solution)/shard_map/all_to_all | solution.py:412

commit v6 on v5

--- a/solution.py
+++ b/solution.py
@@ -32,6 +32,11 @@
 
 def whole(count):
     return [pl.BlockSpec(memory_space=pltpu.VMEM)] * count
+
+
+def run(ids, start, width, present):
+    start = start % LANES
+    return (ids >= start) & (ids < (start + width if present is True else jnp.where(present, start + width, start)))
 
 
 def lane_ids(rows):
@@ -61,9 +66,9 @@
     head = jnp.zeros((rows, LANES), F32)
     tail = jnp.zeros((rows, LANES), F32)
     for field, (at, width) in zip(fields, SLOTS):
-        spot = (ids >= at) & (ids < at + width)
-        head = jnp.where(spot, pltpu.roll(field, at, 1) if at else field, head)
-        tail = jnp.where(spot, pltpu.roll(field, (at + width) % LANES, 1), tail)
+        moved = pltpu.roll(field, at, 1) if at else field
+        head = jnp.where(run(ids, at, width, True), moved, head)
+        tail = jnp.where(run(ids, at - width, width, True), moved, tail)
     for k, field in enumerate(fields):
         own[k] = field
     act = active[...].astype(F32)
@@ -142,13 +147,12 @@
     fields = []
     for k in kinds:
         at, width = SLOTS[k]
-        in_east = ids < jnp.where(has_east, width, 0)
-        in_west = ids >= jnp.where(has_west, LANES - width, LANES)
+        in_east = run(ids, at, width, has_east)
+        in_west = run(ids, at - width, width, has_west)
         parts = []
         for main, e, w in zip(read(k), east_parts, west_parts):
-            e = pltpu.roll(e, (LANES - at) % LANES, 1) if at else e
-            w = pltpu.roll(w, (2 * LANES - width - at) % LANES, 1)
             side = jnp.where(in_east, e, jnp.where(in_west, w, 0.0))
+            side = pltpu.roll(side, LANES - at, 1) if at else side
             parts.append(jnp.concatenate([main, side], axis=1)[None])
         fields.append(jnp.concatenate(parts, axis=0))
     return fields
@@ -171,28 +175,19 @@
 
 
 def move_masks(codes, coef, masks):
-    land = coef > 0.0
     sides = {-1: from_right(codes), 0: codes, 1: from_left(codes)}
+    ends = {-1: from_above(coef), 0: coef, 1: from_below(coef)}
     for k, (drow, dcol) in enumerate(MOVES):
-        seen = sides[dcol]
-        if drow == 1:
-            seen = from_above(seen)
-        elif drow == -1:
-            seen = from_below(seen)
-        masks[k] = jnp.where(land & (seen == float(k)), 1.0, 0.0)
+        masks[k] = jnp.where((ends[drow] > 0.0) & (sides[dcol] == float(k)), 1.0, 0.0)
 
 
 def inflow(flux, masks):
     sides = {-1: from_right(flux), 0: flux, 1: from_left(flux)}
-    total = None
-    for dcol in (0, 1, -1):
-        side = sides[dcol]
-        for drow, seen in ((0, side), (1, from_above(side)), (-1, from_below(side))):
-            if (drow, dcol) == (0, 0):
-                continue
-            term = masks[MOVES.index((drow, dcol))] * seen
-            total = term if total is None else total + term
-    return total
+    totals = {}
+    for k, (drow, dcol) in enumerate(MOVES):
+        term = masks[k] * sides[dcol]
+        totals[drow] = totals[drow] + term if drow in totals else term
+    return totals[0] + (from_above(totals[1]) + from_below(totals[-1]))
 
 
 def speed(depth, coef):

time: 27.7 us -> 27.7 us (level)
  transfers between devices with their start and end apart: 7 -> 7, of which waited for: 3 -> 3; matrix products, arithmetic and copies ran while one was open for 0% -> 0% of each run, Pallas kernels for 23% -> 22%
where the time goes in v6:
time: 27.7 us; the launch traced here: 27.4 us
  starting transfers between devices  12.7 us (46%)
  Pallas kernels  7.75 us (28%)
  waiting for transfers between devices  6.23 us (22%)
  between operations  0.66 us (2%)
    ppermute x3, starting transfers between devices, exchange(): near = lax.ppermute(near, AXES, swaps(axis, 0, counts))  4.66 us
    all_to_all x1, starting transfers between devices, shards(): sums = lax.all_to_all(sums, AXES, 0, 0, tiled=True)  4.34 us
    all_to_all x1, waiting for transfers between devices, shards(): sums = lax.all_to_all(sums, AXES, 0, 0, tiled=True)  3.83 us
    ppermute x3, starting transfers between devices, exchange(): far = lax.ppermute(far, AXES, swaps(axis, 1, counts))  3.7 us
    pallas_call x1, Pallas kernels, shards(): pl.pallas_call(functools.partial(state_kernel, counts), out_shape=(shape(...  3.32 us
    pallas_call x1, Pallas kernels, shards(): pl.pallas_call(functools.partial(depth_kernel, counts), out_shape=(shape(...  2.69 us
    ppermute x3, waiting for transfers between devices, exchange(): near = lax.ppermute(near, AXES, swaps(axis, 0, counts))  1.76 us
    pallas_call x1, Pallas kernels, shards(): pl.pallas_call(pack_columns, out_shape=(shape(7, rows, cols), shape(rows...  1.01 us
  transfers between devices with their start and end apart: 7, of which 3 were waited for; matrix products, arithmetic and copies ran while one was open for 0% of the time, Pallas kernels for 22%

profile of v6, /device:TPU:0, one launch (start us, length us, event | category | flops | bytes accessed | tf_op | source)
XLA Modules:
  0.0 27.4 jit_solution(10659595186779485552)
XLA Ops:
  0.6 1.0 %pack_columns.1 = (f32[7,32,128]{2,1,0:T(8,128)S(1)}, f32[40,128]{1,0:T(8,128)S(1)}, f32[40,128]{1,0:T(8,128)S(1)}, f32[8,128]{1,0:T(8,128)S(1)}) custom-call(f32[32,128]{1,0:T(8,128)} %refs_0_.1, f32[3,32,128]{2,1,0:T(8,128)} %refs_1_.1, f32[32,128]{1,0:T(8,128)} %refs_2_.1, f32[32,128]{1,0:T(8,128)} %refs_3_.1, s32[32,128]{1,0:T(8,128)} %refs_4_.1, ...), custom_call_target="tpu_custom_call" | custom-call | tf_op jit(solution)/shard_map/pack_columns/pallas_call | solution.py:350
  1.6 0.5 %collective-permute-start = (f32[40,128]{1,0:T(8,128)S(1)}, f32[40,128]{1,0:T(8,128)S(1)}, u32[]{:S(2)}, u32[]{:S(2)}) collective-permute-start(f32[40,128]{1,0:T(8,128)S(1)} %get-tuple-element.22), channel_id=1, source_target_pairs={{0,1},{1,0},{2,3},{3,2},{4,5},{5,4},{6,7},{7,6},{8,16},{9,17},{10,... | collective-permute-start | bytes 61448 | tf_op jit(solution)/shard_map/ppermute | solution.py:342
  2.2 4.1 %collective-permute-start.1 = (f32[40,128]{1,0:T(8,128)S(1)}, f32[40,128]{1,0:T(8,128)S(1)}, u32[]{:S(2)}, u32[]{:S(2)}) collective-permute-start(f32[40,128]{1,0:T(8,128)S(1)} %get-tuple-element.23), channel_id=1, source_target_pairs={{0,8},{1,9},{2,10},{3,11},{4,12},{5,13},{6,14},{7,15},{8,0},{9,1},... | collective-permute-start | bytes 61448 | tf_op jit(solution)/shard_map/ppermute | solution.py:341
  6.3 0.0 collective-permute-done.side_far
  6.3 1.8 %collective-permute-done.1.side_near = f32[40,128]{1,0:T(8,128)S(1)} collective-permute-done((f32[40,128]{1,0:T(8,128)S(1)}, f32[40,128]{1,0:T(8,128)S(1)}, u32[]{:S(2)}, u32[]{:S(2)}) %collective-permute-start.1) | collective-permute-done | bytes 20512 | tf_op jit(solution)/shard_map/ppermute | solution.py:341
  8.1 2.1 %collective-permute-start.2 = (f32[128,128]{1,0:T(8,128)S(1)}, f32[128,128]{1,0:T(8,128)S(1)}, u32[]{:S(2)}, u32[]{:S(2)}) collective-permute-start(f32[128,128]{1,0:T(8,128)S(1)} %get-tuple-element.27), channel_id=1, source_target_pairs={{0,8},{1,2},{2,1},{3,4},{4,3},{5,6},{6,5},{7,15},{8,0},{9,10},{10,... | collective-permute-start | bytes 196616 | tf_op jit(solution)/shard_map/ppermute | solution.py:342
  10.2 0.0 collective-permute-start.3
  10.2 0.5 %collective-permute-start.4 = (f32[40,128]{1,0:T(8,128)S(1)}, f32[40,128]{1,0:T(8,128)S(1)}, u32[]{:S(2)}, u32[]{:S(2)}) collective-permute-start(f32[40,128]{1,0:T(8,128)S(1)} %get-tuple-element.30), channel_id=1, source_target_pairs={{0,1},{1,0},{2,3},{3,2},{4,5},{5,4},{6,7},{7,6},{8,9},{9,8},{10,11... | collective-permute-start | bytes 61448 | tf_op jit(solution)/shard_map/ppermute | solution.py:341
  10.7 1.1 %collective-permute-start.5 = (f32[40,128]{1,0:T(8,128)S(1)}, f32[40,128]{1,0:T(8,128)S(1)}, u32[]{:S(2)}, u32[]{:S(2)}) collective-permute-start(f32[40,128]{1,0:T(8,128)S(1)} %get-tuple-element.31), channel_id=1, source_target_pairs={{0,8},{1,2},{2,1},{3,4},{4,3},{5,6},{6,5},{7,15},{8,0},{9,10},{10,... | collective-permute-start | bytes 61448 | tf_op jit(solution)/shard_map/ppermute | solution.py:342
  11.8 0.6 %collective-permute-done.2.far = f32[128,128]{1,0:T(8,128)S(1)} collective-permute-done((f32[128,128]{1,0:T(8,128)S(1)}, f32[128,128]{1,0:T(8,128)S(1)}, u32[]{:S(2)}, u32[]{:S(2)}) %collective-permute-start.2) | collective-permute-done | bytes 65568 | tf_op jit(solution)/shard_map/ppermute | solution.py:342
  12.4 0.0 collective-permute-done.3.near
  12.4 2.7 %depth_and_moments.1 = (f32[32,128]{1,0:T(8,128)}, f32[8,128]{1,0:T(8,128)S(1)}, f32[8,128]{1,0:T(8,128)S(1)}) custom-call(f32[7,32,128]{2,1,0:T(8,128)S(1)} %get-tuple-element.21.own, f32[40,128]{1,0:T(8,128)S(1)} %get-tuple-element.25.east, f32[40,128]{1,0:T(8,128)S(1)} %get-tuple-element.26.west, f32[128,128]{1,0:T(8,128)S(1)} %collective-permute-done.3.near, ...), custom_call_target="tpu_custom_call" | custom-call | flops 20000000 | bytes 20000000 | tf_op jit(solution)/shard_map/depth_and_moments/pallas_call | solution.py:378
  15.1 0.0 collective-permute-done.4.near_late
  15.1 0.0 collective-permute-done.5.far_late
  15.1 4.3 %all-to-all-start = ((f32[32,1,128]{2,1,0:T(1,128)}), f32[32,1,128]{2,1,0:T(1,128)S(1)}, u32[]{:S(2)}, u32[]{:S(2)}) async-start(f32[32,1,128]{2,1,0:T(1,128)} %bitcast.1), calls=%async_computation | async-start | bytes 32768 | tf_op jit(solution)/shard_map/all_to_all | solution.py:407
  19.5 3.3 %all_channels.1 = (f32[32,128]{1,0:T(8,128)}, f32[3,32,128]{2,1,0:T(8,128)}) custom-call(f32[7,32,128]{2,1,0:T(8,128)S(1)} %get-tuple-element.21.own, f32[40,128]{1,0:T(8,128)S(1)} %get-tuple-element.25.east, f32[40,128]{1,0:T(8,128)S(1)} %get-tuple-element.26.west, f32[128,128]{1,0:T(8,128)S(1)} %collective-permute-done.2.far, ...), custom_call_target="tpu_custom_call" | custom-call | flops 20000000 | bytes 20000000 | tf_op jit(solution)/shard_map/all_channels/pallas_call | solution.py:394
  22.8 3.8 %all-to-all-done = f32[32,1,128]{2,1,0:T(1,128)S(1)} async-done(((f32[32,1,128]{2,1,0:T(1,128)}), f32[32,1,128]{2,1,0:T(1,128)S(1)}, u32[]{:S(2)}, u32[]{:S(2)}) %all-to-all-start) | async-done | bytes 16416 | tf_op jit(solution)/shard_map/all_to_all | solution.py:407
  26.6 0.7 %combine_head.1 = f32[8,32]{1,0:T(8,128)} custom-call(f32[32,128]{1,0:T(8,128)S(1)} %bitcast.4, f32[8,128]{1,0:T(8,128)S(1)} %get-tuple-element.37.zc, f32[8,128]{1,0:T(8,128)S(1)} %get-tuple-element.38.uc), custom_call_target="tpu_custom_call" | custom-call | tf_op jit(solution)/shard_map/combine_head/pallas_call | solution.py:408
  (1 shorter events, 0.0 us)
Async XLA Ops:
  1.6 4.7 %collective-permute-start = (f32[40,128]{1,0:T(8,128)S(1)}, f32[40,128]{1,0:T(8,128)S(1)}, u32[]{:S(2)}, u32[]{:S(2)}) collective-permute-start(f32[40,128]{1,0:T(8,128)S(1)} %get-tuple-element.22), channel_id=1, source_target_pairs={{0,1},{1,0},{2,3},{3,2},{4,5},{5,4},{6,7},{7,6},{8,16},{9,17},{10,... | collective-permute-start | bytes 61448 | tf_op jit(solution)/shard_map/ppermute | solution.py:342
  2.2 5.9 %collective-permute-start.1 = (f32[40,128]{1,0:T(8,128)S(1)}, f32[40,128]{1,0:T(8,128)S(1)}, u32[]{:S(2)}, u32[]{:S(2)}) collective-permute-start(f32[40,128]{1,0:T(8,128)S(1)} %get-tuple-element.23), channel_id=1, source_target_pairs={{0,8},{1,9},{2,10},{3,11},{4,12},{5,13},{6,14},{7,15},{8,0},{9,1},... | collective-permute-start | bytes 61448 | tf_op jit(solution)/shard_map/ppermute | solution.py:341
  8.1 4.3 %collective-permute-start.2 = (f32[128,128]{1,0:T(8,128)S(1)}, f32[128,128]{1,0:T(8,128)S(1)}, u32[]{:S(2)}, u32[]{:S(2)}) collective-permute-start(f32[128,128]{1,0:T(8,128)S(1)} %get-tuple-element.27), channel_id=1, source_target_pairs={{0,8},{1,2},{2,1},{3,4},{4,3},{5,6},{6,5},{7,15},{8,0},{9,10},{10,... | collective-permute-start | bytes 196616 | tf_op jit(solution)/shard_map/ppermute | solution.py:342
  10.2 2.2 %collective-permute-start.3 = (f32[128,128]{1,0:T(8,128)S(1)}, f32[128,128]{1,0:T(8,128)S(1)}, u32[]{:S(2)}, u32[]{:S(2)}) collective-permute-start(f32[128,128]{1,0:T(8,128)S(1)} %get-tuple-element.28), channel_id=1, source_target_pairs={{0,1},{1,0},{2,3},{3,2},{4,5},{5,4},{6,7},{7,6},{8,9},{9,8},{10,11... | collective-permute-start | bytes 196616 | tf_op jit(solution)/shard_map/ppermute | solution.py:341
  10.2 4.9 %collective-permute-start.4 = (f32[40,128]{1,0:T(8,128)S(1)}, f32[40,128]{1,0:T(8,128)S(1)}, u32[]{:S(2)}, u32[]{:S(2)}) collective-permute-start(f32[40,128]{1,0:T(8,128)S(1)} %get-tuple-element.30), channel_id=1, source_target_pairs={{0,1},{1,0},{2,3},{3,2},{4,5},{5,4},{6,7},{7,6},{8,9},{9,8},{10,11... | collective-permute-start | bytes 61448 | tf_op jit(solution)/shard_map/ppermute | solution.py:341
  10.7 4.4 %collective-permute-start.5 = (f32[40,128]{1,0:T(8,128)S(1)}, f32[40,128]{1,0:T(8,128)S(1)}, u32[]{:S(2)}, u32[]{:S(2)}) collective-permute-start(f32[40,128]{1,0:T(8,128)S(1)} %get-tuple-element.31), channel_id=1, source_target_pairs={{0,8},{1,2},{2,1},{3,4},{4,3},{5,6},{6,5},{7,15},{8,0},{9,10},{10,... | collective-permute-start | bytes 61448 | tf_op jit(solution)/shard_map/ppermute | solution.py:342
  15.1 11.5 %all-to-all-start = ((f32[32,1,128]{2,1,0:T(1,128)}), f32[32,1,128]{2,1,0:T(1,128)S(1)}, u32[]{:S(2)}, u32[]{:S(2)}) async-start(f32[32,1,128]{2,1,0:T(1,128)} %bitcast.1), calls=%async_computation | async-start | bytes 32768 | tf_op jit(solution)/shard_map/all_to_all | solution.py:407

commit v7 on v6

--- a/solution.py
+++ b/solution.py
@@ -197,7 +197,7 @@
 KEEP = 1.0 - TIME_STEP * INFILTRATION
 
 
-def depth_kernel(counts, own, east, west, near, far, coarse, sums, zc, uc, stage, masks, cst):
+def depth_kernel(counts, own, east, west, far, near, coarse, sums, zc, uc, stage, masks, cst):
     flags = inside(counts)
     depth, rain, coef, codes = gather_fields((0, 1, 2, 3), WIDE, own, east, west, near, far, None, flags, stage)
     move_masks(codes, coef, masks)
@@ -292,7 +292,7 @@
             new.append(held * KEEP - flux + inflow(flux, masks))
         return tuple(new)
 
-    final = lax.fori_loop(0, SUBSTEPS, step, (depth, *species), unroll=4)
+    final = lax.fori_loop(0, SUBSTEPS, step, (depth, *species), unroll=True)
     chunk = depth.shape[0]
     rows = own.shape[1]
     for k, field in enumerate(final):
@@ -388,7 +388,7 @@
         compiler_params=ROOMY,
         cost_estimate=pl.CostEstimate(flops=20000000, bytes_accessed=20000000, transcendentals=0),
         name="depth_and_moments",
-    )(own, east, west, near, far, coarse)
+    )(own, east, west, far, near, coarse)
     sums, near_late, far_late = lax.optimization_barrier((sums, near_late, far_late))
     low = rows + 2 * SLIM
     depth_out, tracers_out = pl.pallas_call(

time: 27.7 us -> 27.7 us (level)
  transfers between devices with their start and end apart: 7 -> 7, of which waited for: 3 -> 3; matrix products, arithmetic and copies ran while one was open for 0% -> 0% of each run, Pallas kernels for 22% -> 21%
where the time goes in v7:
time: 27.7 us; the launch traced here: 27.4 us
  starting transfers between devices  12.7 us (46%)
  Pallas kernels  7.51 us (27%)
  waiting for transfers between devices  6.48 us (23%)
  between operations  0.66 us (2%)
    ppermute x3, starting transfers between devices, exchange(): near = lax.ppermute(near, AXES, swaps(axis, 0, counts))  4.66 us
    all_to_all x1, starting transfers between devices, shards(): sums = lax.all_to_all(sums, AXES, 0, 0, tiled=True)  4.34 us
    all_to_all x1, waiting for transfers between devices, shards(): sums = lax.all_to_all(sums, AXES, 0, 0, tiled=True)  4.07 us
    ppermute x3, starting transfers between devices, exchange(): far = lax.ppermute(far, AXES, swaps(axis, 1, counts))  3.7 us
    pallas_call x1, Pallas kernels, shards(): pl.pallas_call(functools.partial(state_kernel, counts), out_shape=(shape(...  3.07 us
    pallas_call x1, Pallas kernels, shards(): pl.pallas_call(functools.partial(depth_kernel, counts), out_shape=(shape(...  2.69 us
    ppermute x3, waiting for transfers between devices, exchange(): near = lax.ppermute(near, AXES, swaps(axis, 0, counts))  1.76 us
    pallas_call x1, Pallas kernels, shards(): pl.pallas_call(pack_columns, out_shape=(shape(7, rows, cols), shape(rows...  1.01 us
  transfers between devices with their start and end apart: 7, of which 3 were waited for; matrix products, arithmetic and copies ran while one was open for 0% of the time, Pallas kernels for 21%

profile of v7, /device:TPU:0, one launch (start us, length us, event | category | flops | bytes accessed | tf_op | source)
XLA Modules:
  0.0 27.4 jit_solution(10487909958034293093)
XLA Ops:
  0.6 1.0 %pack_columns.1 = (f32[7,32,128]{2,1,0:T(8,128)S(1)}, f32[40,128]{1,0:T(8,128)S(1)}, f32[40,128]{1,0:T(8,128)S(1)}, f32[8,128]{1,0:T(8,128)S(1)}) custom-call(f32[32,128]{1,0:T(8,128)} %refs_0_.1, f32[3,32,128]{2,1,0:T(8,128)} %refs_1_.1, f32[32,128]{1,0:T(8,128)} %refs_2_.1, f32[32,128]{1,0:T(8,128)} %refs_3_.1, s32[32,128]{1,0:T(8,128)} %refs_4_.1, ...), custom_call_target="tpu_custom_call" | custom-call | tf_op jit(solution)/shard_map/pack_columns/pallas_call | solution.py:350
  1.6 0.5 %collective-permute-start = (f32[40,128]{1,0:T(8,128)S(1)}, f32[40,128]{1,0:T(8,128)S(1)}, u32[]{:S(2)}, u32[]{:S(2)}) collective-permute-start(f32[40,128]{1,0:T(8,128)S(1)} %get-tuple-element.22), channel_id=1, source_target_pairs={{0,1},{1,0},{2,3},{3,2},{4,5},{5,4},{6,7},{7,6},{8,16},{9,17},{10,... | collective-permute-start | bytes 61448 | tf_op jit(solution)/shard_map/ppermute | solution.py:342
  2.2 4.1 %collective-permute-start.1 = (f32[40,128]{1,0:T(8,128)S(1)}, f32[40,128]{1,0:T(8,128)S(1)}, u32[]{:S(2)}, u32[]{:S(2)}) collective-permute-start(f32[40,128]{1,0:T(8,128)S(1)} %get-tuple-element.23), channel_id=1, source_target_pairs={{0,8},{1,9},{2,10},{3,11},{4,12},{5,13},{6,14},{7,15},{8,0},{9,1},... | collective-permute-start | bytes 61448 | tf_op jit(solution)/shard_map/ppermute | solution.py:341
  6.3 0.0 collective-permute-done.side_far
  6.3 1.8 %collective-permute-done.1.side_near = f32[40,128]{1,0:T(8,128)S(1)} collective-permute-done((f32[40,128]{1,0:T(8,128)S(1)}, f32[40,128]{1,0:T(8,128)S(1)}, u32[]{:S(2)}, u32[]{:S(2)}) %collective-permute-start.1) | collective-permute-done | bytes 20512 | tf_op jit(solution)/shard_map/ppermute | solution.py:341
  8.1 2.1 %collective-permute-start.2 = (f32[128,128]{1,0:T(8,128)S(1)}, f32[128,128]{1,0:T(8,128)S(1)}, u32[]{:S(2)}, u32[]{:S(2)}) collective-permute-start(f32[128,128]{1,0:T(8,128)S(1)} %get-tuple-element.27), channel_id=1, source_target_pairs={{0,8},{1,2},{2,1},{3,4},{4,3},{5,6},{6,5},{7,15},{8,0},{9,10},{10,... | collective-permute-start | bytes 196616 | tf_op jit(solution)/shard_map/ppermute | solution.py:342
  10.2 0.0 collective-permute-start.3
  10.2 0.5 %collective-permute-start.4 = (f32[40,128]{1,0:T(8,128)S(1)}, f32[40,128]{1,0:T(8,128)S(1)}, u32[]{:S(2)}, u32[]{:S(2)}) collective-permute-start(f32[40,128]{1,0:T(8,128)S(1)} %get-tuple-element.30), channel_id=1, source_target_pairs={{0,1},{1,0},{2,3},{3,2},{4,5},{5,4},{6,7},{7,6},{8,9},{9,8},{10,11... | collective-permute-start | bytes 61448 | tf_op jit(solution)/shard_map/ppermute | solution.py:341
  10.7 1.1 %collective-permute-start.5 = (f32[40,128]{1,0:T(8,128)S(1)}, f32[40,128]{1,0:T(8,128)S(1)}, u32[]{:S(2)}, u32[]{:S(2)}) collective-permute-start(f32[40,128]{1,0:T(8,128)S(1)} %get-tuple-element.31), channel_id=1, source_target_pairs={{0,8},{1,2},{2,1},{3,4},{4,3},{5,6},{6,5},{7,15},{8,0},{9,10},{10,... | collective-permute-start | bytes 61448 | tf_op jit(solution)/shard_map/ppermute | solution.py:342
  11.8 0.6 %collective-permute-done.2.far = f32[128,128]{1,0:T(8,128)S(1)} collective-permute-done((f32[128,128]{1,0:T(8,128)S(1)}, f32[128,128]{1,0:T(8,128)S(1)}, u32[]{:S(2)}, u32[]{:S(2)}) %collective-permute-start.2) | collective-permute-done | bytes 65568 | tf_op jit(solution)/shard_map/ppermute | solution.py:342
  12.4 0.0 collective-permute-done.3.near
  12.4 2.7 %depth_and_moments.1 = (f32[32,128]{1,0:T(8,128)}, f32[8,128]{1,0:T(8,128)S(1)}, f32[8,128]{1,0:T(8,128)S(1)}) custom-call(f32[7,32,128]{2,1,0:T(8,128)S(1)} %get-tuple-element.21.own, f32[40,128]{1,0:T(8,128)S(1)} %get-tuple-element.25.east, f32[40,128]{1,0:T(8,128)S(1)} %get-tuple-element.26.west, f32[128,128]{1,0:T(8,128)S(1)} %collective-permute-done.2.far, ...), custom_call_target="tpu_custom_call" | custom-call | flops 20000000 | bytes 20000000 | tf_op jit(solution)/shard_map/depth_and_moments/pallas_call | solution.py:378
  15.1 0.0 collective-permute-done.4.near_late
  15.1 0.0 collective-permute-done.5.far_late
  15.1 4.3 %all-to-all-start = ((f32[32,1,128]{2,1,0:T(1,128)}), f32[32,1,128]{2,1,0:T(1,128)S(1)}, u32[]{:S(2)}, u32[]{:S(2)}) async-start(f32[32,1,128]{2,1,0:T(1,128)} %bitcast.1), calls=%async_computation | async-start | bytes 32768 | tf_op jit(solution)/shard_map/all_to_all | solution.py:407
  19.5 3.1 %all_channels.1 = (f32[32,128]{1,0:T(8,128)}, f32[3,32,128]{2,1,0:T(8,128)}) custom-call(f32[7,32,128]{2,1,0:T(8,128)S(1)} %get-tuple-element.21.own, f32[40,128]{1,0:T(8,128)S(1)} %get-tuple-element.25.east, f32[40,128]{1,0:T(8,128)S(1)} %get-tuple-element.26.west, f32[128,128]{1,0:T(8,128)S(1)} %collective-permute-done.2.far, ...), custom_call_target="tpu_custom_call" | custom-call | flops 20000000 | bytes 20000000 | tf_op jit(solution)/shard_map/all_channels/pallas_call | solution.py:394
  22.6 4.1 %all-to-all-done = f32[32,1,128]{2,1,0:T(1,128)S(1)} async-done(((f32[32,1,128]{2,1,0:T(1,128)}), f32[32,1,128]{2,1,0:T(1,128)S(1)}, u32[]{:S(2)}, u32[]{:S(2)}) %all-to-all-start) | async-done | bytes 16416 | tf_op jit(solution)/shard_map/all_to_all | solution.py:407
  26.6 0.7 %combine_head.1 = f32[8,32]{1,0:T(8,128)} custom-call(f32[32,128]{1,0:T(8,128)S(1)} %bitcast.4, f32[8,128]{1,0:T(8,128)S(1)} %get-tuple-element.37.zc, f32[8,128]{1,0:T(8,128)S(1)} %get-tuple-element.38.uc), custom_call_target="tpu_custom_call" | custom-call | tf_op jit(solution)/shard_map/combine_head/pallas_call | solution.py:408
  (1 shorter events, 0.0 us)
Async XLA Ops:
  1.6 4.7 %collective-permute-start = (f32[40,128]{1,0:T(8,128)S(1)}, f32[40,128]{1,0:T(8,128)S(1)}, u32[]{:S(2)}, u32[]{:S(2)}) collective-permute-start(f32[40,128]{1,0:T(8,128)S(1)} %get-tuple-element.22), channel_id=1, source_target_pairs={{0,1},{1,0},{2,3},{3,2},{4,5},{5,4},{6,7},{7,6},{8,16},{9,17},{10,... | collective-permute-start | bytes 61448 | tf_op jit(solution)/shard_map/ppermute | solution.py:342
  2.2 5.9 %collective-permute-start.1 = (f32[40,128]{1,0:T(8,128)S(1)}, f32[40,128]{1,0:T(8,128)S(1)}, u32[]{:S(2)}, u32[]{:S(2)}) collective-permute-start(f32[40,128]{1,0:T(8,128)S(1)} %get-tuple-element.23), channel_id=1, source_target_pairs={{0,8},{1,9},{2,10},{3,11},{4,12},{5,13},{6,14},{7,15},{8,0},{9,1},... | collective-permute-start | bytes 61448 | tf_op jit(solution)/shard_map/ppermute | solution.py:341
  8.1 4.3 %collective-permute-start.2 = (f32[128,128]{1,0:T(8,128)S(1)}, f32[128,128]{1,0:T(8,128)S(1)}, u32[]{:S(2)}, u32[]{:S(2)}) collective-permute-start(f32[128,128]{1,0:T(8,128)S(1)} %get-tuple-element.27), channel_id=1, source_target_pairs={{0,8},{1,2},{2,1},{3,4},{4,3},{5,6},{6,5},{7,15},{8,0},{9,10},{10,... | collective-permute-start | bytes 196616 | tf_op jit(solution)/shard_map/ppermute | solution.py:342
  10.2 2.2 %collective-permute-start.3 = (f32[128,128]{1,0:T(8,128)S(1)}, f32[128,128]{1,0:T(8,128)S(1)}, u32[]{:S(2)}, u32[]{:S(2)}) collective-permute-start(f32[128,128]{1,0:T(8,128)S(1)} %get-tuple-element.28), channel_id=1, source_target_pairs={{0,1},{1,0},{2,3},{3,2},{4,5},{5,4},{6,7},{7,6},{8,9},{9,8},{10,11... | collective-permute-start | bytes 196616 | tf_op jit(solution)/shard_map/ppermute | solution.py:341
  10.2 4.9 %collective-permute-start.4 = (f32[40,128]{1,0:T(8,128)S(1)}, f32[40,128]{1,0:T(8,128)S(1)}, u32[]{:S(2)}, u32[]{:S(2)}) collective-permute-start(f32[40,128]{1,0:T(8,128)S(1)} %get-tuple-element.30), channel_id=1, source_target_pairs={{0,1},{1,0},{2,3},{3,2},{4,5},{5,4},{6,7},{7,6},{8,9},{9,8},{10,11... | collective-permute-start | bytes 61448 | tf_op jit(solution)/shard_map/ppermute | solution.py:341
  10.7 4.4 %collective-permute-start.5 = (f32[40,128]{1,0:T(8,128)S(1)}, f32[40,128]{1,0:T(8,128)S(1)}, u32[]{:S(2)}, u32[]{:S(2)}) collective-permute-start(f32[40,128]{1,0:T(8,128)S(1)} %get-tuple-element.31), channel_id=1, source_target_pairs={{0,8},{1,2},{2,1},{3,4},{4,3},{5,6},{6,5},{7,15},{8,0},{9,10},{10,... | collective-permute-start | bytes 61448 | tf_op jit(solution)/shard_map/ppermute | solution.py:342
  15.1 11.5 %all-to-all-start = ((f32[32,1,128]{2,1,0:T(1,128)}), f32[32,1,128]{2,1,0:T(1,128)S(1)}, u32[]{:S(2)}, u32[]{:S(2)}) async-start(f32[32,1,128]{2,1,0:T(1,128)} %bitcast.1), calls=%async_computation | async-start | bytes 32768 | tf_op jit(solution)/shard_map/all_to_all | solution.py:407
